TPU v7x, 32 devices: a whole 2x2x4 slice. The times are simulated.
32 devices in a mesh: fsdp: 4 (over z), ctx: 4 (over x, core), tp: 2 (over y).
Axes of the slice: x: 2, y: 2, z: 4, core: 2. Of those that a mesh axis runs over, the one named last changes fastest.
Arguments:
- tokens: bfloat16 [4, 2560, 512], P('fsdp', ('ctx', 'tp')), may hold values from -6 to 6
- encoder_states: bfloat16 [4, 512, 512], P('fsdp', 'ctx'), may hold values from -6 to 6
- timesteps: int32 [4], P('fsdp'), may hold values from 0 to 999
- parents: int32 [4, 20], P('fsdp'), may hold values from -1 to 11, as said below
- w_mod: bfloat16 [512, 3072], P('fsdp'), may hold values from -0.25 to 0.25
- w_self_qkv: bfloat16 [3, 512, 512], P(None, 'fsdp', 'tp'), may hold values from -0.25 to 0.25
- w_self_out: bfloat16 [512, 512], P('fsdp', 'tp'), may hold values from -1.5 to 1.5
- w_cross_qkv: bfloat16 [3, 512, 512], P(None, 'fsdp', 'tp'), may hold values from -0.25 to 0.25
- w_cross_out: bfloat16 [512, 512], P('fsdp', 'tp'), may hold values from -1.5 to 1.5
- w_up: bfloat16 [512, 2048], P('fsdp', 'tp'), may hold values from -0.25 to 0.25
- w_down: bfloat16 [512, 2048], P('fsdp', 'tp'), may hold values from -0.125 to 0.125
- cotangent: bfloat16 [4, 2560, 512], P('fsdp', ('ctx', 'tp')), may hold values from -6 to 6
Outputs:
- output: bfloat16 [4, 2560, 512], P('fsdp', ('ctx', 'tp'))
- input_grad: float32 [4, 2560, 512], P('fsdp', ('ctx', 'tp'))
- encoder_grad: float32 [4, 512, 512], P('fsdp', 'ctx')
- modulation_weight_gradient: float32 [512, 3072], P('fsdp')
- grad_w_self_qkv: float32 [3, 512, 512], P(None, 'fsdp', 'tp')
- grad_w_self_out: float32 [512, 512], P('fsdp', 'tp')
- grad_w_cross_qkv: float32 [3, 512, 512], P(None, 'fsdp', 'tp')
- grad_w_cross_out: float32 [512, 512], P('fsdp', 'tp')
- grad_w_up: float32 [512, 2048], P('fsdp', 'tp')
- grad_w_down: float32 [512, 2048], P('fsdp', 'tp')
Inputs may be any that keep to these rules, and one draw needn't show every extreme that they name: `parents`: in every tree block 0 has parent -1, block b for 1 <= b < 8 has parent b - 1, blocks 8 to 11 have parent 8 - 1, and each of the last 8 blocks has one of those branch blocks as parent, each branch block being the parent of exactly 2 of them.
All inputs are finite; a program needn't handle non-finite values.
Results may differ from a plain program's by a relative error of at most 0.025.
Values may be sent and summed in bfloat16 or wider, within the bound.
A program may use at most 128 MiB of HBM per device.

v0:
```python
import math

import jax
import jax.numpy as jnp
from jax import lax
from jax.experimental import pallas as pl
from jax.experimental.pallas import tpu as pltpu
from jax.sharding import PartitionSpec as P

BF = jnp.bfloat16
F = jnp.float32
D = 512
FF = 2048
HD = 64
ROWS = 320
LOC = 384
BLK = 128
TRUNK = 8
BRANCHES = 4
TRK = TRUNK * BLK
SHARED = (TRUNK + BRANCHES) * BLK
SPEC = 2 * LOC
KV = TRK + SPEC
ENC = 512
EPS = 1e-05
NEG = -1e30
VMEM_LIMIT = 67043328


def nn(a, b):
    return lax.dot_general(a, b, (((1,), (0,)), ((), ())), preferred_element_type=F)


def nt(a, b):
    return lax.dot_general(a, b, (((1,), (1,)), ((), ())), preferred_element_type=F)


def tn(a, b):
    return lax.dot_general(a, b, (((0,), (0,)), ((), ())), preferred_element_type=F)


def normed(v):
    center = v - jnp.mean(v, axis=-1, keepdims=True)
    rstd = lax.rsqrt(jnp.mean(center * center, axis=-1, keepdims=True) + EPS)
    return center * rstd, rstd


def norm_back(grad, stream, scale):
    n, rstd = normed(stream)
    gn = grad * (1.0 + scale)
    back = rstd * (
        gn
        - jnp.mean(gn, axis=-1, keepdims=True)
        - n * jnp.mean(gn * n, axis=-1, keepdims=True)
    )
    return back, jnp.sum(grad * n, axis=0, keepdims=True), jnp.sum(grad, axis=0, keepdims=True)


def row_loop(total, step, body):
    @pl.loop(0, total // step)
    def _(i):
        body(pl.ds(pl.multiple_of(i * step, step), step))


def half_lanes(shape, half):
    lane = lax.broadcasted_iota(jnp.int32, shape, len(shape) - 1)
    return (lane // HD) == half


def keep(value, half):
    return jnp.where(half_lanes(value.shape, half), value, jnp.zeros_like(value))


def layer_kernel(
    parents_ref,
    tok_tb,
    tok_loc,
    enc,
    cot,
    mod,
    wqkv,
    wso,
    wcqkv,
    wco,
    wup,
    wdn,
    out_ref,
    gstream,
    gpart,
    gown,
    egrad,
    mgrad,
    g_qkv,
    g_so,
    g_cqkv,
    g_co,
    g_up,
    g_dn,
    hid,
    hloc,
    kbuf,
    vbuf,
    qbuf,
    pt,
    ps,
    bias_t,
    bias_s,
    st,
    ss,
    spec_o,
    mixa,
    stream_b,
    stream_c,
    hid_b,
    hid_c,
    kenc,
    venc,
    qb,
    pe,
    mixb,
    t0,
    t1,
    b0,
    b1,
    acc0,
    acc1,
    gbf,
    mgr,
    dq,
    dkb,
    dvb,
    gkv,
    wk_acc,
    wv_acc,
):
    ci = lax.axis_index("ctx") * 2 + lax.axis_index("tp")
    odd = lax.rem(ci, 2)
    off = pl.multiple_of(odd * 64, 64)
    own = pl.ds(off, ROWS)
    base = (ci * 5) // 2
    sa, ba = mod[0:1, :], mod[1:2, :]
    sb, bb = mod[2:3, :], mod[3:4, :]
    sf, bf_ = mod[4:5, :], mod[5:6, :]

    def parent_of(lb):
        return jnp.clip(parents_ref[0, base + lb] - TRUNK, 0, BRANCHES - 1)

    def mask_trunk(rs):
        row = lax.broadcasted_iota(jnp.int32, (32, TRK), 0) + rs.start + ci * ROWS
        col = lax.broadcasted_iota(jnp.int32, (32, TRK), 1)
        bias_t[rs, :] = jnp.where(col <= row, 0.0, NEG)

    row_loop(ROWS, 32, mask_trunk)
    for lb in range(3):
        blk = base + lb
        row = lax.broadcasted_iota(jnp.int32, (BLK, 2 * BLK), 0)
        col = lax.broadcasted_iota(jnp.int32, (BLK, 2 * BLK), 1)
        par_ok = jnp.logical_and(col < BLK, blk >= TRUNK + BRANCHES)
        self_ok = jnp.logical_and(
            jnp.logical_and(col >= BLK, col - BLK <= row), blk >= TRUNK
        )
        bias_s[lb * BLK : (lb + 1) * BLK, :] = jnp.where(
            jnp.logical_or(par_ok, self_ok), 0.0, NEG
        )

    def hidden(x):
        n, _ = normed(x.astype(F))
        return (n * (1.0 + sa) + ba).astype(BF)

    def hid_trunk(rs):
        hid[rs, :] = hidden(tok_tb[rs, :])

    row_loop(TRK, 32, hid_trunk)

    def hid_loc(rs):
        hloc[rs, :] = hidden(tok_loc[rs, :])

    row_loop(LOC, 32, hid_loc)
    for lb in range(3):
        at = pl.multiple_of(TRK + parent_of(lb) * BLK, BLK)
        for piece in range(4):
            hid[TRK + lb * 256 + piece * 32 : TRK + lb * 256 + piece * 32 + 32, :] = hidden(
                tok_tb[pl.ds(at + piece * 32, 32), :]
            )
        hid[TRK + lb * 256 + BLK : TRK + lb * 256 + 2 * BLK, :] = hloc[
            lb * BLK : (lb + 1) * BLK, :
        ]

    def project(rs):
        kbuf[rs, :] = nn(hid[rs, :], wqkv[1]).astype(BF)
        vbuf[rs, :] = nn(hid[rs, :], wqkv[2]).astype(BF)

    row_loop(KV, 256, project)
    qbuf[...] = (nn(hloc[...], wqkv[0]) * 0.125).astype(BF)

    @pl.loop(0, 4)
    def _(hp):
        lanes = pl.ds(pl.multiple_of(hp * 128, 128), 128)
        kt = kbuf[0:TRK, lanes]
        for half in range(2):
            h = hp * 2 + half
            st[...] = nt(keep(qbuf[own, lanes], half), kt)
            for lb in range(3):
                r = slice(lb * BLK, (lb + 1) * BLK)
                ks = kbuf[TRK + lb * 256 : TRK + (lb + 1) * 256, lanes]
                ss[r, :] = nt(keep(qbuf[r, lanes], half), ks)

            @pl.loop(0, ROWS // 32)
            def _(i):
                rs = pl.ds(pl.multiple_of(i * 32, 32), 32)
                ro = pl.ds(pl.multiple_of(i * 32 + off, 32), 32)
                a = st[rs, :] + bias_t[rs, :]
                b = ss[ro, :] + bias_s[ro, :]
                top = jnp.maximum(
                    jnp.max(a, axis=-1, keepdims=True), jnp.max(b, axis=-1, keepdims=True)
                )
                a = jnp.exp(a - top)
                b = jnp.exp(b - top)
                inv = 1.0 / (
                    jnp.sum(a, axis=-1, keepdims=True) + jnp.sum(b, axis=-1, keepdims=True)
                )
                pt[h, rs, :] = (a * inv).astype(BF)
                ps[h, ro, :] = (b * inv).astype(BF)

            for lb in range(3):
                r = slice(lb * BLK, (lb + 1) * BLK)
                vs = vbuf[TRK + lb * 256 : TRK + (lb + 1) * 256, lanes]
                spec_o[half, r, :] = nn(ps[h, r, :], vs)
        vt = vbuf[0:TRK, lanes]
        o0 = nn(pt[hp * 2], vt) + spec_o[0, own, :]
        o1 = nn(pt[hp * 2 + 1], vt) + spec_o[1, own, :]
        mixa[:, lanes] = jnp.where(half_lanes(o0.shape, 0), o0, o1).astype(BF)

    t0[...] = nt(mixa[...], wso[...])

    def after_self(rs):
        ro = pl.ds(pl.multiple_of(rs.start + off, 32), 32)
        sbv = tok_loc[ro, :].astype(F) + t0[rs, :]
        stream_b[rs, :] = sbv
        n, _ = normed(sbv)
        hid_b[rs, :] = (n * (1.0 + sb) + bb).astype(BF)

    row_loop(ROWS, 32, after_self)

    kenc[...] = nn(enc[...], wcqkv[1]).astype(BF)
    venc[...] = nn(enc[...], wcqkv[2]).astype(BF)
    qb[...] = (nn(hid_b[...], wcqkv[0]) * 0.125).astype(BF)

    @pl.loop(0, 4)
    def _(hp):
        lanes = pl.ds(pl.multiple_of(hp * 128, 128), 128)
        kt = kenc[:, lanes]
        for half in range(2):
            h = hp * 2 + half
            t0[...] = nt(keep(qb[:, lanes], half), kt)

            @pl.loop(0, ROWS // 32)
            def _(i):
                rs = pl.ds(pl.multiple_of(i * 32, 32), 32)
                a = t0[rs, :]
                a = jnp.exp(a - jnp.max(a, axis=-1, keepdims=True))
                inv = 1.0 / jnp.sum(a, axis=-1, keepdims=True)
                pe[h, rs, :] = (a * inv).astype(BF)

        vt = venc[:, lanes]
        o0 = nn(pe[hp * 2], vt)
        o1 = nn(pe[hp * 2 + 1], vt)
        mixb[:, lanes] = jnp.where(half_lanes(o0.shape, 0), o0, o1).astype(BF)

    t0[...] = nt(mixb[...], wco[...])

    def after_cross(rs):
        scv = stream_b[rs, :] + t0[rs, :]
        stream_c[rs, :] = scv
        n, _ = normed(scv)
        hid_c[rs, :] = (n * (1.0 + sf) + bf_).astype(BF)

    row_loop(ROWS, 32, after_cross)

    acc0[...] = jnp.zeros_like(acc0)
    acc1[...] = jnp.zeros_like(acc1)

    @pl.loop(0, 4)
    def _(ft):
        cols = pl.ds(pl.multiple_of(ft * 512, 512), 512)
        t0[...] = nn(hid_c[...], wup[:, cols])
        t1[...] = nn(cot[...], wdn[:, cols])

        def gelu(rs):
            u = t0[rs, :]
            phi = 0.5 * (1.0 + lax.erf(u * (2.0**-0.5)))
            b0[rs, :] = (u * phi).astype(BF)
            slope = phi + u * (jnp.exp(-0.5 * u * u) * (1.0 / math.sqrt(2.0 * math.pi)))
            b1[rs, :] = (t1[rs, :] * slope).astype(BF)

        row_loop(ROWS, 32, gelu)
        acc0[...] += nt(b0[...], wdn[:, cols])
        acc1[...] += nt(b1[...], wup[:, cols])
        g_dn[:, cols] = tn(cot[...], b0[...]).astype(BF)
        g_up[:, cols] = tn(hid_c[...], b1[...]).astype(BF)

    def fold_mod(at, sums):
        mgrad[at : at + 1, :] = sums[0]
        mgrad[at + 1 : at + 2, :] = sums[1]

    def back_norm(at, scale, grad_src, stream_src, base_src, want_out):
        mgrad[at : at + 2, :] = jnp.zeros((2, D), F)

        def body(rs):
            back, ds, db = norm_back(grad_src[rs, :], stream_src[rs, :], scale)
            total = base_src[rs, :].astype(F) + back
            gstream[rs, :] = total
            gbf[rs, :] = total.astype(BF)
            mgrad[at : at + 1, :] += ds
            mgrad[at + 1 : at + 2, :] += db
            if want_out:
                out_ref[rs, :] = (stream_c[rs, :] + acc0[rs, :]).astype(BF)

        row_loop(ROWS, 32, body)

    back_norm(4, sf, acc1, stream_c, cot, True)

    g_co[...] = tn(gbf[...], mixb[...]).astype(BF)
    mgr[...] = nn(gbf[...], wco[...]).astype(BF)

    @pl.loop(0, 4)
    def _(hp):
        lanes = pl.ds(pl.multiple_of(hp * 128, 128), 128)
        prod = mgr[:, lanes].astype(F) * mixb[:, lanes].astype(F)
        dqs, dks, dvs = [], [], []
        for half in range(2):
            h = hp * 2 + half
            inner = jnp.sum(keep(prod, half), axis=-1, keepdims=True)
            mg = keep(mgr[:, lanes], half)
            dp = nt(mg, venc[:, lanes])
            b0[...] = (pe[h].astype(F) * (dp - inner)).astype(BF)
            dqs.append(nn(b0[...], kenc[:, lanes]))
            dks.append(tn(b0[...], keep(qb[:, lanes], half)))
            dvs.append(tn(pe[h], mg))
        dq[:, lanes] = (jnp.where(half_lanes(dqs[0].shape, 0), dqs[0], dqs[1]) * 0.125).astype(BF)
        dkb[0:ENC, lanes] = (dks[0] + dks[1]).astype(BF)
        dvb[0:ENC, lanes] = (dvs[0] + dvs[1]).astype(BF)

    g_cqkv[0] = tn(hid_b[...], dq[...]).astype(BF)
    g_cqkv[1] = tn(enc[...], dkb[0:ENC, :]).astype(BF)
    g_cqkv[2] = tn(enc[...], dvb[0:ENC, :]).astype(BF)
    egrad[...] = (nt(dkb[0:ENC, :], wcqkv[1]) + nt(dvb[0:ENC, :], wcqkv[2])).astype(BF)
    acc1[...] = nt(dq[...], wcqkv[0])
    back_norm(2, sb, acc1, stream_b, gstream, False)

    g_so[...] = tn(gbf[...], mixa[...]).astype(BF)
    mgr[...] = nn(gbf[...], wso[...]).astype(BF)

    @pl.when(odd == 0)
    def _():
        for h in range(8):
            ps[h, ROWS:LOC, :] = jnp.zeros((LOC - ROWS, 256), BF)
        spec_o[:, ROWS:LOC, :] = jnp.zeros((2, LOC - ROWS, 128), F)

    @pl.when(odd == 1)
    def _():
        for h in range(8):
            ps[h, 0:64, :] = jnp.zeros((64, 256), BF)
        spec_o[:, 0:64, :] = jnp.zeros((2, 64, 128), F)

    @pl.loop(0, 4)
    def _(hp):
        lanes = pl.ds(pl.multiple_of(hp * 128, 128), 128)
        prod = mgr[:, lanes].astype(F) * mixa[:, lanes].astype(F)
        dqs, dks, dvs = [], [], []
        dks_s = [[], [], []]
        dvs_s = [[], [], []]
        for half in range(2):
            h = hp * 2 + half
            inner = jnp.sum(keep(prod, half), axis=-1, keepdims=True)
            mg = keep(mgr[:, lanes], half)
            qm = keep(qbuf[own, lanes], half)
            dp = nt(mg, vbuf[0:TRK, lanes])
            ds = (pt[h].astype(F) * (dp - inner)).astype(BF)
            spec_o[0, own, :] = mg.astype(F)
            spec_o[1, own, :] = jnp.broadcast_to(inner, (ROWS, 128))
            dq_s = []
            for lb in range(3):
                r = slice(lb * BLK, (lb + 1) * BLK)
                k_rows = slice(TRK + lb * 256, TRK + (lb + 1) * 256)
                mgl = spec_o[0, r, :].astype(BF)
                dpl = nt(mgl, vbuf[k_rows, lanes])
                inner_l = spec_o[1, r, 0:1]
                dsl = (ps[h, r, :].astype(F) * (dpl - inner_l)).astype(BF)
                ss[r, 0:128] = nn(dsl, kbuf[k_rows, lanes])
                dks_s[lb].append(tn(dsl, keep(qbuf[r, lanes], half)))
                dvs_s[lb].append(tn(ps[h, r, :], mgl))
            dqs.append(nn(ds, kbuf[0:TRK, lanes]) + ss[own, 0:128])
            dks.append(tn(ds, qm))
            dvs.append(tn(pt[h], mg))
        dq[:, lanes] = (jnp.where(half_lanes(dqs[0].shape, 0), dqs[0], dqs[1]) * 0.125).astype(BF)
        dkb[0:TRK, lanes] = (dks[0] + dks[1]).astype(BF)
        dvb[0:TRK, lanes] = (dvs[0] + dvs[1]).astype(BF)
        for lb in range(3):
            k_rows = slice(TRK + lb * 256, TRK + (lb + 1) * 256)
            dkb[k_rows, lanes] = (dks_s[lb][0] + dks_s[lb][1]).astype(BF)
            dvb[k_rows, lanes] = (dvs_s[lb][0] + dvs_s[lb][1]).astype(BF)

    wk_acc[...] = jnp.zeros_like(wk_acc)
    wv_acc[...] = jnp.zeros_like(wv_acc)

    def key_side(rs):
        gkv[rs, :] = nt(dkb[rs, :], wqkv[1]) + nt(dvb[rs, :], wqkv[2])
        wk_acc[...] += tn(hid[rs, :], dkb[rs, :])
        wv_acc[...] += tn(hid[rs, :], dvb[rs, :])

    row_loop(KV, 256, key_side)
    g_qkv[0] = tn(hloc[own, :], dq[...]).astype(BF)
    g_qkv[1] = wk_acc[...].astype(BF)
    g_qkv[2] = wv_acc[...].astype(BF)
    gown[...] = nt(dq[...], wqkv[0])

    def put_trunk(rs):
        gpart[rs, :] = gkv[rs, :].astype(BF)

    row_loop(TRK, 32, put_trunk)
    for b in range(BRANCHES):
        for piece in range(4):
            total = jnp.zeros((32, D), F)
            for lb in range(3):
                hit = jnp.logical_and(
                    base + lb >= TRUNK + BRANCHES, parents_ref[0, base + lb] == TRUNK + b
                )
                part = gkv[TRK + lb * 256 + piece * 32 : TRK + lb * 256 + piece * 32 + 32, :]
                total += jnp.where(hit, part, 0.0)
            at = TRK + b * BLK + piece * 32
            gpart[at : at + 32, :] = total.astype(BF)
    for lb in range(3):
        gpart[SHARED + lb * BLK : SHARED + (lb + 1) * BLK, :] = gkv[
            TRK + lb * 256 + BLK : TRK + (lb + 1) * 256, :
        ].astype(BF)


def layer_call(parents, tok_tb, tok_loc, enc, cot, mod, weights):
    vm = pl.BlockSpec(memory_space=pltpu.VMEM)
    sds = jax.ShapeDtypeStruct
    return pl.pallas_call(
        layer_kernel,
        out_shape=(
            sds((ROWS, D), BF),
            sds((ROWS, D), F),
            sds((SHARED + LOC, D), BF),
            sds((ROWS, D), F),
            sds((ENC, D), BF),
            sds((8, D), F),
            sds((3, D, D), BF),
            sds((D, D), BF),
            sds((3, D, D), BF),
            sds((D, D), BF),
            sds((D, FF), BF),
            sds((D, FF), BF),
        ),
        in_specs=[pl.BlockSpec(memory_space=pltpu.SMEM)] + [vm] * 11,
        out_specs=(vm,) * 12,
        scratch_shapes=[
            pltpu.VMEM((KV, D), BF),
            pltpu.VMEM((LOC, D), BF),
            pltpu.VMEM((KV, D), BF),
            pltpu.VMEM((KV, D), BF),
            pltpu.VMEM((LOC, D), BF),
            pltpu.VMEM((8, ROWS, TRK), BF),
            pltpu.VMEM((8, LOC, 256), BF),
            pltpu.VMEM((ROWS, TRK), F),
            pltpu.VMEM((LOC, 256), F),
            pltpu.VMEM((ROWS, TRK), F),
            pltpu.VMEM((LOC, 256), F),
            pltpu.VMEM((2, LOC, 128), F),
            pltpu.VMEM((ROWS, D), BF),
            pltpu.VMEM((ROWS, D), F),
            pltpu.VMEM((ROWS, D), F),
            pltpu.VMEM((ROWS, D), BF),
            pltpu.VMEM((ROWS, D), BF),
            pltpu.VMEM((ENC, D), BF),
            pltpu.VMEM((ENC, D), BF),
            pltpu.VMEM((ROWS, D), BF),
            pltpu.VMEM((8, ROWS, ENC), BF),
            pltpu.VMEM((ROWS, D), BF),
            pltpu.VMEM((ROWS, D), F),
            pltpu.VMEM((ROWS, D), F),
            pltpu.VMEM((ROWS, D), BF),
            pltpu.VMEM((ROWS, D), BF),
            pltpu.VMEM((ROWS, D), F),
            pltpu.VMEM((ROWS, D), F),
            pltpu.VMEM((ROWS, D), BF),
            pltpu.VMEM((ROWS, D), BF),
            pltpu.VMEM((ROWS, D), BF),
            pltpu.VMEM((KV, D), BF),
            pltpu.VMEM((KV, D), BF),
            pltpu.VMEM((KV, D), F),
            pltpu.VMEM((D, D), F),
            pltpu.VMEM((D, D), F),
        ],
        compiler_params=pltpu.CompilerParams(vmem_limit_bytes=VMEM_LIMIT),
        name="layer",
    )(parents, tok_tb, tok_loc, enc, cot, mod, *weights)


def timestep_code(timesteps, width):
    half = width // 2
    frequency = jnp.exp(-math.log(10000.0) * jnp.arange(half, dtype=F) / half)
    angles = timesteps.astype(F)[:, None] * frequency[None, :]
    return jnp.concatenate([jnp.sin(angles), jnp.cos(angles)], axis=-1)


def per_device(
    tokens,
    encoder_states,
    timesteps,
    parents,
    w_mod,
    w_self_qkv,
    w_self_out,
    w_cross_qkv,
    w_cross_out,
    w_up,
    w_down,
    cotangent,
):
    fs = lax.axis_index("fsdp")
    rows = w_mod.shape[0]
    ci = lax.axis_index("ctx") * 2 + lax.axis_index("tp")
    condition = jax.nn.silu(timestep_code(timesteps, D)).astype(BF)
    cond_all = lax.all_gather(condition, "fsdp", axis=0, tiled=True)
    part = jnp.dot(
        lax.dynamic_slice(cond_all, (0, fs * rows), (cond_all.shape[0], rows)),
        w_mod,
        preferred_element_type=F,
    )
    mod = lax.psum_scatter(part, "fsdp", scatter_dimension=0, tiled=True).reshape(6, D)
    mod = jnp.concatenate([mod, jnp.zeros((2, D), F)])

    def whole(w, axis):
        return lax.all_gather(
            lax.all_gather(w, "fsdp", axis=axis, tiled=True), "tp", axis=axis + 1, tiled=True
        )

    weights = (
        whole(w_self_qkv, 1),
        whole(w_self_out, 0),
        whole(w_cross_qkv, 1),
        whole(w_cross_out, 0),
        whole(w_up, 0),
        whole(w_down, 0),
    )
    every = lax.all_gather(tokens[0], ("ctx", "tp"), axis=0, tiled=True)
    enc = lax.all_gather(encoder_states[0], "ctx", axis=0, tiled=True)
    off = lax.rem(ci, 2) * 64
    padded = jnp.concatenate([every, jnp.zeros((64, D), BF)])
    tok_loc = lax.dynamic_slice(padded, (ci * ROWS - off, 0), (LOC, D))
    (out, gstream, gpart, gown, egrad, mgrad, g_qkv, g_so, g_cqkv, g_co, g_up, g_dn) = layer_call(
        parents, every[:SHARED], tok_loc, enc, cotangent[0], mod, weights
    )
    total = jnp.zeros(padded.shape, F)
    total = total.at[:SHARED].set(gpart[:SHARED].astype(F))
    window = lax.dynamic_slice(total, (ci * ROWS - off, 0), (LOC, D)) + gpart[SHARED:].astype(F)
    total = lax.dynamic_update_slice(total, window, (ci * ROWS - off, 0))
    mine = lax.psum_scatter(
        total[: every.shape[0]].astype(BF), ("ctx", "tp"), scatter_dimension=0, tiled=True
    )
    hidden_grad = mine.astype(F) + gown
    stream_grad, ds, db = norm_back(hidden_grad, tokens[0].astype(F), mod[0:1])
    input_grad = gstream + stream_grad
    mod_terms = jnp.concatenate([ds, db, mgrad[2:6]]).reshape(1, 6 * D)
    mod_total = lax.psum(mod_terms, ("ctx", "tp"))
    mod_all = lax.all_gather(mod_total, "fsdp", axis=0, tiled=True)
    cond_mine = lax.dynamic_slice(cond_all, (0, fs * rows), (cond_all.shape[0], rows)).astype(F)
    grad_mod = jnp.dot(cond_mine.T, mod_all, precision=lax.Precision.HIGHEST)
    enc_grad = lax.psum(egrad.astype(F), "tp")
    enc_grad = lax.psum_scatter(enc_grad, "ctx", scatter_dimension=0, tiled=True)

    def owned(g, axis):
        g = lax.psum_scatter(g, "tp", scatter_dimension=axis + 1, tiled=True)
        g = lax.psum(g, "ctx")
        return lax.psum_scatter(g, "fsdp", scatter_dimension=axis, tiled=True).astype(F)

    return (
        out[None],
        input_grad[None],
        enc_grad[None],
        grad_mod,
        owned(g_qkv, 1),
        owned(g_so, 0),
        owned(g_cqkv, 1),
        owned(g_co, 0),
        owned(g_up, 0),
        owned(g_dn, 0),
    )


def solution(mesh):
    rows = P("fsdp", ("ctx", "tp"), None)
    return jax.shard_map(
        per_device,
        mesh=mesh,
        in_specs=(
            rows,
            P("fsdp", "ctx", None),
            P("fsdp"),
            P("fsdp", None),
            P("fsdp", None),
            P(None, "fsdp", "tp"),
            P("fsdp", "tp"),
            P(None, "fsdp", "tp"),
            P("fsdp", "tp"),
            P("fsdp", "tp"),
            P("fsdp", "tp"),
            rows,
        ),
        out_specs=(
            rows,
            rows,
            P("fsdp", "ctx", None),
            P("fsdp", None),
            P(None, "fsdp", "tp"),
            P("fsdp", "tp"),
            P(None, "fsdp", "tp"),
            P("fsdp", "tp"),
            P("fsdp", "tp"),
            P("fsdp", "tp"),
        ),
        check_vma=False,
    )
```

profile of v0, /device:TPU:0, one launch (start us, length us, event | category | flops | bytes accessed | tf_op | source)
XLA Modules:
  0.0 799.4 jit_solution(9234964490139301034)
XLA Ops:
  9.5 27.8 %all_gather.51 = bf16[3,512,256]{2,1,0:T(8,128)(2,1)} all-gather(bf16[3,128,256]{2,1,0:T(8,128)(2,1)} %param.19), channel_id=1, replica_groups=mesh['fsdp'=4,'ctx'=4,'tp'=2] {'fsdp'}, dimensions={1}, use_global_device_ids=true | all-gather | bytes 983040 | tf_op jit(solution)/shard_map/all_gather | solution.py:539
  37.3 23.7 %all_gather.55 = bf16[3,512,256]{2,1,0:T(8,128)(2,1)} all-gather(bf16[3,128,256]{2,1,0:T(8,128)(2,1)S(1)} %copy-done.8), channel_id=1, replica_groups=mesh['fsdp'=4,'ctx'=4,'tp'=2] {'fsdp'}, dimensions={1}, use_global_device_ids=true | all-gather | bytes 983040 | tf_op jit(solution)/shard_map/all_gather | solution.py:539
  61.7 20.4 %all-gather.20.cloned.1.call-done = bf16[512,1024]{1,0:T(8,128)(2,1)} async-done(((bf16[128,1024]{1,0:T(8,128)(2,1)}), bf16[512,1024]{1,0:T(8,128)(2,1)}) %all-gather.20.cloned.1.call-update) | async-done | bytes 1048592 | tf_op jit(solution)/shard_map/all_gather | solution.py:539
  83.6 11.9 %all-gather.2 = bf16[4,1,512]{2,1,0:T(2,128)(2,1)S(1)} all-gather(bf16[1,1,512]{2,1,0:T(2,128)(2,1)S(1)} %convert_bitcast_fusion.1), channel_id=1, replica_groups=mesh['fsdp'=4,'ctx'=4,'tp'=2] {'fsdp'}, dimensions={0}, use_global_device_ids=true | all-gather | bytes 5120 | tf_op jit(solution)/shard_map/all_gather | solution.py:528
  96.2 16.8 %all-reduce.3 = f32[4,3072]{1,0:T(4,128)S(1)} all-reduce(f32[4,3072]{1,0:T(4,128)S(1)} %fusion.17), channel_id=4, replica_groups=mesh['fsdp'=4,'ctx'=4,'tp'=2] {'fsdp'}, use_global_device_ids=true, to_apply=%region_0.1.clone | all-reduce | flops 12288 | bytes 98304
  114.4 14.0 %all_gather.53 = bf16[512,256]{1,0:T(8,128)(2,1)S(1)} all-gather(bf16[128,256]{1,0:T(8,128)(2,1)S(1)} %copy-done.11), channel_id=1, replica_groups=mesh['fsdp'=4,'ctx'=4,'tp'=2] {'fsdp'}, dimensions={0}, use_global_device_ids=true | all-gather | bytes 327680 | tf_op jit(solution)/shard_map/all_gather | solution.py:539
  128.5 13.8 %all_gather.57 = bf16[512,256]{1,0:T(8,128)(2,1)S(1)} all-gather(bf16[128,256]{1,0:T(8,128)(2,1)S(1)} %copy-done.12), channel_id=1, replica_groups=mesh['fsdp'=4,'ctx'=4,'tp'=2] {'fsdp'}, dimensions={0}, use_global_device_ids=true | all-gather | bytes 327680 | tf_op jit(solution)/shard_map/all_gather | solution.py:539
  142.2 9.6 %all_gather.54.wso = bf16[512,512]{1,0:T(8,128)(2,1)} all-gather(bf16[512,256]{1,0:T(8,128)(2,1)S(1)} %all_gather.53), channel_id=1, replica_groups=mesh['fsdp'=4,'ctx'=4,'tp'=2] {'tp'}, dimensions={1}, use_global_device_ids=true | all-gather | bytes 786432 | tf_op jit(solution)/shard_map/all_gather | solution.py:538
  151.8 11.3 %all_gather.58.wco = bf16[512,512]{1,0:T(8,128)(2,1)} all-gather(bf16[512,256]{1,0:T(8,128)(2,1)S(1)} %all_gather.57), channel_id=1, replica_groups=mesh['fsdp'=4,'ctx'=4,'tp'=2] {'tp'}, dimensions={1}, use_global_device_ids=true | all-gather | bytes 786432 | tf_op jit(solution)/shard_map/all_gather | solution.py:538
  163.1 7.3 all-gather.1
  173.6 2.4 all-gather.14.cloned.1.call-done.wcqkv
  175.9 33.3 %all-gather.18.cloned.1.call-done.wup = bf16[512,2048]{1,0:T(8,128)(2,1)} async-done(((bf16[512,1024]{1,0:T(8,128)(2,1)}), bf16[512,2048]{1,0:T(8,128)(2,1)}) %all-gather.18.cloned.1.call-update) | async-done | bytes 2097168 | tf_op jit(solution)/shard_map/all_gather | solution.py:538
  209.2 34.7 %all-gather.22.cloned.1.call-done.wdn = bf16[512,2048]{1,0:T(8,128)(2,1)} async-done(((bf16[512,1024]{1,0:T(8,128)(2,1)}), bf16[512,2048]{1,0:T(8,128)(2,1)}) %all-gather.22.cloned.1.call-update) | async-done | bytes 2097168 | tf_op jit(solution)/shard_map/all_gather | solution.py:538
  243.9 103.8 %layer.1 = (bf16[320,512]{1,0:T(8,128)(2,1)}, f32[320,512]{1,0:T(8,128)}, bf16[1920,512]{1,0:T(8,128)(2,1)}, f32[320,512]{1,0:T(8,128)}, bf16[512,512]{1,0:T(8,1...) custom-call(s32[1,20]{1,0:T(1,128)} %parents_ref.1, ...), custom_call_target="tpu_custom_call" | custom-call | tf_op jit(solution)/shard_map/layer/pallas_call | solution.py:442
  351.2 11.3 %reduce-scatter.19.cloned.1.call-done = bf16[512,256]{1,0:T(8,128)(2,1)} async-done(((bf16[512,512]{1,0:T(8,128)(2,1)}), bf16[512,256]{1,0:T(8,128)(2,1)}) %reduce-scatter.19.cloned.1.call-update) | async-done | bytes 262160 | tf_op jit(solution)/shard_map/reduce_scatter | solution.py:577
  362.5 16.9 %reduce-scatter.23.cloned.1.call-done = bf16[512,256]{1,0:T(8,128)(2,1)} async-done(((bf16[512,512]{1,0:T(8,128)(2,1)}), bf16[512,256]{1,0:T(8,128)(2,1)}) %reduce-scatter.23.cloned.1.call-update) | async-done | bytes 262160 | tf_op jit(solution)/shard_map/reduce_scatter | solution.py:577
  379.4 28.1 %reduce-scatter.17.cloned.1.call-done = bf16[3,512,256]{2,1,0:T(8,128)(2,1)} async-done(((bf16[3,512,512]{2,1,0:T(8,128)(2,1)}), bf16[3,512,256]{2,1,0:T(8,128)(2,1)}) %reduce-scatter.17.cloned.1.call-update) | async-done | bytes 786448 | tf_op jit(solution)/shard_map/reduce_scatter | solution.py:577
  407.6 28.4 %reduce-scatter.21.cloned.1.call-done = bf16[3,512,256]{2,1,0:T(8,128)(2,1)} async-done(((bf16[3,512,512]{2,1,0:T(8,128)(2,1)}), bf16[3,512,256]{2,1,0:T(8,128)(2,1)}) %reduce-scatter.21.cloned.1.call-update) | async-done | bytes 786448 | tf_op jit(solution)/shard_map/reduce_scatter | solution.py:577
  436.1 33.9 %reduce-scatter.25.cloned.1.call-done = bf16[512,1024]{1,0:T(8,128)(2,1)} async-done(((bf16[512,2048]{1,0:T(8,128)(2,1)}), bf16[512,1024]{1,0:T(8,128)(2,1)}) %reduce-scatter.25.cloned.1.call-update) | async-done | bytes 1048592 | tf_op jit(solution)/shard_map/reduce_scatter | solution.py:577
  470.1 34.1 %reduce-scatter.27.cloned.1.call-done = bf16[512,1024]{1,0:T(8,128)(2,1)} async-done(((bf16[512,2048]{1,0:T(8,128)(2,1)}), bf16[512,1024]{1,0:T(8,128)(2,1)}) %reduce-scatter.27.cloned.1.call-update) | async-done | bytes 1048592 | tf_op jit(solution)/shard_map/reduce_scatter | solution.py:577
  509.4 16.6 %reduce-scatter.33.cloned.1.call-done = bf16[128,256]{1,0:T(8,128)(2,1)} async-done(((bf16[512,256]{1,0:T(8,128)(2,1)}), bf16[128,256]{1,0:T(8,128)(2,1)}) %reduce-scatter.33.cloned.1.call-update) | async-done | bytes 65552 | tf_op jit(solution)/shard_map/reduce_scatter | solution.py:579
  526.0 20.1 %reduce-scatter.37.cloned.1.call-done = bf16[128,256]{1,0:T(8,128)(2,1)} async-done(((bf16[512,256]{1,0:T(8,128)(2,1)}), bf16[128,256]{1,0:T(8,128)(2,1)}) %reduce-scatter.37.cloned.1.call-update) | async-done | bytes 65552 | tf_op jit(solution)/shard_map/reduce_scatter | solution.py:579
  546.1 23.7 %reduce-scatter.31.cloned.1.call-done = bf16[3,128,256]{2,1,0:T(8,128)(2,1)} async-done(((bf16[3,512,256]{2,1,0:T(8,128)(2,1)}), bf16[3,128,256]{2,1,0:T(8,128)(2,1)}) %reduce-scatter.31.cloned.1.call-update) | async-done | bytes 196624 | tf_op jit(solution)/shard_map/reduce_scatter | solution.py:579
  569.8 24.7 %reduce-scatter.35.cloned.1.call-done = bf16[3,128,256]{2,1,0:T(8,128)(2,1)} async-done(((bf16[3,512,256]{2,1,0:T(8,128)(2,1)}), bf16[3,128,256]{2,1,0:T(8,128)(2,1)}) %reduce-scatter.35.cloned.1.call-update) | async-done | bytes 196624 | tf_op jit(solution)/shard_map/reduce_scatter | solution.py:579
  594.6 28.5 %reduce-scatter.39.cloned.1.call-done = bf16[128,1024]{1,0:T(8,128)(2,1)} async-done(((bf16[512,1024]{1,0:T(8,128)(2,1)}), bf16[128,1024]{1,0:T(8,128)(2,1)}) %reduce-scatter.39.cloned.1.call-update) | async-done | bytes 262160 | tf_op jit(solution)/shard_map/reduce_scatter | solution.py:579
  623.1 28.2 %reduce-scatter.41.cloned.1.call-done = bf16[128,1024]{1,0:T(8,128)(2,1)} async-done(((bf16[512,1024]{1,0:T(8,128)(2,1)}), bf16[128,1024]{1,0:T(8,128)(2,1)}) %reduce-scatter.41.cloned.1.call-update) | async-done | bytes 262160 | tf_op jit(solution)/shard_map/reduce_scatter | solution.py:579
  653.1 24.8 %reduce-scatter.29.cloned.1.call-done = f32[128,512]{1,0:T(8,128)} async-done(((f32[512,512]{1,0:T(8,128)}), f32[128,512]{1,0:T(8,128)}) %reduce-scatter.29.cloned.1.call-update) | async-done | bytes 262160 | tf_op jit(solution)/shard_map/reduce_scatter | solution.py:574
  677.9 47.4 %reduce-scatter.15.cloned.1.call-done = bf16[320,512]{1,0:T(8,128)(2,1)} async-done(((bf16[2560,512]{1,0:T(8,128)(2,1)}), bf16[320,512]{1,0:T(8,128)(2,1)}) %reduce-scatter.15.cloned.1.call-update) | async-done | bytes 327696 | tf_op jit(solution)/shard_map/reduce_scatter | solution.py:562
  726.7 24.1 %psum.57 = f32[1,3072]{1,0:T(1,128)S(1)} all-reduce(f32[1,3072]{1,0:T(1,128)S(1)} %bitcast.64), channel_id=1, replica_groups=mesh['fsdp'=4,'ctx'=4,'tp'=2] {'ctx','tp'}, use_global_device_ids=true, to_apply=%region_10.11 | all-reduce | flops 3072 | bytes 24576 | tf_op jit(solution)/shard_map/psum | solution.py:569
  750.8 13.2 %all-gather.3 = f32[4,1,3072]{2,1,0:T(1,128)S(1)} all-gather(f32[1,1,3072]{2,1,0:T(1,128)S(1)} %bitcast.65), channel_id=1, replica_groups=mesh['fsdp'=4,'ctx'=4,'tp'=2] {'fsdp'}, dimensions={0}, use_global_device_ids=true | all-gather | bytes 61440 | tf_op jit(solution)/shard_map/all_gather | solution.py:570
  764.0 2.1 fusion.10
  777.2 14.0 %all-reduce.8.cloned.1.call-done = f32[128,512]{1,0:T(8,128)} async-done(((f32[128,512]{1,0:T(8,128)}), f32[128,512]{1,0:T(8,128)}) %all-reduce.8.cloned.1.call-update) | async-done | bytes 262160 | tf_op jit(solution)/shard_map/psum | solution.py:573
  (118 shorter events, 33.6 us)
Async XLA Ops:
  7.2 53.9 %all-gather.16.cloned.1.call-start = ((), (), s32[]{:S(2)}) async-start(), calls=%async_computation.16 | async-start | bytes 1310720 | tf_op jit(solution)/shard_map/all_gather | solution.py:539
  7.9 74.2 %all-gather.20.cloned.1.call-start = ((), (), s32[]{:S(2)}) async-start(), calls=%async_computation.18 | async-start | bytes 1310720 | tf_op jit(solution)/shard_map/all_gather | solution.py:539
  8.7 161.7 %all-gather.24.cloned.1.call-start = ((), (), s32[]{:S(2)}) async-start(), calls=%async_computation.27 | async-start | bytes 2949120 | tf_op jit(solution)/shard_map/all_gather | solution.py:550
  9.4 164.2 %all-gather.12.cloned.1.call-start = ((), (), s32[]{:S(2)}) async-start(), calls=%async_computation.14 | async-start | bytes 2359296 | tf_op jit(solution)/shard_map/all_gather | solution.py:538
  37.3 58.8 %copy-start.4 = (bf16[128,3072]{1,0:T(8,128)(2,1)S(1)}, bf16[128,3072]{1,0:T(8,128)(2,1)}, u32[]{:S(2)}) copy-start(bf16[128,3072]{1,0:T(8,128)(2,1)} %param.18) | copy-start | bytes 2359300
  37.3 138.7 %all-gather.14.cloned.1.call-start = ((), (), s32[]{:S(2)}) async-start(), calls=%async_computation.15 | async-start | bytes 2359296 | tf_op jit(solution)/shard_map/all_gather | solution.py:538
  61.0 67.4 %copy-start.12 = (bf16[128,256]{1,0:T(8,128)(2,1)S(1)}, bf16[128,256]{1,0:T(8,128)(2,1)}, u32[]{:S(2)}) copy-start(bf16[128,256]{1,0:T(8,128)(2,1)} %param.22) | copy-start | bytes 196612
  61.1 148.1 %all-gather.18.cloned.1.call-start = ((), (), s32[]{:S(2)}) async-start(), calls=%async_computation.17 | async-start | bytes 3145728 | tf_op jit(solution)/shard_map/all_gather | solution.py:538
  61.6 182.3 %all-gather.22.cloned.1.call-start = ((), (), s32[]{:S(2)}) async-start(), calls=%async_computation.19 | async-start | bytes 3145728 | tf_op jit(solution)/shard_map/all_gather | solution.py:538
  82.1 81.0 %copy-start.9 = (bf16[1,128,512]{2,1,0:T(8,128)(2,1)S(1)}, bf16[1,128,512]{2,1,0:T(8,128)(2,1)}, u32[]{:S(2)}) copy-start(bf16[1,128,512]{2,1,0:T(8,128)(2,1)} %param.15) | copy-start | bytes 393220
  82.1 280.3 %reduce-scatter.19.cloned.1.call-start = ((), (), s32[]{:S(2)}) async-start(), calls=%async_computation.22 | async-start | bytes 786432 | tf_op jit(solution)/shard_map/reduce_scatter | solution.py:577
  113.1 59.3 %copy-start.10 = (f32[4,3072]{1,0:T(4,128)}, f32[4,3072]{1,0:T(4,128)S(1)}, u32[]{:S(2)}) copy-start(f32[4,3072]{1,0:T(4,128)S(1)} %all-reduce.3) | copy-start | bytes 147460
  347.7 31.6 %reduce-scatter.23.cloned.1.call-start = ((), (), s32[]{:S(2)}) async-start(), calls=%async_computation.24 | async-start | bytes 786432 | tf_op jit(solution)/shard_map/reduce_scatter | solution.py:577
  348.5 59.1 %reduce-scatter.17.cloned.1.call-start = ((), (), s32[]{:S(2)}) async-start(), calls=%async_computation.21 | async-start | bytes 2359296 | tf_op jit(solution)/shard_map/reduce_scatter | solution.py:577
  349.1 87.0 %reduce-scatter.21.cloned.1.call-start = ((), (), s32[]{:S(2)}) async-start(), calls=%async_computation.23 | async-start | bytes 2359296 | tf_op jit(solution)/shard_map/reduce_scatter | solution.py:577
  349.8 120.2 %reduce-scatter.25.cloned.1.call-start = ((), (), s32[]{:S(2)}) async-start(), calls=%async_computation.25 | async-start | bytes 3145728 | tf_op jit(solution)/shard_map/reduce_scatter | solution.py:577
  350.4 153.8 %reduce-scatter.27.cloned.1.call-start = ((), (), s32[]{:S(2)}) async-start(), calls=%async_computation.26 | async-start | bytes 3145728 | tf_op jit(solution)/shard_map/reduce_scatter | solution.py:577
  351.1 174.9 %reduce-scatter.33.cloned.1.call-start = ((), (), s32[]{:S(2)}) async-start(), calls=%async_computation.31 | async-start | bytes 327680 | tf_op jit(solution)/shard_map/reduce_scatter | solution.py:579
  362.4 141.8 %copy-start.6 = (bf16[512,512]{1,0:T(8,128)(2,1)S(1)}, bf16[512,512]{1,0:T(8,128)(2,1)}, u32[]{:S(2)}) copy-start(bf16[512,512]{1,0:T(8,128)(2,1)} %get-tuple-element.38) | copy-start | bytes 1572868
  362.5 183.6 %reduce-scatter.37.cloned.1.call-start = ((), (), s32[]{:S(2)}) async-start(), calls=%async_computation.33 | async-start | bytes 327680 | tf_op jit(solution)/shard_map/reduce_scatter | solution.py:579
  379.4 190.5 %reduce-scatter.31.cloned.1.call-start = ((), (), s32[]{:S(2)}) async-start(), calls=%async_computation.30 | async-start | bytes 983040 | tf_op jit(solution)/shard_map/reduce_scatter | solution.py:579
  407.6 187.0 %reduce-scatter.35.cloned.1.call-start = ((), (), s32[]{:S(2)}) async-start(), calls=%async_computation.32 | async-start | bytes 983040 | tf_op jit(solution)/shard_map/reduce_scatter | solution.py:579
  436.0 187.1 %reduce-scatter.39.cloned.1.call-start = ((), (), s32[]{:S(2)}) async-start(), calls=%async_computation.34 | async-start | bytes 1310720 | tf_op jit(solution)/shard_map/reduce_scatter | solution.py:579
  470.0 181.3 %reduce-scatter.41.cloned.1.call-start = ((), (), s32[]{:S(2)}) async-start(), calls=%async_computation.35 | async-start | bytes 1310720 | tf_op jit(solution)/shard_map/reduce_scatter | solution.py:579
  504.2 173.7 %reduce-scatter.29.cloned.1.call-start = ((), (), s32[]{:S(2)}) async-start(), calls=%async_computation.28 | async-start | bytes 1310720 | tf_op jit(solution)/shard_map/reduce_scatter | solution.py:574
  505.4 219.9 %reduce-scatter.15.cloned.1.call-start = ((), (), s32[]{:S(2)}) async-start(), calls=%async_computation.20 | async-start | bytes 2949120 | tf_op jit(solution)/shard_map/reduce_scatter | solution.py:562
  508.3 144.8 %copy-start.15 = (f32[8,512]{1,0:T(8,128)S(1)}, f32[8,512]{1,0:T(8,128)}, u32[]{:S(2)}) copy-start(f32[8,512]{1,0:T(8,128)} %get-tuple-element.39) | copy-start | bytes 49156
  508.3 217.0 %copy-start.2 = (f32[320,512]{1,0:T(8,128)S(1)}, f32[320,512]{1,0:T(8,128)}, u32[]{:S(2)}) copy-start(f32[320,512]{1,0:T(8,128)} %get-tuple-element.37) | copy-start | bytes 1966084
  508.3 255.7 %copy-start.5 = (f32[320,512]{1,0:T(8,128)S(1)}, f32[320,512]{1,0:T(8,128)}, u32[]{:S(2)}) copy-start(f32[320,512]{1,0:T(8,128)} %get-tuple-element.35) | copy-start | bytes 1966084
  508.3 259.8 %all-reduce.10.cloned.1.call-start = ((), (), s32[]{:S(2)}) async-start(), calls=%async_computation.36 | async-start | bytes 2097152 | tf_op jit(solution)/shard_map/psum | solution.py:578
  651.4 139.8 %all-reduce.8.cloned.1.call-start = ((), (), s32[]{:S(2)}) async-start(), calls=%async_computation.29 | async-start | bytes 524288 | tf_op jit(solution)/shard_map/psum | solution.py:573
  677.9 88.2 %copy-start.14 = (bf16[4,1,128]{2,1,0:T(2,128)(2,1)S(1)}, bf16[4,1,128]{2,1,0:T(2,128)(2,1)}, u32[]{:S(2)}) copy-start(bf16[4,1,128]{2,1,0:T(2,128)(2,1)} %copy-done.13) | copy-start | bytes 3076
  (8 other events, 176.3 us)
Sparse Core Ops, SparseCore 0:
  9.6 43.6 all-gather.15
  54.9 27.1 all-gather.19
  84.0 29.5 all-gather.23
  115.0 29.9 all-gather.11
  146.4 29.4 all-gather.13
  177.3 31.8 all-gather.17
  210.7 33.1 all-gather.21
  347.8 14.5 reduce-scatter.18
  364.8 14.5 reduce-scatter.22
  381.4 26.0 reduce-scatter.16
  409.9 26.0 reduce-scatter.20
  438.1 31.8 reduce-scatter.24
  472.3 31.8 reduce-scatter.26
  506.3 19.6 reduce-scatter.32
  528.2 17.8 reduce-scatter.36
  548.2 21.5 reduce-scatter.30
  572.0 22.5 reduce-scatter.34
  596.7 26.3 reduce-scatter.38
  625.5 25.7 reduce-scatter.40
  654.3 23.5 reduce-scatter.28
  681.6 43.6 reduce-scatter.14
  728.2 37.2 all-reduce.9
  767.9 23.2 all-reduce.7
where the time goes:
time: 800 us; the launch traced here: 799 us
  waiting for transfers between devices  477 us (60%)
  blocking collectives  173 us (22%)
  Pallas kernels  104 us (13%)
  other arithmetic  16.4 us (2%)
  between operations  15 us (2%)
  local copies, waits for them, and re-layouts  10.3 us (1%)
    reduce_scatter x6, waiting for transfers between devices, owned(): g = lax.psum_scatter(g, 'tp', scatter_dimension=axis + 1, tiled=True)  153 us
    reduce_scatter x6, waiting for transfers between devices, owned(): lax.psum_scatter(g, 'fsdp', scatter_dimension=axis, tiled=True).astype(F)  142 us
    pallas_call x1, Pallas kernels, layer_call(): pl.pallas_call(layer_kernel, out_shape=(sds((ROWS, D), BF), sds((ROWS, D)...  104 us
    all_gather x4, blocking collectives, whole(): lax.all_gather(w, 'fsdp', axis=axis, tiled=True)  79.3 us
    all_gather x4, waiting for transfers between devices, whole(): lax.all_gather(lax.all_gather(w, 'fsdp', axis=axis, tiled=True), 'tp', ax...  70.3 us
    reduce_scatter x1, waiting for transfers between devices, per_device(): lax.psum_scatter(total[:every.shape[0]].astype(BF), ('ctx', 'tp'), scatte...  47.4 us
    reduce_scatter x1, waiting for transfers between devices, per_device(): lax.psum_scatter(enc_grad, 'ctx', scatter_dimension=0, tiled=True)  24.8 us
    psum x1, blocking collectives, per_device(): mod_total = lax.psum(mod_terms, ('ctx', 'tp'))  24.1 us
  transfers between devices with their start and end apart: 23, of which 19 were waited for; matrix products, arithmetic and copies ran while one was open for 3% of the time, Pallas kernels for 0%

commit v1 on v0

--- a/solution.py
+++ b/solution.py
@@ -1,3 +1,4 @@
+import functools
 import math
 
 import jax
@@ -71,31 +72,96 @@
     return jnp.where(half_lanes(value.shape, half), value, jnp.zeros_like(value))
 
 
+MESH = pl.DeviceIdType.MESH
+
+
+class Wire:
+    def __init__(self, send, recv):
+        self.send, self.recv, self.used, self.sent = send, recv, 0, []
+
+    def slot(self, count=1):
+        self.used += count
+        return self.used - count
+
+    def copy(self, src, dst, at, to):
+        return pltpu.make_async_remote_copy(
+            src_ref=src,
+            dst_ref=dst,
+            send_sem=self.send.at[at],
+            recv_sem=self.recv.at[at],
+            device_id=to,
+            device_id_type=MESH,
+        )
+
+    def push(self, dst, at, to, when=None, src=None):
+        src = src or dst
+        if when is None:
+            self.copy(src(), dst(), at, to).start()
+        else:
+
+            @pl.when(when)
+            def _():
+                self.copy(src(), dst(), at, to).start()
+
+        self.sent.append((src, dst, at, to, when))
+
+    def arrived(self, dst, at, to, when=None):
+        if when is None:
+            self.copy(dst, dst, at, to).wait_recv()
+        else:
+
+            @pl.when(when)
+            def _():
+                self.copy(dst, dst, at, to).wait_recv()
+
+    def drain(self):
+        for src, dst, at, to, when in self.sent:
+            if when is None:
+                self.copy(src(), dst(), at, to).wait_send()
+            else:
+
+                @pl.when(when)
+                def _(src=src, dst=dst, at=at, to=to):
+                    self.copy(src(), dst(), at, to).wait_send()
+
+        self.sent = []
+
+
 def layer_kernel(
+    n,
     parents_ref,
-    tok_tb,
-    tok_loc,
-    enc,
+    cond_parts,
+    w_mod,
+    tok_in,
+    enc_in,
     cot,
-    mod,
-    wqkv,
-    wso,
-    wcqkv,
-    wco,
-    wup,
-    wdn,
+    w_sqkv,
+    w_so,
+    w_cqkv,
+    w_co,
+    w_up,
+    w_dn,
     out_ref,
     gstream,
     gpart,
     gown,
     egrad,
     mgrad,
+    mod,
+    cond_all,
     g_qkv,
     g_so,
     g_cqkv,
     g_co,
     g_up,
     g_dn,
+    watt,
+    wup,
+    wdn,
+    tok,
+    enc,
+    part_out,
+    part_in,
     hid,
     hloc,
     kbuf,
@@ -132,18 +198,233 @@
     gkv,
     wk_acc,
     wv_acc,
+    send,
+    recv,
+    local,
 ):
-    ci = lax.axis_index("ctx") * 2 + lax.axis_index("tp")
-    odd = lax.rem(ci, 2)
+    fs = lax.axis_index("fsdp")
+    cx = lax.axis_index("ctx")
+    y = lax.axis_index("tp")
+    x, c = cx // 2, lax.rem(cx, 2)
+    ci = cx * 2 + y
+    odd = y
     off = pl.multiple_of(odd * 64, 64)
     own = pl.ds(off, ROWS)
     base = (ci * 5) // 2
+    rows = w_mod.shape[0]
+    to_y = {"tp": 1 - y}
+    to_c = {"ctx": 2 * x + 1 - c}
+    to_x = {"ctx": 2 * (1 - x) + c}
+    wire = Wire(send, recv)
+
+    my_rows = pl.ds(pl.multiple_of(fs * rows, rows), rows)
+
+    def att_cols(yy, cc):
+        return pl.ds(pl.multiple_of(yy * 256 + cc * 128, 128), 128)
+
+    def ffn_cols(yy, xx, cc):
+        return pl.ds(pl.multiple_of(yy * 1024 + xx * 512 + cc * 256, 256), 256)
+
+    half = pl.ds(pl.multiple_of(c * 128, 128), 128)
+    quarter = pl.ds(pl.multiple_of(cx * 256, 256), 256)
+    groups = (
+        (w_sqkv.at[:, :, half], watt, slice(0, 3), 0),
+        (w_so.at[:, half], watt, 3, 0),
+        (w_cqkv.at[:, :, half], watt, slice(4, 7), 0),
+        (w_co.at[:, half], watt, 7, 0),
+        (w_up.at[:, quarter], wup, None, 1),
+        (w_dn.at[:, quarter], wdn, None, 1),
+    )
+
+    def place(g, row_at, yy, xx, cc):
+        _, buf, index, wide = groups[g]
+        if wide:
+            return buf.at[row_at, ffn_cols(yy, xx, cc)]
+        return buf.at[index, row_at, att_cols(yy, cc)]
+
+    def chunk(i):
+        return tok.at[pl.ds(pl.multiple_of(i * ROWS, ROWS), ROWS), :]
+
+    def enc_part(i):
+        return enc.at[pl.ds(pl.multiple_of(i * 128, 128), 128), :]
+
+    all_rows = pl.ds(0, D)
+
+    local_copies = [
+        pltpu.make_async_copy(tok_in.at[0], chunk(ci), local.at[0]),
+        pltpu.make_async_copy(enc_in.at[0], enc_part(cx), local.at[1]),
+    ] + [
+        pltpu.make_async_copy(groups[g][0], place(g, my_rows, y, x, c), local.at[2 + g])
+        for g in range(6)
+    ]
+    for copy in local_copies:
+        copy.start()
+
+    barrier = pltpu.get_barrier_semaphore()
+
+    @pl.loop(1, n)
+    def _(k):
+        pl.semaphore_signal(
+            barrier, inc=1, device_id={"fsdp": lax.rem(fs + k, n)}, device_id_type=MESH
+        )
+
+    @pl.loop(1, 8)
+    def _(k):
+        other = lax.rem(ci + k, 8)
+        pl.semaphore_signal(
+            barrier,
+            inc=1,
+            device_id={"ctx": other // 2, "tp": lax.rem(other, 2)},
+            device_id_type=MESH,
+        )
+
+    pl.semaphore_wait(barrier, n - 1 + 7)
+
+    def peers(make):
+        @pl.loop(1, n)
+        def _(k):
+            make(k, lax.rem(fs + k, n), lax.rem(fs + n - k, n))
+
+    s_cond = wire.slot(n)
+    s_part = wire.slot(n)
+    s_z = [wire.slot(n) for _ in range(6)]
+    s_y = [wire.slot() for _ in range(6)]
+    s_c0 = [wire.slot() for _ in range(6)]
+    s_c1 = [wire.slot() for _ in range(6)]
+    s_x0 = [wire.slot() for _ in range(6)]
+    s_x1 = [wire.slot() for _ in range(6)]
+    s_c2 = [wire.slot() for _ in range(6)]
+    s_c3 = [wire.slot() for _ in range(6)]
+    s_ty, s_tx, s_txy, s_tc0, s_tc1, s_tc2, s_tc3 = (wire.slot() for _ in range(7))
+    s_ex, s_ec0, s_ec1 = (wire.slot() for _ in range(3))
+
+    peers(
+        lambda k, to, _: wire.copy(
+            cond_parts.at[to], cond_all.at[fs], s_cond + k, {"fsdp": to}
+        ).start()
+    )
+    wire.push(lambda: chunk(ci), s_ty, to_y, None, lambda: tok_in.at[0])
+    wire.push(lambda: chunk(ci), s_tx, to_x, x == 0, lambda: tok_in.at[0])
+    wire.push(lambda: chunk(ci), s_tc0, to_c, None, lambda: tok_in.at[0])
+    for g in range(6):
+        peers(
+            lambda k, to, _, g=g: wire.copy(
+                groups[g][0], place(g, my_rows, y, x, c), s_z[g] + k, {"fsdp": to}
+            ).start()
+        )
+    wire.push(lambda: enc_part(cx), s_ex, to_x, None, lambda: enc_in.at[0])
+    wire.push(lambda: enc_part(cx), s_ec0, to_c, None, lambda: enc_in.at[0])
+
+    cond_all[fs] = cond_parts[fs]
+    peers(lambda k, _, src: wire.arrived(cond_all.at[src], s_cond + k, {"fsdp": src}))
+    for v in range(6):
+        part_out[:, v, :] = nn(
+            cond_all[:, 0, 0:rows].astype(BF), w_mod[:, v * D : (v + 1) * D]
+        )
+    part_out[:, 6:8, :] = jnp.zeros((n, 2, D), F)
+    peers(
+        lambda k, to, _: wire.copy(
+            part_out.at[to], part_in.at[fs], s_part + k, {"fsdp": to}
+        ).start()
+    )
+    part_in[fs] = part_out[fs]
+
+    def z_done(g):
+        local_copies[2 + g].wait()
+        peers(
+            lambda k, _, src: wire.arrived(
+                place(g, pl.ds(pl.multiple_of(src * rows, rows), rows), y, x, c),
+                s_z[g] + k,
+                {"fsdp": src},
+            )
+        )
+        slab = lambda: place(g, all_rows, y, x, c)
+        wire.push(slab, s_y[g], to_y)
+        if groups[g][3]:
+            wire.push(slab, s_x0[g], to_x)
+        wire.push(slab, s_c0[g], to_c)
+
+    def y_done(g):
+        slab = lambda: place(g, all_rows, 1 - y, x, c)
+        wire.arrived(slab(), s_y[g], to_y)
+        if groups[g][3]:
+            wire.push(slab, s_x1[g], to_x)
+        wire.push(slab, s_c1[g], to_c)
+
+    def x_done(g):
+        for yy, s_in, s_out in ((y, s_x0[g], s_c2[g]), (1 - y, s_x1[g], s_c3[g])):
+            slab = lambda yy=yy: place(g, all_rows, yy, 1 - x, c)
+            wire.arrived(slab(), s_in, to_x)
+            wire.push(slab, s_out, to_c)
+
+    def c_done(g):
+        wire.arrived(place(g, all_rows, y, x, 1 - c), s_c0[g], to_c)
+        wire.arrived(place(g, all_rows, 1 - y, x, 1 - c), s_c1[g], to_c)
+        if groups[g][3]:
+            wire.arrived(place(g, all_rows, y, 1 - x, 1 - c), s_c2[g], to_c)
+            wire.arrived(place(g, all_rows, 1 - y, 1 - x, 1 - c), s_c3[g], to_c)
+
+    local_copies[0].wait()
+    local_copies[1].wait()
+    ciy = 4 * x + 2 * c + 1 - y
+    cic = 4 * x + 2 * (1 - c) + y
+    ciyc = 4 * x + 2 * (1 - c) + 1 - y
+    low, lowy, lowc, lowyc = 2 * c + y, 2 * c + 1 - y, 2 * (1 - c) + y, 2 * (1 - c) + 1 - y
+    right = x == 1
+    wire.arrived(chunk(ciy), s_ty, to_y)
+    wire.push(lambda: chunk(ciy), s_txy, to_x, x == 0)
+    wire.push(lambda: chunk(ciy), s_tc1, to_c)
+    wire.arrived(chunk(low), s_tx, to_x, right)
+    wire.push(lambda: chunk(low), s_tc2, to_c, right)
+    z_done(0)
+    wire.arrived(enc_part(2 * (1 - x) + c), s_ex, to_x)
+    wire.push(lambda: enc_part(2 * (1 - x) + c), s_ec1, to_c)
+    wire.arrived(chunk(lowy), s_txy, to_x, right)
+    wire.push(lambda: chunk(lowy), s_tc3, to_c, right)
+    y_done(0)
+
+    peers(lambda k, _, src: wire.arrived(part_in.at[src], s_part + k, {"fsdp": src}))
+    mod[...] = jnp.sum(part_in[...], axis=0)
     sa, ba = mod[0:1, :], mod[1:2, :]
     sb, bb = mod[2:3, :], mod[3:4, :]
     sf, bf_ = mod[4:5, :], mod[5:6, :]
 
-    def parent_of(lb):
-        return jnp.clip(parents_ref[0, base + lb] - TRUNK, 0, BRANCHES - 1)
+    wire.arrived(chunk(cic), s_tc0, to_c)
+    wire.arrived(chunk(ciyc), s_tc1, to_c)
+    wire.arrived(chunk(lowc), s_tc2, to_c, right)
+    wire.arrived(chunk(lowyc), s_tc3, to_c, right)
+    wire.arrived(enc_part(2 * x + 1 - c), s_ec0, to_c)
+    wire.arrived(enc_part(2 * (1 - x) + 1 - c), s_ec1, to_c)
+    tok_tb = tok
+    tok_loc = tok.at[pl.ds(pl.multiple_of(ci * ROWS - off, 64), LOC), :]
+
+    def relay(step):
+        if step == 0:
+            z_done(1)
+            z_done(2)
+            z_done(3)
+        if step == 1:
+            for g in (1, 2, 3):
+                y_done(g)
+            z_done(4)
+        if step == 2:
+            z_done(5)
+            for g in (1, 2, 3):
+                c_done(g)
+        if step == 3:
+            y_done(4)
+            x_done(4)
+        if step == 4:
+            y_done(5)
+            x_done(5)
+        if step == 5:
+            c_done(4)
+            c_done(5)
+
+    def is_parent(lb, branch):
+        parent = jnp.full((32, D), parents_ref[0, base + lb], jnp.int32)
+        leaf = jnp.full((32, D), base + lb, jnp.int32) >= TRUNK + BRANCHES
+        return jnp.logical_and(leaf, parent == TRUNK + branch)
 
     def mask_trunk(rs):
         row = lax.broadcasted_iota(jnp.int32, (32, TRK), 0) + rs.start + ci * ROWS
@@ -177,24 +458,34 @@
 
     row_loop(LOC, 32, hid_loc)
     for lb in range(3):
-        at = pl.multiple_of(TRK + parent_of(lb) * BLK, BLK)
+        picks = [is_parent(lb, b) for b in range(1, BRANCHES)]
         for piece in range(4):
-            hid[TRK + lb * 256 + piece * 32 : TRK + lb * 256 + piece * 32 + 32, :] = hidden(
-                tok_tb[pl.ds(at + piece * 32, 32), :]
-            )
+            r = piece * 32
+            picked = tok_tb[TRK + r : TRK + r + 32, :].astype(F)
+            for b in range(1, BRANCHES):
+                at = TRK + b * BLK + r
+                picked = jnp.where(picks[b - 1], tok_tb[at : at + 32, :].astype(F), picked)
+            at = TRK + lb * 256 + r
+            hid[at : at + 32, :] = hidden(picked)
         hid[TRK + lb * 256 + BLK : TRK + lb * 256 + 2 * BLK, :] = hloc[
             lb * BLK : (lb + 1) * BLK, :
         ]
 
     def project(rs):
-        kbuf[rs, :] = nn(hid[rs, :], wqkv[1]).astype(BF)
-        vbuf[rs, :] = nn(hid[rs, :], wqkv[2]).astype(BF)
-
+        kbuf[rs, :] = nn(hid[rs, :], watt[1]).astype(BF)
+        vbuf[rs, :] = nn(hid[rs, :], watt[2]).astype(BF)
+
+    c_done(0)
     row_loop(KV, 256, project)
-    qbuf[...] = (nn(hloc[...], wqkv[0]) * 0.125).astype(BF)
+    relay(0)
+    qbuf[...] = (nn(hloc[...], watt[0]) * 0.125).astype(BF)
 
     @pl.loop(0, 4)
     def _(hp):
+        @pl.when(hp == 2)
+        def _():
+            relay(1)
+
         lanes = pl.ds(pl.multiple_of(hp * 128, 128), 128)
         kt = kbuf[0:TRK, lanes]
         for half in range(2):
@@ -231,7 +522,8 @@
         o1 = nn(pt[hp * 2 + 1], vt) + spec_o[1, own, :]
         mixa[:, lanes] = jnp.where(half_lanes(o0.shape, 0), o0, o1).astype(BF)
 
-    t0[...] = nt(mixa[...], wso[...])
+    relay(2)
+    t0[...] = nt(mixa[...], watt[3])
 
     def after_self(rs):
         ro = pl.ds(pl.multiple_of(rs.start + off, 32), 32)
@@ -242,9 +534,10 @@
 
     row_loop(ROWS, 32, after_self)
 
-    kenc[...] = nn(enc[...], wcqkv[1]).astype(BF)
-    venc[...] = nn(enc[...], wcqkv[2]).astype(BF)
-    qb[...] = (nn(hid_b[...], wcqkv[0]) * 0.125).astype(BF)
+    relay(3)
+    kenc[...] = nn(enc[...], watt[5]).astype(BF)
+    venc[...] = nn(enc[...], watt[6]).astype(BF)
+    qb[...] = (nn(hid_b[...], watt[4]) * 0.125).astype(BF)
 
     @pl.loop(0, 4)
     def _(hp):
@@ -267,7 +560,8 @@
         o1 = nn(pe[hp * 2 + 1], vt)
         mixb[:, lanes] = jnp.where(half_lanes(o0.shape, 0), o0, o1).astype(BF)
 
-    t0[...] = nt(mixb[...], wco[...])
+    relay(4)
+    t0[...] = nt(mixb[...], watt[7])
 
     def after_cross(rs):
         scv = stream_b[rs, :] + t0[rs, :]
@@ -277,6 +571,7 @@
 
     row_loop(ROWS, 32, after_cross)
 
+    relay(5)
     acc0[...] = jnp.zeros_like(acc0)
     acc1[...] = jnp.zeros_like(acc1)
 
@@ -321,7 +616,7 @@
     back_norm(4, sf, acc1, stream_c, cot, True)
 
     g_co[...] = tn(gbf[...], mixb[...]).astype(BF)
-    mgr[...] = nn(gbf[...], wco[...]).astype(BF)
+    mgr[...] = nn(gbf[...], watt[7]).astype(BF)
 
     @pl.loop(0, 4)
     def _(hp):
@@ -344,12 +639,12 @@
     g_cqkv[0] = tn(hid_b[...], dq[...]).astype(BF)
     g_cqkv[1] = tn(enc[...], dkb[0:ENC, :]).astype(BF)
     g_cqkv[2] = tn(enc[...], dvb[0:ENC, :]).astype(BF)
-    egrad[...] = (nt(dkb[0:ENC, :], wcqkv[1]) + nt(dvb[0:ENC, :], wcqkv[2])).astype(BF)
-    acc1[...] = nt(dq[...], wcqkv[0])
+    egrad[...] = (nt(dkb[0:ENC, :], watt[5]) + nt(dvb[0:ENC, :], watt[6])).astype(BF)
+    acc1[...] = nt(dq[...], watt[4])
     back_norm(2, sb, acc1, stream_b, gstream, False)
 
     g_so[...] = tn(gbf[...], mixa[...]).astype(BF)
-    mgr[...] = nn(gbf[...], wso[...]).astype(BF)
+    mgr[...] = nn(gbf[...], watt[3]).astype(BF)
 
     @pl.when(odd == 0)
     def _():
@@ -405,7 +700,7 @@
     wv_acc[...] = jnp.zeros_like(wv_acc)
 
     def key_side(rs):
-        gkv[rs, :] = nt(dkb[rs, :], wqkv[1]) + nt(dvb[rs, :], wqkv[2])
+        gkv[rs, :] = nt(dkb[rs, :], watt[1]) + nt(dvb[rs, :], watt[2])
         wk_acc[...] += tn(hid[rs, :], dkb[rs, :])
         wv_acc[...] += tn(hid[rs, :], dvb[rs, :])
 
@@ -413,7 +708,7 @@
     g_qkv[0] = tn(hloc[own, :], dq[...]).astype(BF)
     g_qkv[1] = wk_acc[...].astype(BF)
     g_qkv[2] = wv_acc[...].astype(BF)
-    gown[...] = nt(dq[...], wqkv[0])
+    gown[...] = nt(dq[...], watt[0])
 
     def put_trunk(rs):
         gpart[rs, :] = gkv[rs, :].astype(BF)
@@ -423,9 +718,7 @@
         for piece in range(4):
             total = jnp.zeros((32, D), F)
             for lb in range(3):
-                hit = jnp.logical_and(
-                    base + lb >= TRUNK + BRANCHES, parents_ref[0, base + lb] == TRUNK + b
-                )
+                hit = is_parent(lb, b)
                 part = gkv[TRK + lb * 256 + piece * 32 : TRK + lb * 256 + piece * 32 + 32, :]
                 total += jnp.where(hit, part, 0.0)
             at = TRK + b * BLK + piece * 32
@@ -435,12 +728,31 @@
             TRK + lb * 256 + BLK : TRK + (lb + 1) * 256, :
         ].astype(BF)
 
-
-def layer_call(parents, tok_tb, tok_loc, enc, cot, mod, weights):
+    wire.drain()
+    peers(
+        lambda k, to, _: wire.copy(
+            cond_parts.at[to], cond_all.at[fs], s_cond + k, {"fsdp": to}
+        ).wait_send()
+    )
+    peers(
+        lambda k, to, _: wire.copy(
+            part_out.at[to], part_in.at[fs], s_part + k, {"fsdp": to}
+        ).wait_send()
+    )
+    for g in range(6):
+        peers(
+            lambda k, to, _, g=g: wire.copy(
+                groups[g][0], place(g, my_rows, y, x, c), s_z[g] + k, {"fsdp": to}
+            ).wait_send()
+        )
+
+
+def layer_call(n, parents, cond_parts, w_mod, tokens, enc, cot, weights):
     vm = pl.BlockSpec(memory_space=pltpu.VMEM)
+    hbm = pl.BlockSpec(memory_space=pl.ANY)
     sds = jax.ShapeDtypeStruct
     return pl.pallas_call(
-        layer_kernel,
+        functools.partial(layer_kernel, n),
         out_shape=(
             sds((ROWS, D), BF),
             sds((ROWS, D), F),
@@ -448,6 +760,8 @@
             sds((ROWS, D), F),
             sds((ENC, D), BF),
             sds((8, D), F),
+            sds((8, D), F),
+            sds(cond_parts.shape, F),
             sds((3, D, D), BF),
             sds((D, D), BF),
             sds((3, D, D), BF),
@@ -455,9 +769,16 @@
             sds((D, FF), BF),
             sds((D, FF), BF),
         ),
-        in_specs=[pl.BlockSpec(memory_space=pltpu.SMEM)] + [vm] * 11,
-        out_specs=(vm,) * 12,
+        in_specs=[pl.BlockSpec(memory_space=pltpu.SMEM), vm, vm, hbm, hbm, vm] + [hbm] * 6,
+        out_specs=(vm,) * 14,
         scratch_shapes=[
+            pltpu.VMEM((8, D, D), BF),
+            pltpu.VMEM((D, FF), BF),
+            pltpu.VMEM((D, FF), BF),
+            pltpu.VMEM((8 * ROWS + 64, D), BF),
+            pltpu.VMEM((ENC, D), BF),
+            pltpu.VMEM((n, 8, D), F),
+            pltpu.VMEM((n, 8, D), F),
             pltpu.VMEM((KV, D), BF),
             pltpu.VMEM((LOC, D), BF),
             pltpu.VMEM((KV, D), BF),
@@ -494,10 +815,15 @@
             pltpu.VMEM((KV, D), F),
             pltpu.VMEM((D, D), F),
             pltpu.VMEM((D, D), F),
+            pltpu.SemaphoreType.DMA((8 * n + 66,)),
+            pltpu.SemaphoreType.DMA((8 * n + 66,)),
+            pltpu.SemaphoreType.DMA((8,)),
         ],
-        compiler_params=pltpu.CompilerParams(vmem_limit_bytes=VMEM_LIMIT),
+        compiler_params=pltpu.CompilerParams(
+            vmem_limit_bytes=VMEM_LIMIT, collective_id=0, has_side_effects=True
+        ),
         name="layer",
-    )(parents, tok_tb, tok_loc, enc, cot, mod, *weights)
+    )(parents, cond_parts, w_mod, tokens, enc, cot, *weights)
 
 
 def timestep_code(timesteps, width):
@@ -521,46 +847,29 @@
     w_down,
     cotangent,
 ):
-    fs = lax.axis_index("fsdp")
     rows = w_mod.shape[0]
     ci = lax.axis_index("ctx") * 2 + lax.axis_index("tp")
     condition = jax.nn.silu(timestep_code(timesteps, D)).astype(BF)
-    cond_all = lax.all_gather(condition, "fsdp", axis=0, tiled=True)
-    part = jnp.dot(
-        lax.dynamic_slice(cond_all, (0, fs * rows), (cond_all.shape[0], rows)),
+    n = lax.axis_size("fsdp")
+    padded_cond = jnp.pad(condition.astype(F).reshape(n, 1, rows), ((0, 0), (0, 7), (0, max(128 - rows, 0))))
+    (out, gstream, gpart, gown, egrad, mgrad, mod, cond_all, g_qkv, g_so, g_cqkv, g_co, g_up, g_dn) = layer_call(
+        n,
+        parents,
+        padded_cond,
         w_mod,
-        preferred_element_type=F,
+        tokens,
+        encoder_states,
+        cotangent[0],
+        (w_self_qkv, w_self_out, w_cross_qkv, w_cross_out, w_up, w_down),
     )
-    mod = lax.psum_scatter(part, "fsdp", scatter_dimension=0, tiled=True).reshape(6, D)
-    mod = jnp.concatenate([mod, jnp.zeros((2, D), F)])
-
-    def whole(w, axis):
-        return lax.all_gather(
-            lax.all_gather(w, "fsdp", axis=axis, tiled=True), "tp", axis=axis + 1, tiled=True
-        )
-
-    weights = (
-        whole(w_self_qkv, 1),
-        whole(w_self_out, 0),
-        whole(w_cross_qkv, 1),
-        whole(w_cross_out, 0),
-        whole(w_up, 0),
-        whole(w_down, 0),
-    )
-    every = lax.all_gather(tokens[0], ("ctx", "tp"), axis=0, tiled=True)
-    enc = lax.all_gather(encoder_states[0], "ctx", axis=0, tiled=True)
+    cond_mine = cond_all[:, 0, :rows]
     off = lax.rem(ci, 2) * 64
-    padded = jnp.concatenate([every, jnp.zeros((64, D), BF)])
-    tok_loc = lax.dynamic_slice(padded, (ci * ROWS - off, 0), (LOC, D))
-    (out, gstream, gpart, gown, egrad, mgrad, g_qkv, g_so, g_cqkv, g_co, g_up, g_dn) = layer_call(
-        parents, every[:SHARED], tok_loc, enc, cotangent[0], mod, weights
-    )
-    total = jnp.zeros(padded.shape, F)
+    total = jnp.zeros((8 * ROWS + 64, D), F)
     total = total.at[:SHARED].set(gpart[:SHARED].astype(F))
     window = lax.dynamic_slice(total, (ci * ROWS - off, 0), (LOC, D)) + gpart[SHARED:].astype(F)
     total = lax.dynamic_update_slice(total, window, (ci * ROWS - off, 0))
     mine = lax.psum_scatter(
-        total[: every.shape[0]].astype(BF), ("ctx", "tp"), scatter_dimension=0, tiled=True
+        total[: 8 * ROWS].astype(BF), ("ctx", "tp"), scatter_dimension=0, tiled=True
     )
     hidden_grad = mine.astype(F) + gown
     stream_grad, ds, db = norm_back(hidden_grad, tokens[0].astype(F), mod[0:1])
@@ -568,7 +877,6 @@
     mod_terms = jnp.concatenate([ds, db, mgrad[2:6]]).reshape(1, 6 * D)
     mod_total = lax.psum(mod_terms, ("ctx", "tp"))
     mod_all = lax.all_gather(mod_total, "fsdp", axis=0, tiled=True)
-    cond_mine = lax.dynamic_slice(cond_all, (0, fs * rows), (cond_all.shape[0], rows)).astype(F)
     grad_mod = jnp.dot(cond_mine.T, mod_all, precision=lax.Precision.HIGHEST)
     enc_grad = lax.psum(egrad.astype(F), "tp")
     enc_grad = lax.psum_scatter(enc_grad, "ctx", scatter_dimension=0, tiled=True)

time: 800 us -> 625 us (0.78)
  blocking collectives: 173 us -> 37.3 us
  waiting for transfers between devices: 477 us -> 383 us
  Pallas kernels: 104 us -> 164 us
    all_gather x8 -> x0, blocking collectives: 119 us -> none  [the longest x4 79.3 us: whole(): lax.all_gather(w, 'fsdp', axis=axis, tiled=True)]
    all_gather x7 -> x0, waiting for transfers between devices: 90.7 us -> none  [the longest x4 70.3 us: whole(): lax.all_gather(lax.all_gather(w, 'fsdp', axis=axis, tiled=True), 'tp', ax...]
    pallas_call x1, Pallas kernels: 104 us -> 164 us  [layer_call(): pl.pallas_call(functools.partial(layer_kernel, n), out_shape=(sds((ROWS,...]
    unnamed x1 -> x0, blocking collectives: 16.8 us -> none
  transfers between devices with their start and end apart: 23 -> 16, of which waited for: 19 -> 15; matrix products, arithmetic and copies ran while one was open for 3% -> 3% of each run, Pallas kernels for 0% -> 0%
where the time goes in v1:
time: 625 us
  waiting for transfers between devices  383 us (61%)
  Pallas kernels  164 us (26%)
  blocking collectives  37.3 us (6%)
  other arithmetic  16.4 us (3%)
  between operations  14.8 us (2%)
    pallas_call x1, Pallas kernels, layer_call(): pl.pallas_call(functools.partial(layer_kernel, n), out_shape=(sds((ROWS,...  164 us
    reduce_scatter x6, waiting for transfers between devices, owned(): g = lax.psum_scatter(g, 'tp', scatter_dimension=axis + 1, tiled=True)  152 us
    reduce_scatter x6, waiting for transfers between devices, owned(): lax.psum_scatter(g, 'fsdp', scatter_dimension=axis, tiled=True).astype(F)  142 us
    reduce_scatter x1, waiting for transfers between devices, per_device(): lax.psum_scatter(total[:8 * ROWS].astype(BF), ('ctx', 'tp'), scatter_dime...  47.2 us
    reduce_scatter x1, waiting for transfers between devices, per_device(): lax.psum_scatter(enc_grad, 'ctx', scatter_dimension=0, tiled=True)  25.6 us
    psum x1, blocking collectives, per_device(): mod_total = lax.psum(mod_terms, ('ctx', 'tp'))  24.1 us
    all_gather x1, blocking collectives, per_device(): mod_all = lax.all_gather(mod_total, 'fsdp', axis=0, tiled=True)  13.2 us
    psum x1, waiting for transfers between devices, per_device(): enc_grad = lax.psum(egrad.astype(F), 'tp')  13 us
  transfers between devices with their start and end apart: 16, of which 15 were waited for; matrix products, arithmetic and copies ran while one was open for 3% of the time, Pallas kernels for 0%

profile of v1, /device:TPU:0, one launch (start us, length us, event | category | flops | bytes accessed | tf_op | source)
XLA Modules:
  0.0 624.9 jit_solution(4890563418955753973)
XLA Ops:
  8.6 164.5 %layer.1 = (bf16[320,512]{1,0:T(8,128)(2,1)}, f32[320,512]{1,0:T(8,128)}, bf16[1920,512]{1,0:T(8,128)(2,1)}, f32[320,512]{1,0:T(8,128)}, bf16[512,512]{1,0:T(8,1...) custom-call(s32[1,20]{1,0:T(1,128)} %parents_ref.1, ...), custom_call_target="tpu_custom_call" | custom-call | tf_op jit(solution)/shard_map/layer/pallas_call | solution.py:754
  176.4 10.9 %reduce-scatter.19.cloned.1.call-done = bf16[512,256]{1,0:T(8,128)(2,1)} async-done(((bf16[512,512]{1,0:T(8,128)(2,1)}), bf16[512,256]{1,0:T(8,128)(2,1)}) %reduce-scatter.19.cloned.1.call-update) | async-done | bytes 262160 | tf_op jit(solution)/shard_map/reduce_scatter | solution.py:885
  187.4 16.9 %reduce-scatter.23.cloned.1.call-done = bf16[512,256]{1,0:T(8,128)(2,1)} async-done(((bf16[512,512]{1,0:T(8,128)(2,1)}), bf16[512,256]{1,0:T(8,128)(2,1)}) %reduce-scatter.23.cloned.1.call-update) | async-done | bytes 262160 | tf_op jit(solution)/shard_map/reduce_scatter | solution.py:885
  204.3 28.3 %reduce-scatter.17.cloned.1.call-done = bf16[3,512,256]{2,1,0:T(8,128)(2,1)} async-done(((bf16[3,512,512]{2,1,0:T(8,128)(2,1)}), bf16[3,512,256]{2,1,0:T(8,128)(2,1)}) %reduce-scatter.17.cloned.1.call-update) | async-done | bytes 786448 | tf_op jit(solution)/shard_map/reduce_scatter | solution.py:885
  232.7 28.2 %reduce-scatter.21.cloned.1.call-done = bf16[3,512,256]{2,1,0:T(8,128)(2,1)} async-done(((bf16[3,512,512]{2,1,0:T(8,128)(2,1)}), bf16[3,512,256]{2,1,0:T(8,128)(2,1)}) %reduce-scatter.21.cloned.1.call-update) | async-done | bytes 786448 | tf_op jit(solution)/shard_map/reduce_scatter | solution.py:885
  261.0 33.9 %reduce-scatter.25.cloned.1.call-done = bf16[512,1024]{1,0:T(8,128)(2,1)} async-done(((bf16[512,2048]{1,0:T(8,128)(2,1)}), bf16[512,1024]{1,0:T(8,128)(2,1)}) %reduce-scatter.25.cloned.1.call-update) | async-done | bytes 1048592 | tf_op jit(solution)/shard_map/reduce_scatter | solution.py:885
  294.9 34.0 %reduce-scatter.27.cloned.1.call-done = bf16[512,1024]{1,0:T(8,128)(2,1)} async-done(((bf16[512,2048]{1,0:T(8,128)(2,1)}), bf16[512,1024]{1,0:T(8,128)(2,1)}) %reduce-scatter.27.cloned.1.call-update) | async-done | bytes 1048592 | tf_op jit(solution)/shard_map/reduce_scatter | solution.py:885
  329.0 1.1 convert_element_type.68
  331.2 1.8 slice.45
  333.1 0.8 slice.39
  334.2 16.7 %reduce-scatter.33.cloned.1.call-done = bf16[128,256]{1,0:T(8,128)(2,1)} async-done(((bf16[512,256]{1,0:T(8,128)(2,1)}), bf16[128,256]{1,0:T(8,128)(2,1)}) %reduce-scatter.33.cloned.1.call-update) | async-done | bytes 65552 | tf_op jit(solution)/shard_map/reduce_scatter | solution.py:887
  350.9 20.3 %reduce-scatter.37.cloned.1.call-done = bf16[128,256]{1,0:T(8,128)(2,1)} async-done(((bf16[512,256]{1,0:T(8,128)(2,1)}), bf16[128,256]{1,0:T(8,128)(2,1)}) %reduce-scatter.37.cloned.1.call-update) | async-done | bytes 65552 | tf_op jit(solution)/shard_map/reduce_scatter | solution.py:887
  371.1 23.8 %reduce-scatter.31.cloned.1.call-done = bf16[3,128,256]{2,1,0:T(8,128)(2,1)} async-done(((bf16[3,512,256]{2,1,0:T(8,128)(2,1)}), bf16[3,128,256]{2,1,0:T(8,128)(2,1)}) %reduce-scatter.31.cloned.1.call-update) | async-done | bytes 196624 | tf_op jit(solution)/shard_map/reduce_scatter | solution.py:887
  394.9 24.7 %reduce-scatter.35.cloned.1.call-done = bf16[3,128,256]{2,1,0:T(8,128)(2,1)} async-done(((bf16[3,512,256]{2,1,0:T(8,128)(2,1)}), bf16[3,128,256]{2,1,0:T(8,128)(2,1)}) %reduce-scatter.35.cloned.1.call-update) | async-done | bytes 196624 | tf_op jit(solution)/shard_map/reduce_scatter | solution.py:887
  419.7 28.7 %reduce-scatter.39.cloned.1.call-done = bf16[128,1024]{1,0:T(8,128)(2,1)} async-done(((bf16[512,1024]{1,0:T(8,128)(2,1)}), bf16[128,1024]{1,0:T(8,128)(2,1)}) %reduce-scatter.39.cloned.1.call-update) | async-done | bytes 262160 | tf_op jit(solution)/shard_map/reduce_scatter | solution.py:887
  448.4 28.1 %reduce-scatter.41.cloned.1.call-done = bf16[128,1024]{1,0:T(8,128)(2,1)} async-done(((bf16[512,1024]{1,0:T(8,128)(2,1)}), bf16[128,1024]{1,0:T(8,128)(2,1)}) %reduce-scatter.41.cloned.1.call-update) | async-done | bytes 262160 | tf_op jit(solution)/shard_map/reduce_scatter | solution.py:887
  476.9 0.7 slice_add_fusion
  477.6 25.6 %reduce-scatter.29.cloned.1.call-done = f32[128,512]{1,0:T(8,128)} async-done(((f32[512,512]{1,0:T(8,128)}), f32[128,512]{1,0:T(8,128)}) %reduce-scatter.29.cloned.1.call-update) | async-done | bytes 262160 | tf_op jit(solution)/shard_map/reduce_scatter | solution.py:882
  503.2 47.2 %reduce-scatter.15.cloned.1.call-done = bf16[320,512]{1,0:T(8,128)(2,1)} async-done(((bf16[2560,512]{1,0:T(8,128)(2,1)}), bf16[320,512]{1,0:T(8,128)(2,1)}) %reduce-scatter.15.cloned.1.call-update) | async-done | bytes 327696 | tf_op jit(solution)/shard_map/reduce_scatter | solution.py:871
  550.5 1.4 fusion.11
  551.9 24.1 %psum.57 = f32[1,3072]{1,0:T(1,128)S(1)} all-reduce(f32[1,3072]{1,0:T(1,128)S(1)} %bitcast.58), channel_id=1, replica_groups=mesh['fsdp'=4,'ctx'=4,'tp'=2] {'ctx','tp'}, use_global_device_ids=true, to_apply=%region_9.10 | all-reduce | flops 3072 | bytes 24576 | tf_op jit(solution)/shard_map/psum | solution.py:878
  576.0 13.2 %all-gather = f32[4,1,3072]{2,1,0:T(1,128)S(1)} all-gather(f32[1,1,3072]{2,1,0:T(1,128)S(1)} %bitcast.59), channel_id=1, replica_groups=mesh['fsdp'=4,'ctx'=4,'tp'=2] {'fsdp'}, dimensions={0}, use_global_device_ids=true | all-gather | bytes 61440 | tf_op jit(solution)/shard_map/all_gather | solution.py:879
  589.2 2.1 fusion.10
  591.3 2.6 fusion.13
  593.9 1.5 convert_element_type.70
  595.4 1.5 convert_element_type.72
  596.9 1.7 convert_element_type.69
  598.6 1.7 convert_element_type.71
  600.3 1.8 convert_element_type.73
  602.1 0.8 convert_element_type.74
  603.0 13.0 %all-reduce.6.cloned.1.call-done = f32[128,512]{1,0:T(8,128)} async-done(((f32[128,512]{1,0:T(8,128)}), f32[128,512]{1,0:T(8,128)}) %all-reduce.6.cloned.1.call-update) | async-done | bytes 262160 | tf_op jit(solution)/shard_map/psum | solution.py:881
  616.7 1.7 copy.41
  (66 shorter events, 6.7 us)
Async XLA Ops:
  7.2 180.1 %reduce-scatter.19.cloned.1.call-start = ((), (), s32[]{:S(2)}) async-start(), calls=%async_computation.16 | async-start | bytes 786432 | tf_op jit(solution)/shard_map/reduce_scatter | solution.py:885
  173.1 31.1 %reduce-scatter.23.cloned.1.call-start = ((), (), s32[]{:S(2)}) async-start(), calls=%async_computation.18 | async-start | bytes 786432 | tf_op jit(solution)/shard_map/reduce_scatter | solution.py:885
  173.9 58.7 %reduce-scatter.17.cloned.1.call-start = ((), (), s32[]{:S(2)}) async-start(), calls=%async_computation.15 | async-start | bytes 2359296 | tf_op jit(solution)/shard_map/reduce_scatter | solution.py:885
  174.6 86.3 %reduce-scatter.21.cloned.1.call-start = ((), (), s32[]{:S(2)}) async-start(), calls=%async_computation.17 | async-start | bytes 2359296 | tf_op jit(solution)/shard_map/reduce_scatter | solution.py:885
  175.2 119.7 %reduce-scatter.25.cloned.1.call-start = ((), (), s32[]{:S(2)}) async-start(), calls=%async_computation.19 | async-start | bytes 3145728 | tf_op jit(solution)/shard_map/reduce_scatter | solution.py:885
  175.8 153.1 %reduce-scatter.27.cloned.1.call-start = ((), (), s32[]{:S(2)}) async-start(), calls=%async_computation.20 | async-start | bytes 3145728 | tf_op jit(solution)/shard_map/reduce_scatter | solution.py:885
  176.3 174.5 %reduce-scatter.33.cloned.1.call-start = ((), (), s32[]{:S(2)}) async-start(), calls=%async_computation.24 | async-start | bytes 327680 | tf_op jit(solution)/shard_map/reduce_scatter | solution.py:887
  187.3 141.7 %copy-start.4 = (bf16[512,512]{1,0:T(8,128)(2,1)S(1)}, bf16[512,512]{1,0:T(8,128)(2,1)}, u32[]{:S(2)}) copy-start(bf16[512,512]{1,0:T(8,128)(2,1)} %get-tuple-element.41) | copy-start | bytes 1572868
  187.3 183.8 %reduce-scatter.37.cloned.1.call-start = ((), (), s32[]{:S(2)}) async-start(), calls=%async_computation.26 | async-start | bytes 327680 | tf_op jit(solution)/shard_map/reduce_scatter | solution.py:887
  204.3 190.7 %reduce-scatter.31.cloned.1.call-start = ((), (), s32[]{:S(2)}) async-start(), calls=%async_computation.23 | async-start | bytes 983040 | tf_op jit(solution)/shard_map/reduce_scatter | solution.py:887
  232.6 187.1 %reduce-scatter.35.cloned.1.call-start = ((), (), s32[]{:S(2)}) async-start(), calls=%async_computation.25 | async-start | bytes 983040 | tf_op jit(solution)/shard_map/reduce_scatter | solution.py:887
  260.9 187.5 %reduce-scatter.39.cloned.1.call-start = ((), (), s32[]{:S(2)}) async-start(), calls=%async_computation.27 | async-start | bytes 1310720 | tf_op jit(solution)/shard_map/reduce_scatter | solution.py:887
  294.9 35.3 %copy-start.2 = (bf16[1920,512]{1,0:T(8,128)(2,1)S(1)}, bf16[1920,512]{1,0:T(8,128)(2,1)}, u32[]{:S(2)}) copy-start(bf16[1920,512]{1,0:T(8,128)(2,1)} %get-tuple-element.38) | copy-start | bytes 5898244
  294.9 181.7 %reduce-scatter.41.cloned.1.call-start = ((), (), s32[]{:S(2)}) async-start(), calls=%async_computation.28 | async-start | bytes 1310720 | tf_op jit(solution)/shard_map/reduce_scatter | solution.py:887
  328.9 174.3 %reduce-scatter.29.cloned.1.call-start = ((), (), s32[]{:S(2)}) async-start(), calls=%async_computation.21 | async-start | bytes 1310720 | tf_op jit(solution)/shard_map/reduce_scatter | solution.py:882
  330.1 220.3 %reduce-scatter.15.cloned.1.call-start = ((), (), s32[]{:S(2)}) async-start(), calls=%async_computation.14 | async-start | bytes 2949120 | tf_op jit(solution)/shard_map/reduce_scatter | solution.py:871
  333.0 0.9 copy-start.7
  333.0 1.0 copy-start
  333.0 217.4 %copy-start.1 = (f32[320,512]{1,0:T(8,128)S(1)}, f32[320,512]{1,0:T(8,128)}, u32[]{:S(2)}) copy-start(f32[320,512]{1,0:T(8,128)} %get-tuple-element.39) | copy-start | bytes 1966084
  333.0 256.1 %copy-start.3 = (f32[320,512]{1,0:T(8,128)S(1)}, f32[320,512]{1,0:T(8,128)}, u32[]{:S(2)}) copy-start(f32[320,512]{1,0:T(8,128)} %get-tuple-element.37) | copy-start | bytes 1966084
  333.1 260.8 %all-reduce.8.cloned.1.call-start = ((), (), s32[]{:S(2)}) async-start(), calls=%async_computation.29 | async-start | bytes 2097152 | tf_op jit(solution)/shard_map/psum | solution.py:886
  476.6 139.4 %all-reduce.6.cloned.1.call-start = ((), (), s32[]{:S(2)}) async-start(), calls=%async_computation.22 | async-start | bytes 524288 | tf_op jit(solution)/shard_map/psum | solution.py:881
  591.3 24.7 %copy-start.5 = (bf16[320,512]{1,0:T(8,128)(2,1)S(1)}, bf16[320,512]{1,0:T(8,128)(2,1)}, u32[]{:S(2)}) copy-start(bf16[320,512]{1,0:T(8,128)(2,1)} %get-tuple-element.36) | copy-start | bytes 983044
  593.9 8.3 %copy-start.6 = (bf16[128,1024]{1,0:T(8,128)(2,1)S(1)}, bf16[128,1024]{1,0:T(8,128)(2,1)}, u32[]{:S(2)}) copy-start(bf16[128,1024]{1,0:T(8,128)(2,1)} %get-tuple-element.59) | copy-start | bytes 786436
Sparse Core Ops, SparseCore 0:
  173.2 14.0 reduce-scatter.18
  189.6 14.5 reduce-scatter.22
  206.5 26.0 reduce-scatter.16
  234.8 26.0 reduce-scatter.20
  263.0 31.8 reduce-scatter.24
  297.0 31.8 reduce-scatter.26
  331.2 19.6 reduce-scatter.32
  353.2 17.8 reduce-scatter.36
  373.4 21.4 reduce-scatter.30
  397.1 22.5 reduce-scatter.34
  422.0 26.4 reduce-scatter.38
  450.7 25.8 reduce-scatter.40
  479.6 23.5 reduce-scatter.28
  506.7 43.6 reduce-scatter.14
  553.3 37.2 all-reduce.7
  592.6 23.2 all-reduce.5

commit v2 on v1

--- a/solution.py
+++ b/solution.py
@@ -142,19 +142,11 @@
     w_up,
     w_dn,
     out_ref,
-    gstream,
-    gpart,
-    gown,
-    egrad,
-    mgrad,
-    mod,
-    cond_all,
-    g_qkv,
-    g_so,
-    g_cqkv,
-    g_co,
-    g_up,
-    g_dn,
+    in_grad,
+    enc_out,
+    mod_out,
+    att_out,
+    ffn_out,
     watt,
     wup,
     wdn,
@@ -162,6 +154,10 @@
     enc,
     part_out,
     part_in,
+    mod,
+    cond_all,
+    tok_own,
+    mgrad,
     hid,
     hloc,
     kbuf,
@@ -184,8 +180,6 @@
     qb,
     pe,
     mixb,
-    t0,
-    t1,
     b0,
     b1,
     acc0,
@@ -193,15 +187,30 @@
     gbf,
     mgr,
     dq,
-    dkb,
-    dvb,
-    gkv,
     wk_acc,
     wv_acc,
+    gatt,
+    gffn,
+    egrad,
+    rc_att,
+    rx_att,
+    zr_att,
+    rg_att,
+    zr_ffn,
+    rg_ffn,
+    rc_g,
+    rx_g,
+    halo,
+    rc_e,
+    rx_e,
+    mod1,
+    mod2,
     send,
     recv,
     local,
+    ready,
 ):
+    t0, t1 = st.at[:, 0:D], st.at[:, D : 2 * D]
     fs = lax.axis_index("fsdp")
     cx = lax.axis_index("ctx")
     y = lax.axis_index("tp")
@@ -257,6 +266,7 @@
         pltpu.make_async_copy(groups[g][0], place(g, my_rows, y, x, c), local.at[2 + g])
         for g in range(6)
     ]
+    local_copies.append(pltpu.make_async_copy(tok_in.at[0], tok_own, local.at[8]))
     for copy in local_copies:
         copy.start()
 
@@ -371,6 +381,7 @@
     ciyc = 4 * x + 2 * (1 - c) + 1 - y
     low, lowy, lowc, lowyc = 2 * c + y, 2 * c + 1 - y, 2 * (1 - c) + y, 2 * (1 - c) + 1 - y
     right = x == 1
+    local_copies[8].wait()
     wire.arrived(chunk(ciy), s_ty, to_y)
     wire.push(lambda: chunk(ciy), s_txy, to_x, x == 0)
     wire.push(lambda: chunk(ciy), s_tc1, to_c)
@@ -421,15 +432,322 @@
             c_done(4)
             c_done(5)
 
+    spec_g = qbuf
+
     def is_parent(lb, branch):
         parent = jnp.full((32, D), parents_ref[0, base + lb], jnp.int32)
         leaf = jnp.full((32, D), base + lb, jnp.int32) >= TRUNK + BRANCHES
         return jnp.logical_and(leaf, parent == TRUNK + branch)
 
+    to_xy = {"ctx": 2 * (1 - x) + c, "tp": 1 - y}
+    s_rcf = [wire.slot() for _ in range(8)]
+    s_rxf = [wire.slot() for _ in range(6)]
+    s_zf = wire.slot(n)
+    s_gf = wire.slot(4)
+    s_rca = [[wire.slot(), wire.slot()] for _ in range(2)]
+    s_rxa = [[wire.slot() for _ in range(3)] for _ in range(2)]
+    s_za = [wire.slot(n) for _ in range(2)]
+    s_ga = [wire.slot(4) for _ in range(2)]
+    s_rcg, s_rcg4, s_rcg5, s_halo = (wire.slot() for _ in range(4))
+    s_rxg = [wire.slot() for _ in range(3)]
+    s_rce = [wire.slot(), wire.slot()]
+    s_rxe = [wire.slot() for _ in range(3)]
+    s_m1 = wire.slot(8)
+    s_m2 = wire.slot(n)
+    quad = ((to_y, x, 1 - y), (to_x, 1 - x, y), (to_xy, 1 - x, 1 - y))
+
+    def add_rows(target, terms, total, step=64):
+        def body(rs):
+            value = terms[0][rs, :].astype(F)
+            for term in terms[1:]:
+                value += term[rs, :].astype(F)
+            target[rs, :] = value.astype(BF)
+
+        row_loop(total, step, body)
+
+    def ctx_peers(make):
+        @pl.loop(1, 4)
+        def _(k):
+            make(k, lax.rem(cx + k, 4), lax.rem(cx + 4 - k, 4))
+
+    def strip(buf, at):
+        return buf.at[:, at * 256 : (at + 1) * 256]
+
+    def ffn_core_send():
+        wire.drain()
+        for target in (to_c, to_y, to_x, to_xy):
+            pl.semaphore_signal(ready, inc=1, device_id=target, device_id_type=MESH)
+        pl.semaphore_wait(ready, 4)
+        for t in range(4):
+            for m in range(2):
+                wire.push(
+                    lambda t=t, m=m: strip(wup, t * 2 + m),
+                    s_rcf[t * 2 + m],
+                    to_c,
+                    None,
+                    lambda t=t, m=m: gffn.at[m, :, ffn_cols(t // 2, t % 2, 1 - c)],
+                )
+
+    def ffn_chip_send():
+        for t in range(4):
+            for m in range(2):
+                wire.arrived(strip(wup, t * 2 + m), s_rcf[t * 2 + m], to_c)
+                own_slab = gffn.at[m, :, ffn_cols(t // 2, t % 2, c)]
+                add_rows(own_slab, (own_slab, strip(wup, t * 2 + m)), D)
+        for r, (target, xx, yy) in enumerate(quad):
+            for m in range(2):
+                wire.push(
+                    lambda r=r, m=m: strip(wdn, r * 2 + m),
+                    s_rxf[r * 2 + m],
+                    target,
+                    None,
+                    lambda m=m, xx=xx, yy=yy: gffn.at[m, :, ffn_cols(yy, xx, c)],
+                )
+
+    def ffn_tree_send():
+        for r, (target, _, _) in enumerate(quad):
+            for m in range(2):
+                wire.arrived(strip(wdn, r * 2 + m), s_rxf[r * 2 + m], target)
+        for m in range(2):
+            mine = gffn.at[m, :, ffn_cols(y, x, c)]
+            add_rows(mine, [mine] + [strip(wdn, r * 2 + m) for r in range(3)], D)
+        peers(lambda k, to, _: ffn_z(k, to).start())
+        zr_ffn[fs] = gffn[:, my_rows, ffn_cols(y, x, c)]
+
+    def ffn_z(k, to):
+        part = pl.ds(pl.multiple_of(to * rows, rows), rows)
+        return wire.copy(gffn.at[:, part, ffn_cols(y, x, c)], zr_ffn.at[fs], s_zf + k, {"fsdp": to})
+
+    def ffn_copy_send():
+        peers(lambda k, _, src: wire.arrived(zr_ffn.at[src], s_zf + k, {"fsdp": src}))
+        rg_ffn[cx] = jnp.sum(zr_ffn[...].astype(F), axis=0).astype(BF)
+        ctx_peers(lambda k, to, _: ffn_g(k, to).start())
+
+    def ffn_g(k, to):
+        return wire.copy(rg_ffn.at[cx], rg_ffn.at[cx], s_gf + k, {"ctx": to})
+
+    def ffn_finish():
+        ctx_peers(lambda k, _, src: wire.arrived(rg_ffn.at[src], s_gf + k, {"ctx": src}))
+        for q in range(4):
+            ffn_out[:, :, q * 256 : (q + 1) * 256] = rg_ffn[q].astype(F)
+
+    def att_core_send(a):
+        for yy in range(2):
+            wire.push(
+                lambda yy=yy: rc_att.at[a, yy],
+                s_rca[a][yy],
+                to_c,
+                None,
+                lambda yy=yy: gatt.at[4 * a : 4 * a + 4, :, att_cols(yy, 1 - c)],
+            )
+
+    def att_chip_send(a):
+        for yy in range(2):
+            wire.arrived(rc_att.at[a, yy], s_rca[a][yy], to_c)
+            for m in range(4):
+                mine = gatt.at[4 * a + m, :, att_cols(yy, c)]
+                add_rows(mine, (mine, rc_att.at[a, yy, m]), D)
+        for r, (target, xx, yy) in enumerate(quad):
+            wire.push(
+                lambda r=r: rx_att.at[a, r],
+                s_rxa[a][r],
+                target,
+                None,
+                lambda xx=xx, yy=yy: gatt.at[pl.ds(4 * a + 2 * xx, 2), :, att_cols(yy, c)],
+            )
+
+    def att_tree_send(a):
+        for r, (target, _, _) in enumerate(quad):
+            wire.arrived(rx_att.at[a, r], s_rxa[a][r], target)
+        for m in range(2):
+            mine = gatt.at[4 * a + 2 * x + m, :, att_cols(y, c)]
+            add_rows(mine, [mine] + [rx_att.at[a, r, m] for r in range(3)], D)
+        peers(lambda k, to, _: att_z(a, k, to).start())
+        zr_att[a, fs] = gatt[pl.ds(4 * a + 2 * x, 2), my_rows, att_cols(y, c)]
+
+    def att_z(a, k, to):
+        part = pl.ds(pl.multiple_of(to * rows, rows), rows)
+        return wire.copy(
+            gatt.at[pl.ds(4 * a + 2 * x, 2), part, att_cols(y, c)],
+            zr_att.at[a, fs],
+            s_za[a] + k,
+            {"fsdp": to},
+        )
+
+    def att_copy_send(a):
+        peers(lambda k, _, src: wire.arrived(zr_att.at[a, src], s_za[a] + k, {"fsdp": src}))
+        rg_att[a, cx] = jnp.sum(zr_att[a].astype(F), axis=0).astype(BF)
+        ctx_peers(lambda k, to, _: att_g(a, k, to).start())
+
+    def att_g(a, k, to):
+        return wire.copy(rg_att.at[a, cx], rg_att.at[a, cx], s_ga[a] + k, {"ctx": to})
+
+    def att_finish(a):
+        ctx_peers(lambda k, _, src: wire.arrived(rg_att.at[a, src], s_ga[a] + k, {"ctx": src}))
+        for q in range(4):
+            for m in range(2):
+                at = 4 * a + 2 * (q // 2) + m
+                att_out[at, :, (q % 2) * 128 : (q % 2) * 128 + 128] = rg_att[a, q, m].astype(F)
+
+    def enc_core_send():
+        for xx in range(2):
+            wire.push(
+                lambda xx=xx: rc_e.at[xx],
+                s_rce[xx],
+                to_c,
+                None,
+                lambda xx=xx: egrad.at[pl.ds(pl.multiple_of((2 * xx + 1 - c) * 128, 128), 128), :],
+            )
+
+    def enc_rows(xx):
+        return egrad.at[pl.ds(pl.multiple_of((2 * xx + c) * 128, 128), 128), :]
+
+    def enc_chip_send():
+        for xx in range(2):
+            wire.arrived(rc_e.at[xx], s_rce[xx], to_c)
+            add_rows(enc_rows(xx), (enc_rows(xx), rc_e.at[xx]), 128)
+        for r, (target, xx, _) in enumerate(quad):
+            wire.push(
+                lambda: rx_e.at[2 * x + y], s_rxe[r], target, None, lambda xx=xx: enc_rows(xx)
+            )
+        rx_e[2 * x + y] = enc_rows(x)[...]
+
+    def enc_finish():
+        for r, (target, xx, yy) in enumerate(quad):
+            wire.arrived(rx_e.at[2 * xx + yy], s_rxe[r], target)
+        enc_out[...] = jnp.sum(rx_e[...].astype(F), axis=0)
+
+    def shared_core_send():
+        to_core = pl.ds(pl.multiple_of(640 * (1 - c), 640), 640)
+        wire.push(lambda: rc_g.at[0:640], s_rcg, to_c, None, lambda: tok.at[to_core, :])
+        wire.push(
+            lambda: rc_g.at[640:896],
+            s_rcg4,
+            to_c,
+            jnp.logical_and(x == 1, c == 1),
+            lambda: tok.at[1280:1536, :],
+        )
+        wire.push(lambda: halo, s_halo, to_y, y == 1, lambda: spec_g.at[0:64, :])
+
+    def shared_chip_send():
+        wire.arrived(rc_g.at[0:640], s_rcg, to_c)
+        mine = tok.at[pl.ds(pl.multiple_of(640 * c, 640), 640), :]
+        add_rows(mine, (mine, rc_g.at[0:640]), 640)
+        last = jnp.logical_and(x == 1, c == 0)
+
+        @pl.when(last)
+        def _():
+            wire.arrived(rc_g.at[640:896], s_rcg4, to_c)
+            four = tok.at[1280:1536, :]
+            add_rows(four, (four, rc_g.at[640:896]), 256)
+
+        def rows_of(yy):
+            return lambda: chunk(2 * c + yy)
+
+        wire.push(lambda: rx_g.at[0], s_rxg[0], to_y, x == 0, rows_of(1 - y))
+        wire.push(lambda: rx_g.at[1], s_rxg[1], to_x, x == 1, rows_of(y))
+        wire.push(lambda: rx_g.at[2], s_rxg[2], to_xy, x == 1, rows_of(1 - y))
+        wire.push(
+            lambda: rx_g.at[0, 0:256],
+            s_rcg5,
+            to_y,
+            jnp.logical_and(last, y == 1),
+            lambda: tok.at[1280:1536, :],
+        )
+
+    def shared_arrived():
+        wire.arrived(rx_g.at[0], s_rxg[0], to_y, x == 0)
+        wire.arrived(rx_g.at[1], s_rxg[1], to_x, x == 0)
+        wire.arrived(rx_g.at[2], s_rxg[2], to_xy, x == 0)
+        wire.arrived(rx_g.at[0, 0:256], s_rcg5, to_y, ci == 4)
+
+    def tree_peers(make):
+        @pl.loop(1, 8)
+        def _(k):
+            make(k, lax.rem(ci + k, 8), lax.rem(ci + 8 - k, 8))
+
+    def device_of(i):
+        return {"ctx": i // 2, "tp": lax.rem(i, 2)}
+
+    def mod_1(k, to):
+        return wire.copy(mgrad, mod1.at[ci], s_m1 + k, device_of(to))
+
+    def mod_2(k, to):
+        return wire.copy(mod2.at[fs], mod2.at[fs], s_m2 + k, {"fsdp": to})
+
+    def mod_tree_send():
+        tree_peers(lambda k, to, _: mod_1(k, to).start())
+        mod1[ci] = mgrad[...]
+
+    def mod_all_send():
+        tree_peers(lambda k, _, src: wire.arrived(mod1.at[src], s_m1 + k, device_of(src)))
+        mod2[fs] = jnp.sum(mod1[...], axis=0)
+        peers(lambda k, to, _: mod_2(k, to).start())
+
+    def mod_finish():
+        peers(lambda k, _, src: wire.arrived(mod2.at[src], s_m2 + k, {"fsdp": src}))
+        cond = cond_all[:, 0, 0:rows]
+        for v in range(6):
+            held = (wk_acc, wv_acc)[v // 4]
+            at = (v % 4) * rows
+            held[at : at + rows, :] = lax.dot_general(
+                cond,
+                mod2[:, v, :],
+                (((0,), (0,)), ((), ())),
+                precision=lax.Precision.HIGHEST,
+                preferred_element_type=F,
+            )
+        copies = [
+            pltpu.make_async_copy(
+                (wk_acc, wv_acc)[v // 4].at[(v % 4) * rows : (v % 4 + 1) * rows, :],
+                mod_out.at[:, v * D : (v + 1) * D],
+                local.at[v],
+            )
+            for v in range(6)
+        ]
+        for copy in copies:
+            copy.start()
+        for copy in copies:
+            copy.wait()
+
+    def leave(step):
+        if step == 0:
+            ffn_core_send()
+        if step == 1:
+            att_core_send(1)
+            enc_core_send()
+            ffn_chip_send()
+        if step == 2:
+            att_chip_send(1)
+            enc_chip_send()
+            ffn_tree_send()
+        if step == 3:
+            ffn_copy_send()
+            att_tree_send(1)
+        if step == 4:
+            shared_core_send()
+        if step == 5:
+            att_core_send(0)
+        if step == 6:
+            shared_chip_send()
+            att_chip_send(0)
+            att_copy_send(1)
+            enc_finish()
+            ffn_finish()
+            shared_arrived()
+        if step == 7:
+            mod_tree_send()
+            att_tree_send(0)
+            mod_all_send()
+            att_copy_send(0)
+            att_finish(1)
+            mod_finish()
+            att_finish(0)
+
     def mask_trunk(rs):
         row = lax.broadcasted_iota(jnp.int32, (32, TRK), 0) + rs.start + ci * ROWS
         col = lax.broadcasted_iota(jnp.int32, (32, TRK), 1)
-        bias_t[rs, :] = jnp.where(col <= row, 0.0, NEG)
+        bias_t[rs, :] = jnp.where(col <= row, 0.0, NEG).astype(BF)
 
     row_loop(ROWS, 32, mask_trunk)
     for lb in range(3):
@@ -442,7 +760,7 @@
         )
         bias_s[lb * BLK : (lb + 1) * BLK, :] = jnp.where(
             jnp.logical_or(par_ok, self_ok), 0.0, NEG
-        )
+        ).astype(BF)
 
     def hidden(x):
         n, _ = normed(x.astype(F))
@@ -500,8 +818,8 @@
             def _(i):
                 rs = pl.ds(pl.multiple_of(i * 32, 32), 32)
                 ro = pl.ds(pl.multiple_of(i * 32 + off, 32), 32)
-                a = st[rs, :] + bias_t[rs, :]
-                b = ss[ro, :] + bias_s[ro, :]
+                a = st[rs, :] + bias_t[rs, :].astype(F)
+                b = ss[ro, :] + bias_s[ro, :].astype(F)
                 top = jnp.maximum(
                     jnp.max(a, axis=-1, keepdims=True), jnp.max(b, axis=-1, keepdims=True)
                 )
@@ -526,8 +844,7 @@
     t0[...] = nt(mixa[...], watt[3])
 
     def after_self(rs):
-        ro = pl.ds(pl.multiple_of(rs.start + off, 32), 32)
-        sbv = tok_loc[ro, :].astype(F) + t0[rs, :]
+        sbv = tok_own[rs, :].astype(F) + t0[rs, :]
         stream_b[rs, :] = sbv
         n, _ = normed(sbv)
         hid_b[rs, :] = (n * (1.0 + sb) + bb).astype(BF)
@@ -591,12 +908,8 @@
         row_loop(ROWS, 32, gelu)
         acc0[...] += nt(b0[...], wdn[:, cols])
         acc1[...] += nt(b1[...], wup[:, cols])
-        g_dn[:, cols] = tn(cot[...], b0[...]).astype(BF)
-        g_up[:, cols] = tn(hid_c[...], b1[...]).astype(BF)
-
-    def fold_mod(at, sums):
-        mgrad[at : at + 1, :] = sums[0]
-        mgrad[at + 1 : at + 2, :] = sums[1]
+        gffn[1, :, cols] = tn(cot[...], b0[...]).astype(BF)
+        gffn[0, :, cols] = tn(hid_c[...], b1[...]).astype(BF)
 
     def back_norm(at, scale, grad_src, stream_src, base_src, want_out):
         mgrad[at : at + 2, :] = jnp.zeros((2, D), F)
@@ -604,7 +917,7 @@
         def body(rs):
             back, ds, db = norm_back(grad_src[rs, :], stream_src[rs, :], scale)
             total = base_src[rs, :].astype(F) + back
-            gstream[rs, :] = total
+            in_grad[rs, :] = total
             gbf[rs, :] = total.astype(BF)
             mgrad[at : at + 1, :] += ds
             mgrad[at + 1 : at + 2, :] += db
@@ -613,9 +926,10 @@
 
         row_loop(ROWS, 32, body)
 
+    leave(0)
     back_norm(4, sf, acc1, stream_c, cot, True)
 
-    g_co[...] = tn(gbf[...], mixb[...]).astype(BF)
+    gatt[7] = tn(gbf[...], mixb[...]).astype(BF)
     mgr[...] = nn(gbf[...], watt[7]).astype(BF)
 
     @pl.loop(0, 4)
@@ -633,17 +947,18 @@
             dks.append(tn(b0[...], keep(qb[:, lanes], half)))
             dvs.append(tn(pe[h], mg))
         dq[:, lanes] = (jnp.where(half_lanes(dqs[0].shape, 0), dqs[0], dqs[1]) * 0.125).astype(BF)
-        dkb[0:ENC, lanes] = (dks[0] + dks[1]).astype(BF)
-        dvb[0:ENC, lanes] = (dvs[0] + dvs[1]).astype(BF)
-
-    g_cqkv[0] = tn(hid_b[...], dq[...]).astype(BF)
-    g_cqkv[1] = tn(enc[...], dkb[0:ENC, :]).astype(BF)
-    g_cqkv[2] = tn(enc[...], dvb[0:ENC, :]).astype(BF)
-    egrad[...] = (nt(dkb[0:ENC, :], watt[5]) + nt(dvb[0:ENC, :], watt[6])).astype(BF)
+        kenc[:, lanes] = (dks[0] + dks[1]).astype(BF)
+        venc[:, lanes] = (dvs[0] + dvs[1]).astype(BF)
+
+    gatt[4] = tn(hid_b[...], dq[...]).astype(BF)
+    gatt[5] = tn(enc[...], kenc[...]).astype(BF)
+    gatt[6] = tn(enc[...], venc[...]).astype(BF)
+    egrad[...] = (nt(kenc[...], watt[5]) + nt(venc[...], watt[6])).astype(BF)
+    leave(1)
     acc1[...] = nt(dq[...], watt[4])
-    back_norm(2, sb, acc1, stream_b, gstream, False)
-
-    g_so[...] = tn(gbf[...], mixa[...]).astype(BF)
+    back_norm(2, sb, acc1, stream_b, in_grad, False)
+
+    gatt[3] = tn(gbf[...], mixa[...]).astype(BF)
     mgr[...] = nn(gbf[...], watt[3]).astype(BF)
 
     @pl.when(odd == 0)
@@ -689,46 +1004,105 @@
             dks.append(tn(ds, qm))
             dvs.append(tn(pt[h], mg))
         dq[:, lanes] = (jnp.where(half_lanes(dqs[0].shape, 0), dqs[0], dqs[1]) * 0.125).astype(BF)
-        dkb[0:TRK, lanes] = (dks[0] + dks[1]).astype(BF)
-        dvb[0:TRK, lanes] = (dvs[0] + dvs[1]).astype(BF)
+        kbuf[0:TRK, lanes] = (dks[0] + dks[1]).astype(BF)
+        vbuf[0:TRK, lanes] = (dvs[0] + dvs[1]).astype(BF)
         for lb in range(3):
             k_rows = slice(TRK + lb * 256, TRK + (lb + 1) * 256)
-            dkb[k_rows, lanes] = (dks_s[lb][0] + dks_s[lb][1]).astype(BF)
-            dvb[k_rows, lanes] = (dvs_s[lb][0] + dvs_s[lb][1]).astype(BF)
+            kbuf[k_rows, lanes] = (dks_s[lb][0] + dks_s[lb][1]).astype(BF)
+            vbuf[k_rows, lanes] = (dvs_s[lb][0] + dvs_s[lb][1]).astype(BF)
+
+        @pl.when(hp == 1)
+        def _():
+            leave(2)
+
+        @pl.when(hp == 3)
+        def _():
+            leave(3)
 
     wk_acc[...] = jnp.zeros_like(wk_acc)
     wv_acc[...] = jnp.zeros_like(wv_acc)
 
     def key_side(rs):
-        gkv[rs, :] = nt(dkb[rs, :], watt[1]) + nt(dvb[rs, :], watt[2])
-        wk_acc[...] += tn(hid[rs, :], dkb[rs, :])
-        wv_acc[...] += tn(hid[rs, :], dvb[rs, :])
+        wk_acc[...] += tn(hid[rs, :], kbuf[rs, :])
+        wv_acc[...] += tn(hid[rs, :], vbuf[rs, :])
+        hid[rs, :] = (nt(kbuf[rs, :], watt[1]) + nt(vbuf[rs, :], watt[2])).astype(BF)
 
     row_loop(KV, 256, key_side)
-    g_qkv[0] = tn(hloc[own, :], dq[...]).astype(BF)
-    g_qkv[1] = wk_acc[...].astype(BF)
-    g_qkv[2] = wv_acc[...].astype(BF)
-    gown[...] = nt(dq[...], watt[0])
 
     def put_trunk(rs):
-        gpart[rs, :] = gkv[rs, :].astype(BF)
-
-    row_loop(TRK, 32, put_trunk)
+        tok[rs, :] = hid[rs, :]
+
+    row_loop(TRK, 64, put_trunk)
     for b in range(BRANCHES):
+        hits = [is_parent(lb, b) for lb in range(3)]
         for piece in range(4):
             total = jnp.zeros((32, D), F)
             for lb in range(3):
-                hit = is_parent(lb, b)
-                part = gkv[TRK + lb * 256 + piece * 32 : TRK + lb * 256 + piece * 32 + 32, :]
-                total += jnp.where(hit, part, 0.0)
+                at = TRK + lb * 256 + piece * 32
+                total += jnp.where(hits[lb], hid[at : at + 32, :].astype(F), 0.0)
             at = TRK + b * BLK + piece * 32
-            gpart[at : at + 32, :] = total.astype(BF)
+            tok[at : at + 32, :] = total.astype(BF)
     for lb in range(3):
-        gpart[SHARED + lb * BLK : SHARED + (lb + 1) * BLK, :] = gkv[
-            TRK + lb * 256 + BLK : TRK + (lb + 1) * 256, :
-        ].astype(BF)
+        spec_g[lb * BLK : (lb + 1) * BLK, :] = hid[TRK + lb * 256 + BLK : TRK + (lb + 1) * 256, :]
+
+    leave(4)
+    gatt[0] = tn(hloc[own, :], dq[...]).astype(BF)
+    gatt[1] = wk_acc[...].astype(BF)
+    gatt[2] = wv_acc[...].astype(BF)
+    leave(5)
+    acc1[...] = nt(dq[...], watt[0])
+    leave(6)
+
+    wire.arrived(halo, s_halo, to_y, y == 0)
+
+    def own_sum(rs):
+        extra = spec_g[pl.ds(pl.multiple_of(rs.start + off, 32), 32), :].astype(F)
+        acc1[rs, :] += extra
+
+    row_loop(ROWS, 32, own_sum)
+
+    @pl.when(y == 0)
+    def _():
+        acc1[ROWS - 64 : ROWS, :] += halo[...].astype(F)
+
+    @pl.when(x == 0)
+    def _():
+        def body(rs):
+            mine = tok[pl.ds(pl.multiple_of(ci * ROWS + rs.start, 32), 32), :].astype(F)
+            for r in range(3):
+                mine += rx_g[r, rs, :].astype(F)
+            acc1[rs, :] += mine
+
+        row_loop(ROWS, 32, body)
+
+    @pl.when(ci == 4)
+    def _():
+        def body(rs):
+            mine = tok[pl.ds(pl.multiple_of(4 * ROWS + rs.start, 32), 32), :].astype(F)
+            acc1[rs, :] += mine + rx_g[0, rs, :].astype(F)
+
+        row_loop(256, 32, body)
+
+    mgrad[0:2, :] = jnp.zeros((2, D), F)
+    mgrad[6:8, :] = jnp.zeros((2, D), F)
+
+    def first_norm(rs):
+        back, ds, db = norm_back(acc1[rs, :], tok_own[rs, :].astype(F), sa)
+        in_grad[rs, :] += back
+        mgrad[0:1, :] += ds
+        mgrad[1:2, :] += db
+
+    row_loop(ROWS, 32, first_norm)
+    leave(7)
 
     wire.drain()
+    peers(lambda k, to, _: ffn_z(k, to).wait_send())
+    ctx_peers(lambda k, to, _: ffn_g(k, to).wait_send())
+    for a in range(2):
+        peers(lambda k, to, _, a=a: att_z(a, k, to).wait_send())
+        ctx_peers(lambda k, to, _, a=a: att_g(a, k, to).wait_send())
+    tree_peers(lambda k, to, _: mod_1(k, to).wait_send())
+    peers(lambda k, to, _: mod_2(k, to).wait_send())
     peers(
         lambda k, to, _: wire.copy(
             cond_parts.at[to], cond_all.at[fs], s_cond + k, {"fsdp": to}
@@ -751,26 +1125,19 @@
     vm = pl.BlockSpec(memory_space=pltpu.VMEM)
     hbm = pl.BlockSpec(memory_space=pl.ANY)
     sds = jax.ShapeDtypeStruct
+    rows = w_mod.shape[0]
     return pl.pallas_call(
         functools.partial(layer_kernel, n),
         out_shape=(
             sds((ROWS, D), BF),
             sds((ROWS, D), F),
-            sds((SHARED + LOC, D), BF),
-            sds((ROWS, D), F),
-            sds((ENC, D), BF),
-            sds((8, D), F),
-            sds((8, D), F),
-            sds(cond_parts.shape, F),
-            sds((3, D, D), BF),
-            sds((D, D), BF),
-            sds((3, D, D), BF),
-            sds((D, D), BF),
-            sds((D, FF), BF),
-            sds((D, FF), BF),
+            sds((ENC // 4, D), F),
+            sds((rows, 6 * D), F),
+            sds((8, rows, 256), F),
+            sds((2, rows, 1024), F),
         ),
         in_specs=[pl.BlockSpec(memory_space=pltpu.SMEM), vm, vm, hbm, hbm, vm] + [hbm] * 6,
-        out_specs=(vm,) * 14,
+        out_specs=(vm, vm, vm, hbm, vm, vm),
         scratch_shapes=[
             pltpu.VMEM((8, D, D), BF),
             pltpu.VMEM((D, FF), BF),
@@ -779,6 +1146,10 @@
             pltpu.VMEM((ENC, D), BF),
             pltpu.VMEM((n, 8, D), F),
             pltpu.VMEM((n, 8, D), F),
+            pltpu.VMEM((8, D), F),
+            pltpu.VMEM((*cond_parts.shape,), F),
+            pltpu.VMEM((ROWS, D), BF),
+            pltpu.VMEM((8, D), F),
             pltpu.VMEM((KV, D), BF),
             pltpu.VMEM((LOC, D), BF),
             pltpu.VMEM((KV, D), BF),
@@ -786,8 +1157,8 @@
             pltpu.VMEM((LOC, D), BF),
             pltpu.VMEM((8, ROWS, TRK), BF),
             pltpu.VMEM((8, LOC, 256), BF),
-            pltpu.VMEM((ROWS, TRK), F),
-            pltpu.VMEM((LOC, 256), F),
+            pltpu.VMEM((ROWS, TRK), BF),
+            pltpu.VMEM((LOC, 256), BF),
             pltpu.VMEM((ROWS, TRK), F),
             pltpu.VMEM((LOC, 256), F),
             pltpu.VMEM((2, LOC, 128), F),
@@ -801,8 +1172,6 @@
             pltpu.VMEM((ROWS, D), BF),
             pltpu.VMEM((8, ROWS, ENC), BF),
             pltpu.VMEM((ROWS, D), BF),
-            pltpu.VMEM((ROWS, D), F),
-            pltpu.VMEM((ROWS, D), F),
             pltpu.VMEM((ROWS, D), BF),
             pltpu.VMEM((ROWS, D), BF),
             pltpu.VMEM((ROWS, D), F),
@@ -810,14 +1179,28 @@
             pltpu.VMEM((ROWS, D), BF),
             pltpu.VMEM((ROWS, D), BF),
             pltpu.VMEM((ROWS, D), BF),
-            pltpu.VMEM((KV, D), BF),
-            pltpu.VMEM((KV, D), BF),
-            pltpu.VMEM((KV, D), F),
             pltpu.VMEM((D, D), F),
             pltpu.VMEM((D, D), F),
-            pltpu.SemaphoreType.DMA((8 * n + 66,)),
-            pltpu.SemaphoreType.DMA((8 * n + 66,)),
-            pltpu.SemaphoreType.DMA((8,)),
+            pltpu.VMEM((8, D, D), BF),
+            pltpu.VMEM((2, D, FF), BF),
+            pltpu.VMEM((ENC, D), BF),
+            pltpu.VMEM((2, 2, 4, D, 128), BF),
+            pltpu.VMEM((2, 3, 2, D, 128), BF),
+            pltpu.VMEM((2, n, 2, rows, 128), BF),
+            pltpu.VMEM((2, 4, 2, rows, 128), BF),
+            pltpu.VMEM((n, 2, rows, 256), BF),
+            pltpu.VMEM((4, 2, rows, 256), BF),
+            pltpu.VMEM((896, D), BF),
+            pltpu.VMEM((3, ROWS, D), BF),
+            pltpu.VMEM((64, D), BF),
+            pltpu.VMEM((2, 128, D), BF),
+            pltpu.VMEM((4, 128, D), BF),
+            pltpu.VMEM((8, 8, D), F),
+            pltpu.VMEM((n, 8, D), F),
+            pltpu.SemaphoreType.DMA((12 * n + 124,)),
+            pltpu.SemaphoreType.DMA((12 * n + 124,)),
+            pltpu.SemaphoreType.DMA((9,)),
+            pltpu.SemaphoreType.REGULAR,
         ],
         compiler_params=pltpu.CompilerParams(
             vmem_limit_bytes=VMEM_LIMIT, collective_id=0, has_side_effects=True
@@ -848,11 +1231,10 @@
     cotangent,
 ):
     rows = w_mod.shape[0]
-    ci = lax.axis_index("ctx") * 2 + lax.axis_index("tp")
     condition = jax.nn.silu(timestep_code(timesteps, D)).astype(BF)
     n = lax.axis_size("fsdp")
     padded_cond = jnp.pad(condition.astype(F).reshape(n, 1, rows), ((0, 0), (0, 7), (0, max(128 - rows, 0))))
-    (out, gstream, gpart, gown, egrad, mgrad, mod, cond_all, g_qkv, g_so, g_cqkv, g_co, g_up, g_dn) = layer_call(
+    out, in_grad, enc_grad, grad_mod, att, ffn = layer_call(
         n,
         parents,
         padded_cond,
@@ -862,41 +1244,17 @@
         cotangent[0],
         (w_self_qkv, w_self_out, w_cross_qkv, w_cross_out, w_up, w_down),
     )
-    cond_mine = cond_all[:, 0, :rows]
-    off = lax.rem(ci, 2) * 64
-    total = jnp.zeros((8 * ROWS + 64, D), F)
-    total = total.at[:SHARED].set(gpart[:SHARED].astype(F))
-    window = lax.dynamic_slice(total, (ci * ROWS - off, 0), (LOC, D)) + gpart[SHARED:].astype(F)
-    total = lax.dynamic_update_slice(total, window, (ci * ROWS - off, 0))
-    mine = lax.psum_scatter(
-        total[: 8 * ROWS].astype(BF), ("ctx", "tp"), scatter_dimension=0, tiled=True
-    )
-    hidden_grad = mine.astype(F) + gown
-    stream_grad, ds, db = norm_back(hidden_grad, tokens[0].astype(F), mod[0:1])
-    input_grad = gstream + stream_grad
-    mod_terms = jnp.concatenate([ds, db, mgrad[2:6]]).reshape(1, 6 * D)
-    mod_total = lax.psum(mod_terms, ("ctx", "tp"))
-    mod_all = lax.all_gather(mod_total, "fsdp", axis=0, tiled=True)
-    grad_mod = jnp.dot(cond_mine.T, mod_all, precision=lax.Precision.HIGHEST)
-    enc_grad = lax.psum(egrad.astype(F), "tp")
-    enc_grad = lax.psum_scatter(enc_grad, "ctx", scatter_dimension=0, tiled=True)
-
-    def owned(g, axis):
-        g = lax.psum_scatter(g, "tp", scatter_dimension=axis + 1, tiled=True)
-        g = lax.psum(g, "ctx")
-        return lax.psum_scatter(g, "fsdp", scatter_dimension=axis, tiled=True).astype(F)
-
     return (
         out[None],
-        input_grad[None],
+        in_grad[None],
         enc_grad[None],
         grad_mod,
-        owned(g_qkv, 1),
-        owned(g_so, 0),
-        owned(g_cqkv, 1),
-        owned(g_co, 0),
-        owned(g_up, 0),
-        owned(g_dn, 0),
+        att[0:3],
+        att[3],
+        att[4:7],
+        att[7],
+        ffn[0],
+        ffn[1],
     )
 
 

time: 625 us -> 240 us (0.38)
  waiting for transfers between devices: 383 us -> 0 us
  Pallas kernels: 164 us -> 230 us
  blocking collectives: 37.3 us -> 0 us
  other arithmetic: 16.4 us -> 0.69 us
  between operations: 14.8 us -> 1.34 us
    reduce_scatter x14 -> x0, waiting for transfers between devices: 367 us -> none  [the longest x6 152 us: owned(): g = lax.psum_scatter(g, 'tp', scatter_dimension=axis + 1, tiled=True)]
    pallas_call x1, Pallas kernels: 164 us -> 230 us  [layer_call(): pl.pallas_call(functools.partial(layer_kernel, n), out_shape=(sds((ROWS,...]
    psum x1 -> x0, blocking collectives: 24.1 us -> none  [per_device(): mod_total = lax.psum(mod_terms, ('ctx', 'tp'))]
    all_gather x1 -> x0, blocking collectives: 13.2 us -> none  [per_device(): mod_all = lax.all_gather(mod_total, 'fsdp', axis=0, tiled=True)]
    psum x2 -> x0, waiting for transfers between devices: 13 us -> none  [the longest x1 13 us: per_device(): enc_grad = lax.psum(egrad.astype(F), 'tp')]
    convert_element_type x7 -> x0, other arithmetic: 10.2 us -> none  [the longest x6 9.09 us: owned(): lax.psum_scatter(g, 'fsdp', scatter_dimension=axis, tiled=True).astype(F)]
  transfers between devices with their start and end apart: 16 -> 0, of which waited for: 15 -> 0; matrix products, arithmetic and copies ran while one was open for 3% -> 0% of each run, Pallas kernels for 0% -> 0%
where the time goes in v2:
time: 240 us
  Pallas kernels  230 us (96%)
  local copies, waits for them, and re-layouts  8.4 us (4%)
    pallas_call x1, Pallas kernels, layer_call(): pl.pallas_call(functools.partial(layer_kernel, n), out_shape=(sds((ROWS,...  230 us

profile of v2, /device:TPU:0, one launch (start us, length us, event | category | flops | bytes accessed | tf_op | source)
XLA Modules:
  0.0 240.0 jit_solution(2512435466120348351)
XLA Ops:
  1.3 0.1 fusion.2
  1.4 0.6 pad_convert_fusion.cond_parts
  2.0 229.6 %layer.1 = (bf16[320,512]{1,0:T(8,128)(2,1)}, f32[320,512]{1,0:T(8,128)}, f32[128,512]{1,0:T(8,128)}, f32[128,3072]{1,0:T(8,128)}, f32[8,128,256]{2,1,0:T(8,128)}, /*index=5*/f32[2,128,1024]{2,1,0:T(8,128)}) custom-call(s32[1,20]{1,0:T(1,128)} %parents_ref.1, f32[4,8,128]{2,1,0:T(8,128)} %pad_convert_fusion.cond_parts, bf16[128,3072]{1,0:T(8,128)(2,1)} %w_mod.1, ...), custom_call_target="tpu_custom_call" | custom-call | tf_op jit(solution)/shard_map/layer/pallas_call | solution.py:1129
  231.6 0.0 copy-start.1
  231.6 1.8 slice_bitcast_fusion.2
  233.4 0.0 copy-start.3
  233.4 2.1 fusion.4
  235.5 0.0 copy-start.2
  235.5 0.0 copy-done.1
  235.5 0.0 copy-start.4
  235.5 1.1 slice_bitcast_fusion
  236.6 0.0 copy-start
  236.6 0.0 copy-done.3
  236.6 0.7 copy.29
  237.4 0.0 copy-done.2
  237.4 0.8 copy.30
  238.2 0.0 copy-done.4
  238.2 0.7 copy.31
  238.9 0.0 copy-done
  238.9 1.1 copy.32
  (2 shorter events, 0.0 us)
Async XLA Ops:
  231.6 3.9 %copy-start.1 = (f32[2,128,1024]{2,1,0:T(8,128)S(1)}, f32[2,128,1024]{2,1,0:T(8,128)}, u32[]{:S(2)}) copy-start(f32[2,128,1024]{2,1,0:T(8,128)} %get-tuple-element.21) | copy-start | bytes 3145732
  233.4 3.2 %copy-start.3 = (bf16[320,512]{1,0:T(8,128)(2,1)S(1)}, bf16[320,512]{1,0:T(8,128)(2,1)}, u32[]{:S(2)}) copy-start(bf16[320,512]{1,0:T(8,128)(2,1)} %get-tuple-element.16) | copy-start | bytes 983044
  235.5 1.8 copy-start.2
  235.5 2.7 %copy-start.4 = (f32[128,512]{1,0:T(8,128)S(1)}, f32[128,512]{1,0:T(8,128)}, u32[]{:S(2)}) copy-start(f32[128,512]{1,0:T(8,128)} %get-tuple-element.18) | copy-start | bytes 786436
  236.6 2.3 copy-start

commit v3 on v2

--- a/solution.py
+++ b/solution.py
@@ -57,10 +57,16 @@
     return back, jnp.sum(grad * n, axis=0, keepdims=True), jnp.sum(grad, axis=0, keepdims=True)
 
 
-def row_loop(total, step, body):
-    @pl.loop(0, total // step)
+def row_loop(total, step, body, unroll=1):
+    if unroll == 0:
+        for i in range(total // step):
+            body(pl.ds(i * step, step))
+        return
+
+    @pl.loop(0, total // (step * unroll))
     def _(i):
-        body(pl.ds(pl.multiple_of(i * step, step), step))
+        for j in range(unroll):
+            body(pl.ds(pl.multiple_of((i * unroll + j) * step, step), step))
 
 
 def half_lanes(shape, half):
@@ -316,14 +322,35 @@
     wire.push(lambda: chunk(ci), s_ty, to_y, None, lambda: tok_in.at[0])
     wire.push(lambda: chunk(ci), s_tx, to_x, x == 0, lambda: tok_in.at[0])
     wire.push(lambda: chunk(ci), s_tc0, to_c, None, lambda: tok_in.at[0])
-    for g in range(6):
+
+    def z_start(g):
         peers(
-            lambda k, to, _, g=g: wire.copy(
+            lambda k, to, _: wire.copy(
                 groups[g][0], place(g, my_rows, y, x, c), s_z[g] + k, {"fsdp": to}
             ).start()
         )
+
+    z_start(0)
     wire.push(lambda: enc_part(cx), s_ex, to_x, None, lambda: enc_in.at[0])
     wire.push(lambda: enc_part(cx), s_ec0, to_c, None, lambda: enc_in.at[0])
+
+    def mask_trunk(rs):
+        row = lax.broadcasted_iota(jnp.int32, (32, TRK), 0) + rs.start + ci * ROWS
+        col = lax.broadcasted_iota(jnp.int32, (32, TRK), 1)
+        bias_t[rs, :] = jnp.where(col <= row, 0.0, NEG).astype(BF)
+
+    row_loop(ROWS, 32, mask_trunk)
+    for lb in range(3):
+        blk = base + lb
+        row = lax.broadcasted_iota(jnp.int32, (BLK, 2 * BLK), 0)
+        col = lax.broadcasted_iota(jnp.int32, (BLK, 2 * BLK), 1)
+        par_ok = jnp.logical_and(col < BLK, blk >= TRUNK + BRANCHES)
+        self_ok = jnp.logical_and(
+            jnp.logical_and(col >= BLK, col - BLK <= row), blk >= TRUNK
+        )
+        bias_s[lb * BLK : (lb + 1) * BLK, :] = jnp.where(
+            jnp.logical_or(par_ok, self_ok), 0.0, NEG
+        ).astype(BF)
 
     cond_all[fs] = cond_parts[fs]
     peers(lambda k, _, src: wire.arrived(cond_all.at[src], s_cond + k, {"fsdp": src}))
@@ -388,6 +415,8 @@
     wire.arrived(chunk(low), s_tx, to_x, right)
     wire.push(lambda: chunk(low), s_tc2, to_c, right)
     z_done(0)
+    for g in (1, 2, 3):
+        z_start(g)
     wire.arrived(enc_part(2 * (1 - x) + c), s_ex, to_x)
     wire.push(lambda: enc_part(2 * (1 - x) + c), s_ec1, to_c)
     wire.arrived(chunk(lowy), s_txy, to_x, right)
@@ -411,24 +440,26 @@
 
     def relay(step):
         if step == 0:
-            z_done(1)
-            z_done(2)
-            z_done(3)
+            for g in (1, 2, 3):
+                z_done(g)
+            z_start(4)
+            z_start(5)
         if step == 1:
-            for g in (1, 2, 3):
-                y_done(g)
             z_done(4)
         if step == 2:
             z_done(5)
             for g in (1, 2, 3):
-                c_done(g)
+                y_done(g)
         if step == 3:
             y_done(4)
+        if step == 4:
+            for g in (1, 2, 3):
+                c_done(g)
+            y_done(5)
             x_done(4)
-        if step == 4:
-            y_done(5)
+        if step == 5:
             x_done(5)
-        if step == 5:
+        if step == 6:
             c_done(4)
             c_done(5)
 
@@ -440,14 +471,6 @@
         return jnp.logical_and(leaf, parent == TRUNK + branch)
 
     to_xy = {"ctx": 2 * (1 - x) + c, "tp": 1 - y}
-    s_rcf = [wire.slot() for _ in range(8)]
-    s_rxf = [wire.slot() for _ in range(6)]
-    s_zf = wire.slot(n)
-    s_gf = wire.slot(4)
-    s_rca = [[wire.slot(), wire.slot()] for _ in range(2)]
-    s_rxa = [[wire.slot() for _ in range(3)] for _ in range(2)]
-    s_za = [wire.slot(n) for _ in range(2)]
-    s_ga = [wire.slot(4) for _ in range(2)]
     s_rcg, s_rcg4, s_rcg5, s_halo = (wire.slot() for _ in range(4))
     s_rxg = [wire.slot() for _ in range(3)]
     s_rce = [wire.slot(), wire.slot()]
@@ -473,117 +496,148 @@
     def strip(buf, at):
         return buf.at[:, at * 256 : (at + 1) * 256]
 
+    class Family:
+        def __init__(self, unit, core_box, box, landing, held, shape_rows):
+            self.unit, self.core_box, self.box = unit, core_box, box
+            self.landing, self.held = landing, held
+            self.s_core = [[wire.slot() for _ in range(4)] for _ in range(2)]
+            self.s_one = [[wire.slot() for _ in range(2)] for _ in range(2)]
+            self.s_two = [wire.slot() for _ in range(2)]
+            self.s_z = [wire.slot(n) for _ in range(2)]
+            self.s_g = wire.slot(4)
+
+        def core_send(self):
+            for m in range(2):
+                for t in range(4):
+                    wire.push(
+                        lambda m=m, t=t: self.core_box(m, t),
+                        self.s_core[m][t],
+                        to_c,
+                        None,
+                        lambda m=m, t=t: self.unit(m, t // 2, t % 2, 1 - c),
+                    )
+
+        def first_send(self):
+            for m in range(2):
+                for t in range(4):
+                    wire.arrived(self.core_box(m, t), self.s_core[m][t], to_c)
+                    mine = self.unit(m, t // 2, t % 2, c)
+                    add_rows(mine, (mine, self.core_box(m, t)), D)
+            for j in range(2):
+                wire.push(
+                    lambda j=j: self.box(j),
+                    self.s_one[0][j],
+                    to_x,
+                    None,
+                    lambda j=j: self.unit(0, j, 1 - x, c),
+                )
+                wire.push(
+                    lambda j=j: self.box(2 + j),
+                    self.s_one[1][j],
+                    to_y,
+                    None,
+                    lambda j=j: self.unit(1, 1 - y, j, c),
+                )
+
+        def second_send(self):
+            for j in range(2):
+                wire.arrived(self.box(j), self.s_one[0][j], to_x)
+                mine = self.unit(0, j, x, c)
+                add_rows(mine, (mine, self.box(j)), D)
+            wire.push(
+                lambda: self.box(4),
+                self.s_two[0],
+                to_y,
+                None,
+                lambda: self.unit(0, 1 - y, x, c),
+            )
+            for j in range(2):
+                wire.arrived(self.box(2 + j), self.s_one[1][j], to_y)
+                mine = self.unit(1, y, j, c)
+                add_rows(mine, (mine, self.box(2 + j)), D)
+            wire.push(
+                lambda: self.box(5),
+                self.s_two[1],
+                to_x,
+                None,
+                lambda: self.unit(1, y, 1 - x, c),
+            )
+
+        def z_copy(self, m, k, to):
+            part = pl.ds(pl.multiple_of(to * rows, rows), rows)
+            return wire.copy(
+                self.unit(m, y, x, c).at[part, :],
+                self.landing.at[fs, m],
+                self.s_z[m] + k,
+                {"fsdp": to},
+            )
+
+        def tree_send(self):
+            for m, target in ((0, to_y), (1, to_x)):
+                wire.arrived(self.box(4 + m), self.s_two[m], target)
+                mine = self.unit(m, y, x, c)
+                add_rows(mine, (mine, self.box(4 + m)), D)
+                peers(lambda k, to, _, m=m: self.z_copy(m, k, to).start())
+                self.landing[fs, m] = self.unit(m, y, x, c)[my_rows, :]
+
+        def g_copy(self, k, to):
+            return wire.copy(self.held.at[cx], self.held.at[cx], self.s_g + k, {"ctx": to})
+
+        def copy_send(self):
+            for m in range(2):
+                peers(
+                    lambda k, _, src, m=m: wire.arrived(
+                        self.landing.at[src, m], self.s_z[m] + k, {"fsdp": src}
+                    )
+                )
+            self.held[cx] = jnp.sum(self.landing[...].astype(F), axis=0).astype(BF)
+            ctx_peers(lambda k, to, _: self.g_copy(k, to).start())
+
+        def collect(self):
+            ctx_peers(
+                lambda k, _, src: wire.arrived(self.held.at[src], self.s_g + k, {"ctx": src})
+            )
+
+        def drain(self):
+            for m in range(2):
+                peers(lambda k, to, _, m=m: self.z_copy(m, k, to).wait_send())
+            ctx_peers(lambda k, to, _: self.g_copy(k, to).wait_send())
+
+    ffn = Family(
+        lambda m, yy, xx, cc: gffn.at[m, :, ffn_cols(yy, xx, cc)],
+        lambda m, t: strip(wup, m * 4 + t),
+        lambda i: strip(wdn, i),
+        zr_ffn,
+        rg_ffn,
+        rows,
+    )
+
+    def attention_family(a):
+        return Family(
+            lambda m, yy, xx, cc: gatt.at[4 * a + 2 * xx + m, :, att_cols(yy, cc)],
+            lambda m, t: rc_att.at[a, m, t],
+            lambda i: rx_att.at[a, i],
+            zr_att.at[a],
+            rg_att.at[a],
+            rows,
+        )
+
+    att = (attention_family(0), attention_family(1))
+
     def ffn_core_send():
         wire.drain()
-        for target in (to_c, to_y, to_x, to_xy):
+        for target in (to_c, to_y, to_x):
             pl.semaphore_signal(ready, inc=1, device_id=target, device_id_type=MESH)
-        pl.semaphore_wait(ready, 4)
-        for t in range(4):
-            for m in range(2):
-                wire.push(
-                    lambda t=t, m=m: strip(wup, t * 2 + m),
-                    s_rcf[t * 2 + m],
-                    to_c,
-                    None,
-                    lambda t=t, m=m: gffn.at[m, :, ffn_cols(t // 2, t % 2, 1 - c)],
-                )
-
-    def ffn_chip_send():
-        for t in range(4):
-            for m in range(2):
-                wire.arrived(strip(wup, t * 2 + m), s_rcf[t * 2 + m], to_c)
-                own_slab = gffn.at[m, :, ffn_cols(t // 2, t % 2, c)]
-                add_rows(own_slab, (own_slab, strip(wup, t * 2 + m)), D)
-        for r, (target, xx, yy) in enumerate(quad):
-            for m in range(2):
-                wire.push(
-                    lambda r=r, m=m: strip(wdn, r * 2 + m),
-                    s_rxf[r * 2 + m],
-                    target,
-                    None,
-                    lambda m=m, xx=xx, yy=yy: gffn.at[m, :, ffn_cols(yy, xx, c)],
-                )
-
-    def ffn_tree_send():
-        for r, (target, _, _) in enumerate(quad):
-            for m in range(2):
-                wire.arrived(strip(wdn, r * 2 + m), s_rxf[r * 2 + m], target)
-        for m in range(2):
-            mine = gffn.at[m, :, ffn_cols(y, x, c)]
-            add_rows(mine, [mine] + [strip(wdn, r * 2 + m) for r in range(3)], D)
-        peers(lambda k, to, _: ffn_z(k, to).start())
-        zr_ffn[fs] = gffn[:, my_rows, ffn_cols(y, x, c)]
-
-    def ffn_z(k, to):
-        part = pl.ds(pl.multiple_of(to * rows, rows), rows)
-        return wire.copy(gffn.at[:, part, ffn_cols(y, x, c)], zr_ffn.at[fs], s_zf + k, {"fsdp": to})
-
-    def ffn_copy_send():
-        peers(lambda k, _, src: wire.arrived(zr_ffn.at[src], s_zf + k, {"fsdp": src}))
-        rg_ffn[cx] = jnp.sum(zr_ffn[...].astype(F), axis=0).astype(BF)
-        ctx_peers(lambda k, to, _: ffn_g(k, to).start())
-
-    def ffn_g(k, to):
-        return wire.copy(rg_ffn.at[cx], rg_ffn.at[cx], s_gf + k, {"ctx": to})
+        pl.semaphore_wait(ready, 3)
+        ffn.core_send()
 
     def ffn_finish():
-        ctx_peers(lambda k, _, src: wire.arrived(rg_ffn.at[src], s_gf + k, {"ctx": src}))
+        ffn.collect()
         for q in range(4):
             ffn_out[:, :, q * 256 : (q + 1) * 256] = rg_ffn[q].astype(F)
 
-    def att_core_send(a):
-        for yy in range(2):
-            wire.push(
-                lambda yy=yy: rc_att.at[a, yy],
-                s_rca[a][yy],
-                to_c,
-                None,
-                lambda yy=yy: gatt.at[4 * a : 4 * a + 4, :, att_cols(yy, 1 - c)],
-            )
-
-    def att_chip_send(a):
-        for yy in range(2):
-            wire.arrived(rc_att.at[a, yy], s_rca[a][yy], to_c)
-            for m in range(4):
-                mine = gatt.at[4 * a + m, :, att_cols(yy, c)]
-                add_rows(mine, (mine, rc_att.at[a, yy, m]), D)
-        for r, (target, xx, yy) in enumerate(quad):
-            wire.push(
-                lambda r=r: rx_att.at[a, r],
-                s_rxa[a][r],
-                target,
-                None,
-                lambda xx=xx, yy=yy: gatt.at[pl.ds(4 * a + 2 * xx, 2), :, att_cols(yy, c)],
-            )
-
-    def att_tree_send(a):
-        for r, (target, _, _) in enumerate(quad):
-            wire.arrived(rx_att.at[a, r], s_rxa[a][r], target)
-        for m in range(2):
-            mine = gatt.at[4 * a + 2 * x + m, :, att_cols(y, c)]
-            add_rows(mine, [mine] + [rx_att.at[a, r, m] for r in range(3)], D)
-        peers(lambda k, to, _: att_z(a, k, to).start())
-        zr_att[a, fs] = gatt[pl.ds(4 * a + 2 * x, 2), my_rows, att_cols(y, c)]
-
-    def att_z(a, k, to):
-        part = pl.ds(pl.multiple_of(to * rows, rows), rows)
-        return wire.copy(
-            gatt.at[pl.ds(4 * a + 2 * x, 2), part, att_cols(y, c)],
-            zr_att.at[a, fs],
-            s_za[a] + k,
-            {"fsdp": to},
-        )
-
-    def att_copy_send(a):
-        peers(lambda k, _, src: wire.arrived(zr_att.at[a, src], s_za[a] + k, {"fsdp": src}))
-        rg_att[a, cx] = jnp.sum(zr_att[a].astype(F), axis=0).astype(BF)
-        ctx_peers(lambda k, to, _: att_g(a, k, to).start())
-
-    def att_g(a, k, to):
-        return wire.copy(rg_att.at[a, cx], rg_att.at[a, cx], s_ga[a] + k, {"ctx": to})
-
     def att_finish(a):
-        ctx_peers(lambda k, _, src: wire.arrived(rg_att.at[a, src], s_ga[a] + k, {"ctx": src}))
+        att[a].collect()
         for q in range(4):
             for m in range(2):
                 at = 4 * a + 2 * (q // 2) + m
@@ -629,7 +683,7 @@
         )
         wire.push(lambda: halo, s_halo, to_y, y == 1, lambda: spec_g.at[0:64, :])
 
-    def shared_chip_send():
+    def shared_y_send():
         wire.arrived(rc_g.at[0:640], s_rcg, to_c)
         mine = tok.at[pl.ds(pl.multiple_of(640 * c, 640), 640), :]
         add_rows(mine, (mine, rc_g.at[0:640]), 640)
@@ -644,22 +698,24 @@
         def rows_of(yy):
             return lambda: chunk(2 * c + yy)
 
-        wire.push(lambda: rx_g.at[0], s_rxg[0], to_y, x == 0, rows_of(1 - y))
-        wire.push(lambda: rx_g.at[1], s_rxg[1], to_x, x == 1, rows_of(y))
-        wire.push(lambda: rx_g.at[2], s_rxg[2], to_xy, x == 1, rows_of(1 - y))
+        wire.push(lambda: rx_g.at[0], s_rxg[0], to_y, None, rows_of(1 - y))
         wire.push(
-            lambda: rx_g.at[0, 0:256],
+            lambda: rx_g.at[1, 0:256],
             s_rcg5,
             to_y,
             jnp.logical_and(last, y == 1),
             lambda: tok.at[1280:1536, :],
         )
 
+    def shared_x_send():
+        wire.arrived(rx_g.at[0], s_rxg[0], to_y)
+        mine = chunk(2 * c + y)
+        add_rows(mine, (mine, rx_g.at[0]), ROWS)
+        wire.push(lambda: rx_g.at[1], s_rxg[1], to_x, x == 1, lambda: chunk(2 * c + y))
+
     def shared_arrived():
-        wire.arrived(rx_g.at[0], s_rxg[0], to_y, x == 0)
         wire.arrived(rx_g.at[1], s_rxg[1], to_x, x == 0)
-        wire.arrived(rx_g.at[2], s_rxg[2], to_xy, x == 0)
-        wire.arrived(rx_g.at[0, 0:256], s_rcg5, to_y, ci == 4)
+        wire.arrived(rx_g.at[1, 0:256], s_rcg5, to_y, ci == 4)
 
     def tree_peers(make):
         @pl.loop(1, 8)
@@ -714,53 +770,41 @@
         if step == 0:
             ffn_core_send()
         if step == 1:
-            att_core_send(1)
+            ffn.first_send()
+        if step == 2:
+            att[1].core_send()
             enc_core_send()
-            ffn_chip_send()
-        if step == 2:
-            att_chip_send(1)
+        if step == 3:
+            att[1].first_send()
             enc_chip_send()
-            ffn_tree_send()
-        if step == 3:
-            ffn_copy_send()
-            att_tree_send(1)
         if step == 4:
+            ffn.second_send()
+        if step == 5:
+            att[1].second_send()
+            ffn.tree_send()
+        if step == 6:
             shared_core_send()
-        if step == 5:
-            att_core_send(0)
-        if step == 6:
-            shared_chip_send()
-            att_chip_send(0)
-            att_copy_send(1)
+        if step == 7:
+            att[0].core_send()
+            shared_y_send()
+        if step == 8:
+            att[0].first_send()
+            att[1].tree_send()
+            ffn.copy_send()
+            shared_x_send()
             enc_finish()
+            att[0].second_send()
+            att[1].copy_send()
             ffn_finish()
             shared_arrived()
-        if step == 7:
+        if step == 9:
             mod_tree_send()
-            att_tree_send(0)
+            att[0].tree_send()
+            att_finish(1)
             mod_all_send()
-            att_copy_send(0)
-            att_finish(1)
+            att[0].copy_send()
             mod_finish()
             att_finish(0)
-
-    def mask_trunk(rs):
-        row = lax.broadcasted_iota(jnp.int32, (32, TRK), 0) + rs.start + ci * ROWS
-        col = lax.broadcasted_iota(jnp.int32, (32, TRK), 1)
-        bias_t[rs, :] = jnp.where(col <= row, 0.0, NEG).astype(BF)
-
-    row_loop(ROWS, 32, mask_trunk)
-    for lb in range(3):
-        blk = base + lb
-        row = lax.broadcasted_iota(jnp.int32, (BLK, 2 * BLK), 0)
-        col = lax.broadcasted_iota(jnp.int32, (BLK, 2 * BLK), 1)
-        par_ok = jnp.logical_and(col < BLK, blk >= TRUNK + BRANCHES)
-        self_ok = jnp.logical_and(
-            jnp.logical_and(col >= BLK, col - BLK <= row), blk >= TRUNK
-        )
-        bias_s[lb * BLK : (lb + 1) * BLK, :] = jnp.where(
-            jnp.logical_or(par_ok, self_ok), 0.0, NEG
-        ).astype(BF)
 
     def hidden(x):
         n, _ = normed(x.astype(F))
@@ -769,12 +813,12 @@
     def hid_trunk(rs):
         hid[rs, :] = hidden(tok_tb[rs, :])
 
-    row_loop(TRK, 32, hid_trunk)
+    row_loop(TRK, 32, hid_trunk, 8)
 
     def hid_loc(rs):
         hloc[rs, :] = hidden(tok_loc[rs, :])
 
-    row_loop(LOC, 32, hid_loc)
+    row_loop(LOC, 32, hid_loc, 6)
     for lb in range(3):
         picks = [is_parent(lb, b) for b in range(1, BRANCHES)]
         for piece in range(4):
@@ -795,52 +839,55 @@
 
     c_done(0)
     row_loop(KV, 256, project)
-    relay(0)
     qbuf[...] = (nn(hloc[...], watt[0]) * 0.125).astype(BF)
+
+    linv_a, linv_b = wk_acc.at[0:ROWS, :], wv_acc.at[0:ROWS, :]
+
+    def with_ones(values, half):
+        return jnp.where(half_lanes(values.shape, half), values, jnp.ones_like(values))
+
+    def finish_heads(o0, o1, mixed, linv, lanes):
+        inv0, inv1 = 1.0 / pltpu.roll(o0, HD, 1), 1.0 / pltpu.roll(o1, HD, 1)
+        first = half_lanes(o0.shape, 0)
+        mixed[:, lanes] = jnp.where(first, o0 * inv0, o1 * inv1).astype(BF)
+        linv[:, lanes] = jnp.where(first, inv0, inv1)
 
     @pl.loop(0, 4)
     def _(hp):
-        @pl.when(hp == 2)
-        def _():
-            relay(1)
+        for step in range(4):
+
+            @pl.when(hp == step)
+            def _(step=step):
+                relay(step)
 
         lanes = pl.ds(pl.multiple_of(hp * 128, 128), 128)
         kt = kbuf[0:TRK, lanes]
+        vt = vbuf[0:TRK, lanes]
+        outs = []
         for half in range(2):
             h = hp * 2 + half
-            st[...] = nt(keep(qbuf[own, lanes], half), kt)
+            st[...] = nt(keep(qbuf[own, lanes], half), kt) + bias_t[...].astype(F)
             for lb in range(3):
                 r = slice(lb * BLK, (lb + 1) * BLK)
                 ks = kbuf[TRK + lb * 256 : TRK + (lb + 1) * 256, lanes]
-                ss[r, :] = nt(keep(qbuf[r, lanes], half), ks)
-
-            @pl.loop(0, ROWS // 32)
-            def _(i):
-                rs = pl.ds(pl.multiple_of(i * 32, 32), 32)
+                ss[r, :] = nt(keep(qbuf[r, lanes], half), ks) + bias_s[r, :].astype(F)
+            for i in range(ROWS // 32):
+                rs = slice(i * 32, i * 32 + 32)
                 ro = pl.ds(pl.multiple_of(i * 32 + off, 32), 32)
-                a = st[rs, :] + bias_t[rs, :].astype(F)
-                b = ss[ro, :] + bias_s[ro, :].astype(F)
+                a, b = st[rs, :], ss[ro, :]
                 top = jnp.maximum(
                     jnp.max(a, axis=-1, keepdims=True), jnp.max(b, axis=-1, keepdims=True)
                 )
-                a = jnp.exp(a - top)
-                b = jnp.exp(b - top)
-                inv = 1.0 / (
-                    jnp.sum(a, axis=-1, keepdims=True) + jnp.sum(b, axis=-1, keepdims=True)
-                )
-                pt[h, rs, :] = (a * inv).astype(BF)
-                ps[h, ro, :] = (b * inv).astype(BF)
-
+                pt[h, rs, :] = jnp.exp(a - top).astype(BF)
+                ps[h, ro, :] = jnp.exp(b - top).astype(BF)
             for lb in range(3):
                 r = slice(lb * BLK, (lb + 1) * BLK)
                 vs = vbuf[TRK + lb * 256 : TRK + (lb + 1) * 256, lanes]
-                spec_o[half, r, :] = nn(ps[h, r, :], vs)
-        vt = vbuf[0:TRK, lanes]
-        o0 = nn(pt[hp * 2], vt) + spec_o[0, own, :]
-        o1 = nn(pt[hp * 2 + 1], vt) + spec_o[1, own, :]
-        mixa[:, lanes] = jnp.where(half_lanes(o0.shape, 0), o0, o1).astype(BF)
-
-    relay(2)
+                spec_o[half, r, :] = nn(ps[h, r, :], with_ones(vs, half))
+            outs.append(nn(pt[h], with_ones(vt, half)) + spec_o[half, own, :])
+        finish_heads(outs[0], outs[1], mixa, linv_a, lanes)
+
+    relay(4)
     t0[...] = nt(mixa[...], watt[3])
 
     def after_self(rs):
@@ -849,9 +896,8 @@
         n, _ = normed(sbv)
         hid_b[rs, :] = (n * (1.0 + sb) + bb).astype(BF)
 
-    row_loop(ROWS, 32, after_self)
-
-    relay(3)
+    row_loop(ROWS, 32, after_self, 0)
+
     kenc[...] = nn(enc[...], watt[5]).astype(BF)
     venc[...] = nn(enc[...], watt[6]).astype(BF)
     qb[...] = (nn(hid_b[...], watt[4]) * 0.125).astype(BF)
@@ -860,24 +906,19 @@
     def _(hp):
         lanes = pl.ds(pl.multiple_of(hp * 128, 128), 128)
         kt = kenc[:, lanes]
+        vt = venc[:, lanes]
+        outs = []
         for half in range(2):
             h = hp * 2 + half
             t0[...] = nt(keep(qb[:, lanes], half), kt)
-
-            @pl.loop(0, ROWS // 32)
-            def _(i):
-                rs = pl.ds(pl.multiple_of(i * 32, 32), 32)
+            for i in range(ROWS // 32):
+                rs = slice(i * 32, i * 32 + 32)
                 a = t0[rs, :]
-                a = jnp.exp(a - jnp.max(a, axis=-1, keepdims=True))
-                inv = 1.0 / jnp.sum(a, axis=-1, keepdims=True)
-                pe[h, rs, :] = (a * inv).astype(BF)
-
-        vt = venc[:, lanes]
-        o0 = nn(pe[hp * 2], vt)
-        o1 = nn(pe[hp * 2 + 1], vt)
-        mixb[:, lanes] = jnp.where(half_lanes(o0.shape, 0), o0, o1).astype(BF)
-
-    relay(4)
+                pe[h, rs, :] = jnp.exp(a - jnp.max(a, axis=-1, keepdims=True)).astype(BF)
+            outs.append(nn(pe[h], with_ones(vt, half)))
+        finish_heads(outs[0], outs[1], mixb, linv_b, lanes)
+
+    relay(5)
     t0[...] = nt(mixb[...], watt[7])
 
     def after_cross(rs):
@@ -886,9 +927,9 @@
         n, _ = normed(scv)
         hid_c[rs, :] = (n * (1.0 + sf) + bf_).astype(BF)
 
-    row_loop(ROWS, 32, after_cross)
-
-    relay(5)
+    row_loop(ROWS, 32, after_cross, 0)
+
+    relay(6)
     acc0[...] = jnp.zeros_like(acc0)
     acc1[...] = jnp.zeros_like(acc1)
 
@@ -912,25 +953,24 @@
         gffn[0, :, cols] = tn(hid_c[...], b1[...]).astype(BF)
 
     def back_norm(at, scale, grad_src, stream_src, base_src, want_out):
-        mgrad[at : at + 2, :] = jnp.zeros((2, D), F)
-
-        def body(rs):
+        sums = [jnp.zeros((1, D), F), jnp.zeros((1, D), F)]
+        for i in range(ROWS // 32):
+            rs = slice(i * 32, i * 32 + 32)
             back, ds, db = norm_back(grad_src[rs, :], stream_src[rs, :], scale)
             total = base_src[rs, :].astype(F) + back
             in_grad[rs, :] = total
             gbf[rs, :] = total.astype(BF)
-            mgrad[at : at + 1, :] += ds
-            mgrad[at + 1 : at + 2, :] += db
+            sums = [sums[0] + ds, sums[1] + db]
             if want_out:
                 out_ref[rs, :] = (stream_c[rs, :] + acc0[rs, :]).astype(BF)
-
-        row_loop(ROWS, 32, body)
+        mgrad[at : at + 1, :] = sums[0]
+        mgrad[at + 1 : at + 2, :] = sums[1]
 
     leave(0)
     back_norm(4, sf, acc1, stream_c, cot, True)
 
     gatt[7] = tn(gbf[...], mixb[...]).astype(BF)
-    mgr[...] = nn(gbf[...], watt[7]).astype(BF)
+    mgr[...] = (nn(gbf[...], watt[7]) * linv_b[...]).astype(BF)
 
     @pl.loop(0, 4)
     def _(hp):
@@ -950,16 +990,17 @@
         kenc[:, lanes] = (dks[0] + dks[1]).astype(BF)
         venc[:, lanes] = (dvs[0] + dvs[1]).astype(BF)
 
+    leave(1)
     gatt[4] = tn(hid_b[...], dq[...]).astype(BF)
     gatt[5] = tn(enc[...], kenc[...]).astype(BF)
     gatt[6] = tn(enc[...], venc[...]).astype(BF)
     egrad[...] = (nt(kenc[...], watt[5]) + nt(venc[...], watt[6])).astype(BF)
-    leave(1)
+    leave(2)
     acc1[...] = nt(dq[...], watt[4])
     back_norm(2, sb, acc1, stream_b, in_grad, False)
 
     gatt[3] = tn(gbf[...], mixa[...]).astype(BF)
-    mgr[...] = nn(gbf[...], watt[3]).astype(BF)
+    mgr[...] = (nn(gbf[...], watt[3]) * linv_a[...]).astype(BF)
 
     @pl.when(odd == 0)
     def _():
@@ -1011,13 +1052,11 @@
             kbuf[k_rows, lanes] = (dks_s[lb][0] + dks_s[lb][1]).astype(BF)
             vbuf[k_rows, lanes] = (dvs_s[lb][0] + dvs_s[lb][1]).astype(BF)
 
-        @pl.when(hp == 1)
-        def _():
-            leave(2)
-
-        @pl.when(hp == 3)
-        def _():
-            leave(3)
+        for step in range(3):
+
+            @pl.when(hp == step)
+            def _(step=step):
+                leave(3 + step)
 
     wk_acc[...] = jnp.zeros_like(wk_acc)
     wv_acc[...] = jnp.zeros_like(wv_acc)
@@ -1045,13 +1084,13 @@
     for lb in range(3):
         spec_g[lb * BLK : (lb + 1) * BLK, :] = hid[TRK + lb * 256 + BLK : TRK + (lb + 1) * 256, :]
 
-    leave(4)
+    leave(6)
     gatt[0] = tn(hloc[own, :], dq[...]).astype(BF)
     gatt[1] = wk_acc[...].astype(BF)
     gatt[2] = wv_acc[...].astype(BF)
-    leave(5)
+    leave(7)
     acc1[...] = nt(dq[...], watt[0])
-    leave(6)
+    leave(8)
 
     wire.arrived(halo, s_halo, to_y, y == 0)
 
@@ -1059,7 +1098,7 @@
         extra = spec_g[pl.ds(pl.multiple_of(rs.start + off, 32), 32), :].astype(F)
         acc1[rs, :] += extra
 
-    row_loop(ROWS, 32, own_sum)
+    row_loop(ROWS, 32, own_sum, 5)
 
     @pl.when(y == 0)
     def _():
@@ -1069,9 +1108,7 @@
     def _():
         def body(rs):
             mine = tok[pl.ds(pl.multiple_of(ci * ROWS + rs.start, 32), 32), :].astype(F)
-            for r in range(3):
-                mine += rx_g[r, rs, :].astype(F)
-            acc1[rs, :] += mine
+            acc1[rs, :] += mine + rx_g[1, rs, :].astype(F)
 
         row_loop(ROWS, 32, body)
 
@@ -1079,28 +1116,24 @@
     def _():
         def body(rs):
             mine = tok[pl.ds(pl.multiple_of(4 * ROWS + rs.start, 32), 32), :].astype(F)
-            acc1[rs, :] += mine + rx_g[0, rs, :].astype(F)
+            acc1[rs, :] += mine + rx_g[1, rs, :].astype(F)
 
         row_loop(256, 32, body)
 
-    mgrad[0:2, :] = jnp.zeros((2, D), F)
     mgrad[6:8, :] = jnp.zeros((2, D), F)
-
-    def first_norm(rs):
+    sums = [jnp.zeros((1, D), F), jnp.zeros((1, D), F)]
+    for i in range(ROWS // 32):
+        rs = slice(i * 32, i * 32 + 32)
         back, ds, db = norm_back(acc1[rs, :], tok_own[rs, :].astype(F), sa)
         in_grad[rs, :] += back
-        mgrad[0:1, :] += ds
-        mgrad[1:2, :] += db
-
-    row_loop(ROWS, 32, first_norm)
-    leave(7)
+        sums = [sums[0] + ds, sums[1] + db]
+    mgrad[0:1, :] = sums[0]
+    mgrad[1:2, :] = sums[1]
+    leave(9)
 
     wire.drain()
-    peers(lambda k, to, _: ffn_z(k, to).wait_send())
-    ctx_peers(lambda k, to, _: ffn_g(k, to).wait_send())
-    for a in range(2):
-        peers(lambda k, to, _, a=a: att_z(a, k, to).wait_send())
-        ctx_peers(lambda k, to, _, a=a: att_g(a, k, to).wait_send())
+    for family in (ffn, *att):
+        family.drain()
     tree_peers(lambda k, to, _: mod_1(k, to).wait_send())
     peers(lambda k, to, _: mod_2(k, to).wait_send())
     peers(
@@ -1185,20 +1218,20 @@
             pltpu.VMEM((2, D, FF), BF),
             pltpu.VMEM((ENC, D), BF),
             pltpu.VMEM((2, 2, 4, D, 128), BF),
-            pltpu.VMEM((2, 3, 2, D, 128), BF),
+            pltpu.VMEM((2, 6, D, 128), BF),
             pltpu.VMEM((2, n, 2, rows, 128), BF),
             pltpu.VMEM((2, 4, 2, rows, 128), BF),
             pltpu.VMEM((n, 2, rows, 256), BF),
             pltpu.VMEM((4, 2, rows, 256), BF),
             pltpu.VMEM((896, D), BF),
-            pltpu.VMEM((3, ROWS, D), BF),
+            pltpu.VMEM((2, ROWS, D), BF),
             pltpu.VMEM((64, D), BF),
             pltpu.VMEM((2, 128, D), BF),
             pltpu.VMEM((4, 128, D), BF),
             pltpu.VMEM((8, 8, D), F),
             pltpu.VMEM((n, 8, D), F),
-            pltpu.SemaphoreType.DMA((12 * n + 124,)),
-            pltpu.SemaphoreType.DMA((12 * n + 124,)),
+            pltpu.SemaphoreType.DMA((16 * n + 160,)),
+            pltpu.SemaphoreType.DMA((16 * n + 160,)),
             pltpu.SemaphoreType.DMA((9,)),
             pltpu.SemaphoreType.REGULAR,
         ],

time: 240 us -> 177 us (0.74)
  Pallas kernels: 230 us -> 167 us
    pallas_call x1, Pallas kernels: 230 us -> 167 us  [layer_call(): pl.pallas_call(functools.partial(layer_kernel, n), out_shape=(sds((ROWS,...]
where the time goes in v3:
time: 177 us
  Pallas kernels  167 us (94%)
  local copies, waits for them, and re-layouts  8.4 us (5%)
    pallas_call x1, Pallas kernels, layer_call(): pl.pallas_call(functools.partial(layer_kernel, n), out_shape=(sds((ROWS,...  167 us

profile of v3, /device:TPU:0, one launch (start us, length us, event | category | flops | bytes accessed | tf_op | source)
XLA Modules:
  0.0 177.0 jit_solution(11162333921067289407)
XLA Ops:
  1.3 0.1 fusion.2
  1.4 0.6 pad_convert_fusion.cond_parts
  2.0 166.6 %layer.1 = (bf16[320,512]{1,0:T(8,128)(2,1)}, f32[320,512]{1,0:T(8,128)}, f32[128,512]{1,0:T(8,128)}, f32[128,3072]{1,0:T(8,128)}, f32[8,128,256]{2,1,0:T(8,128)}, /*index=5*/f32[2,128,1024]{2,1,0:T(8,128)}) custom-call(s32[1,20]{1,0:T(1,128)} %parents_ref.1, f32[4,8,128]{2,1,0:T(8,128)} %pad_convert_fusion.cond_parts, bf16[128,3072]{1,0:T(8,128)(2,1)} %w_mod.1, ...), custom_call_target="tpu_custom_call" | custom-call | tf_op jit(solution)/shard_map/layer/pallas_call | solution.py:1162
  168.6 0.0 copy-start.1
  168.6 1.8 %slice_bitcast_fusion.2 = (f32[128,256]{1,0:T(8,128)}, f32[128,256]{1,0:T(8,128)}) fusion(f32[8,128,256]{2,1,0:T(8,128)} %get-tuple-element.20), kind=kLoop, calls=%fused_computation.2 | loop fusion | bytes 524288 | tf_op jit(solution)/shard_map/squeeze | solution.py:1288
  170.4 0.0 copy-start.3
  170.4 2.1 %fusion.4 = (f32[3,128,256]{2,1,0:T(8,128)}, f32[3,128,256]{2,1,0:T(8,128)}) fusion(f32[8,128,256]{2,1,0:T(8,128)} %get-tuple-element.20), kind=kLoop, calls=%fused_computation.12 | loop fusion | bytes 1572864 | tf_op jit(solution)/shard_map/slice | solution.py:1287
  172.5 0.0 copy-start.2
  172.5 0.0 copy-done.1
  172.5 0.0 copy-start.4
  172.5 1.1 slice_bitcast_fusion
  173.6 0.0 copy-start
  173.6 0.0 copy-done.3
  173.6 0.7 copy.29
  174.3 0.0 copy-done.2
  174.3 0.8 copy.30
  175.1 0.0 copy-done.4
  175.1 0.7 copy.31
  175.8 0.0 copy-done
  175.8 1.1 copy.32
  (2 shorter events, 0.0 us)
Async XLA Ops:
  168.6 3.9 %copy-start.1 = (f32[2,128,1024]{2,1,0:T(8,128)S(1)}, f32[2,128,1024]{2,1,0:T(8,128)}, u32[]{:S(2)}) copy-start(f32[2,128,1024]{2,1,0:T(8,128)} %get-tuple-element.21) | copy-start | bytes 3145732
  170.4 3.2 %copy-start.3 = (bf16[320,512]{1,0:T(8,128)(2,1)S(1)}, bf16[320,512]{1,0:T(8,128)(2,1)}, u32[]{:S(2)}) copy-start(bf16[320,512]{1,0:T(8,128)(2,1)} %get-tuple-element.16) | copy-start | bytes 983044
  172.5 1.8 %copy-start.2 = (f32[320,512]{1,0:T(8,128)S(1)}, f32[320,512]{1,0:T(8,128)}, u32[]{:S(2)}) copy-start(f32[320,512]{1,0:T(8,128)} %get-tuple-element.17) | copy-start | bytes 1966084
  172.5 2.7 %copy-start.4 = (f32[128,512]{1,0:T(8,128)S(1)}, f32[128,512]{1,0:T(8,128)}, u32[]{:S(2)}) copy-start(f32[128,512]{1,0:T(8,128)} %get-tuple-element.18) | copy-start | bytes 786436
  173.6 2.3 %copy-start = (f32[128,3072]{1,0:T(8,128)S(1)}, f32[128,3072]{1,0:T(8,128)}, u32[]{:S(2)}) copy-start(f32[128,3072]{1,0:T(8,128)} %get-tuple-element.43) | copy-start | bytes 4718596

commit v4 on v3

--- a/solution.py
+++ b/solution.py
@@ -197,7 +197,6 @@
     wv_acc,
     gatt,
     gffn,
-    egrad,
     rc_att,
     rx_att,
     zr_att,
@@ -217,6 +216,7 @@
     ready,
 ):
     t0, t1 = st.at[:, 0:D], st.at[:, D : 2 * D]
+    egrad = enc
     fs = lax.axis_index("fsdp")
     cx = lax.axis_index("ctx")
     y = lax.axis_index("tp")
@@ -311,7 +311,9 @@
     s_x1 = [wire.slot() for _ in range(6)]
     s_c2 = [wire.slot() for _ in range(6)]
     s_c3 = [wire.slot() for _ in range(6)]
-    s_ty, s_tx, s_txy, s_tc0, s_tc1, s_tc2, s_tc3 = (wire.slot() for _ in range(7))
+    s_ty, s_tx, s_txy, s_tc0, s_tc1, s_tc2, s_tc3, s_ty2 = (
+        wire.slot() for _ in range(8)
+    )
     s_ex, s_ec0, s_ec1 = (wire.slot() for _ in range(3))
 
     peers(
@@ -319,9 +321,21 @@
             cond_parts.at[to], cond_all.at[fs], s_cond + k, {"fsdp": to}
         ).start()
     )
-    wire.push(lambda: chunk(ci), s_ty, to_y, None, lambda: tok_in.at[0])
+    left = x == 0
+
+    def tail_rows(i):
+        return tok.at[pl.ds(pl.multiple_of(i * ROWS + ROWS - 64, 64), 64), :]
+
+    wire.push(
+        lambda: chunk(ci), s_ty, to_y, jnp.logical_or(left, ci == 4), lambda: tok_in.at[0]
+    )
+    wire.push(
+        lambda: tail_rows(ci), s_ty2, to_y, ci == 6, lambda: tok_in.at[0, ROWS - 64 : ROWS, :]
+    )
     wire.push(lambda: chunk(ci), s_tx, to_x, x == 0, lambda: tok_in.at[0])
-    wire.push(lambda: chunk(ci), s_tc0, to_c, None, lambda: tok_in.at[0])
+    wire.push(
+        lambda: chunk(ci), s_tc0, to_c, jnp.logical_or(left, ci == 4), lambda: tok_in.at[0]
+    )
 
     def z_start(g):
         peers(
@@ -331,8 +345,6 @@
         )
 
     z_start(0)
-    wire.push(lambda: enc_part(cx), s_ex, to_x, None, lambda: enc_in.at[0])
-    wire.push(lambda: enc_part(cx), s_ec0, to_c, None, lambda: enc_in.at[0])
 
     def mask_trunk(rs):
         row = lax.broadcasted_iota(jnp.int32, (32, TRK), 0) + rs.start + ci * ROWS
@@ -388,19 +400,24 @@
             wire.push(slab, s_x1[g], to_x)
         wire.push(slab, s_c1[g], to_c)
 
-    def x_done(g):
-        for yy, s_in, s_out in ((y, s_x0[g], s_c2[g]), (1 - y, s_x1[g], s_c3[g])):
-            slab = lambda yy=yy: place(g, all_rows, yy, 1 - x, c)
-            wire.arrived(slab(), s_in, to_x)
-            wire.push(slab, s_out, to_c)
+    def x_done(g, part):
+        s_in, s_out = ((s_x0[g], s_c2[g]), (s_x1[g], s_c3[g]))[part]
+        slab = lambda: place(g, all_rows, 1 - y if part else y, 1 - x, c)
+        wire.arrived(slab(), s_in, to_x)
+        wire.push(slab, s_out, to_c)
+
+    def c_part(g, part):
+        yy, xx, at = (
+            (y, x, s_c0[g]),
+            (1 - y, x, s_c1[g]),
+            (y, 1 - x, s_c2[g]),
+            (1 - y, 1 - x, s_c3[g]),
+        )[part]
+        wire.arrived(place(g, all_rows, yy, xx, 1 - c), at, to_c)
 
     def c_done(g):
         wire.arrived(place(g, all_rows, y, x, 1 - c), s_c0[g], to_c)
         wire.arrived(place(g, all_rows, 1 - y, x, 1 - c), s_c1[g], to_c)
-        if groups[g][3]:
-            wire.arrived(place(g, all_rows, y, 1 - x, 1 - c), s_c2[g], to_c)
-            wire.arrived(place(g, all_rows, 1 - y, 1 - x, 1 - c), s_c3[g], to_c)
-
     local_copies[0].wait()
     local_copies[1].wait()
     ciy = 4 * x + 2 * c + 1 - y
@@ -409,19 +426,30 @@
     low, lowy, lowc, lowyc = 2 * c + y, 2 * c + 1 - y, 2 * (1 - c) + y, 2 * (1 - c) + 1 - y
     right = x == 1
     local_copies[8].wait()
-    wire.arrived(chunk(ciy), s_ty, to_y)
-    wire.push(lambda: chunk(ciy), s_txy, to_x, x == 0)
-    wire.push(lambda: chunk(ciy), s_tc1, to_c)
+    wire.arrived(chunk(ciy), s_ty, to_y, jnp.logical_or(left, ci == 5))
+    wire.push(lambda: chunk(ciy), s_txy, to_x, left)
+    wire.push(lambda: chunk(ciy), s_tc1, to_c, jnp.logical_or(left, ci == 5))
+    wire.arrived(tail_rows(ciy), s_ty2, to_y, ci == 7)
+
+    @pl.when(jnp.logical_and(right, y == 0))
+    def _():
+        tok[pl.ds(pl.multiple_of((ci + 1) * ROWS, 64), 64), :] = jnp.zeros((64, D), BF)
+
+    z_start(1)
+    z_start(4)
     wire.arrived(chunk(low), s_tx, to_x, right)
     wire.push(lambda: chunk(low), s_tc2, to_c, right)
     z_done(0)
-    for g in (1, 2, 3):
-        z_start(g)
-    wire.arrived(enc_part(2 * (1 - x) + c), s_ex, to_x)
-    wire.push(lambda: enc_part(2 * (1 - x) + c), s_ec1, to_c)
+    z_start(2)
     wire.arrived(chunk(lowy), s_txy, to_x, right)
     wire.push(lambda: chunk(lowy), s_tc3, to_c, right)
+    wire.push(lambda: enc_part(cx), s_ex, to_x, None, lambda: enc_in.at[0])
+    wire.push(lambda: enc_part(cx), s_ec0, to_c, None, lambda: enc_in.at[0])
     y_done(0)
+    z_done(1)
+    z_done(4)
+    z_start(5)
+    z_start(3)
 
     peers(lambda k, _, src: wire.arrived(part_in.at[src], s_part + k, {"fsdp": src}))
     mod[...] = jnp.sum(part_in[...], axis=0)
@@ -429,39 +457,43 @@
     sb, bb = mod[2:3, :], mod[3:4, :]
     sf, bf_ = mod[4:5, :], mod[5:6, :]
 
-    wire.arrived(chunk(cic), s_tc0, to_c)
-    wire.arrived(chunk(ciyc), s_tc1, to_c)
+    wire.arrived(chunk(cic), s_tc0, to_c, jnp.logical_or(left, ci == 6))
+    wire.arrived(chunk(ciyc), s_tc1, to_c, jnp.logical_or(left, ci == 7))
     wire.arrived(chunk(lowc), s_tc2, to_c, right)
     wire.arrived(chunk(lowyc), s_tc3, to_c, right)
-    wire.arrived(enc_part(2 * x + 1 - c), s_ec0, to_c)
-    wire.arrived(enc_part(2 * (1 - x) + 1 - c), s_ec1, to_c)
+
+    def enc_done(step):
+        if step == 0:
+            wire.arrived(enc_part(2 * (1 - x) + c), s_ex, to_x)
+            wire.push(lambda: enc_part(2 * (1 - x) + c), s_ec1, to_c)
+        else:
+            wire.arrived(enc_part(2 * x + 1 - c), s_ec0, to_c)
+            wire.arrived(enc_part(2 * (1 - x) + 1 - c), s_ec1, to_c)
+
     tok_tb = tok
     tok_loc = tok.at[pl.ds(pl.multiple_of(ci * ROWS - off, 64), LOC), :]
 
     def relay(step):
-        if step == 0:
-            for g in (1, 2, 3):
-                z_done(g)
-            z_start(4)
-            z_start(5)
         if step == 1:
-            z_done(4)
+            y_done(1)
+            y_done(4)
+            enc_done(0)
         if step == 2:
             z_done(5)
-            for g in (1, 2, 3):
-                y_done(g)
-        if step == 3:
-            y_done(4)
+            z_done(3)
         if step == 4:
-            for g in (1, 2, 3):
-                c_done(g)
+            c_done(1)
+        if step == 5:
+            y_done(3)
+            c_done(3)
+        if step == 6:
+            x_done(4, 0)
+            x_done(5, 0)
+        if step == 7:
+            y_done(2)
             y_done(5)
-            x_done(4)
-        if step == 5:
-            x_done(5)
-        if step == 6:
-            c_done(4)
-            c_done(5)
+            enc_done(1)
+            c_done(2)
 
     spec_g = qbuf
 
@@ -472,7 +504,8 @@
 
     to_xy = {"ctx": 2 * (1 - x) + c, "tp": 1 - y}
     s_rcg, s_rcg4, s_rcg5, s_halo = (wire.slot() for _ in range(4))
-    s_rxg = [wire.slot() for _ in range(3)]
+    s_rxy = [wire.slot() for _ in range(2)]
+    s_rxx = [wire.slot() for _ in range(2)]
     s_rce = [wire.slot(), wire.slot()]
     s_rxe = [wire.slot() for _ in range(3)]
     s_m1 = wire.slot(8)
@@ -488,11 +521,6 @@
 
         row_loop(total, step, body)
 
-    def ctx_peers(make):
-        @pl.loop(1, 4)
-        def _(k):
-            make(k, lax.rem(cx + k, 4), lax.rem(cx + 4 - k, 4))
-
     def strip(buf, at):
         return buf.at[:, at * 256 : (at + 1) * 256]
 
@@ -500,27 +528,29 @@
         def __init__(self, unit, core_box, box, landing, held, shape_rows):
             self.unit, self.core_box, self.box = unit, core_box, box
             self.landing, self.held = landing, held
-            self.s_core = [[wire.slot() for _ in range(4)] for _ in range(2)]
+            self.s_core = [wire.slot(4) for _ in range(2)]
             self.s_one = [[wire.slot() for _ in range(2)] for _ in range(2)]
             self.s_two = [wire.slot() for _ in range(2)]
             self.s_z = [wire.slot(n) for _ in range(2)]
             self.s_g = wire.slot(4)
 
+        def core_copy(self, m, t):
+            return wire.copy(
+                self.unit(m, t // 2, lax.rem(t, 2), 1 - c),
+                self.core_box(m, t),
+                self.s_core[m] + t,
+                to_c,
+            )
+
         def core_send(self):
             for m in range(2):
                 for t in range(4):
-                    wire.push(
-                        lambda m=m, t=t: self.core_box(m, t),
-                        self.s_core[m][t],
-                        to_c,
-                        None,
-                        lambda m=m, t=t: self.unit(m, t // 2, t % 2, 1 - c),
-                    )
+                    self.core_copy(m, t).start()
 
         def first_send(self):
             for m in range(2):
                 for t in range(4):
-                    wire.arrived(self.core_box(m, t), self.s_core[m][t], to_c)
+                    wire.arrived(self.core_box(m, t), self.s_core[m] + t, to_c)
                     mine = self.unit(m, t // 2, t % 2, c)
                     add_rows(mine, (mine, self.core_box(m, t)), D)
             for j in range(2):
@@ -580,8 +610,9 @@
                 peers(lambda k, to, _, m=m: self.z_copy(m, k, to).start())
                 self.landing[fs, m] = self.unit(m, y, x, c)[my_rows, :]
 
-        def g_copy(self, k, to):
-            return wire.copy(self.held.at[cx], self.held.at[cx], self.s_g + k, {"ctx": to})
+        def g_copy(self, i):
+            target, at = ((to_x, cx), (to_c, cx), (to_c, 2 * (1 - x) + c))[i]
+            return wire.copy(self.held.at[at], self.held.at[at], self.s_g + i, target)
 
         def copy_send(self):
             for m in range(2):
@@ -591,21 +622,28 @@
                     )
                 )
             self.held[cx] = jnp.sum(self.landing[...].astype(F), axis=0).astype(BF)
-            ctx_peers(lambda k, to, _: self.g_copy(k, to).start())
+            self.g_copy(0).start()
+            self.g_copy(1).start()
+
+        def relay_copy(self):
+            wire.arrived(self.held.at[2 * (1 - x) + c], self.s_g, to_x)
+            self.g_copy(2).start()
 
         def collect(self):
-            ctx_peers(
-                lambda k, _, src: wire.arrived(self.held.at[src], self.s_g + k, {"ctx": src})
-            )
+            wire.arrived(self.held.at[2 * x + 1 - c], self.s_g + 1, to_c)
+            wire.arrived(self.held.at[2 * (1 - x) + 1 - c], self.s_g + 2, to_c)
 
         def drain(self):
             for m in range(2):
+                for t in range(4):
+                    self.core_copy(m, t).wait_send()
                 peers(lambda k, to, _, m=m: self.z_copy(m, k, to).wait_send())
-            ctx_peers(lambda k, to, _: self.g_copy(k, to).wait_send())
+            for i in range(3):
+                self.g_copy(i).wait_send()
 
     ffn = Family(
         lambda m, yy, xx, cc: gffn.at[m, :, ffn_cols(yy, xx, cc)],
-        lambda m, t: strip(wup, m * 4 + t),
+        lambda m, t: rc_att.at[m * 4 + t],
         lambda i: strip(wdn, i),
         zr_ffn,
         rg_ffn,
@@ -615,7 +653,9 @@
     def attention_family(a):
         return Family(
             lambda m, yy, xx, cc: gatt.at[4 * a + 2 * xx + m, :, att_cols(yy, cc)],
-            lambda m, t: rc_att.at[a, m, t],
+            lambda m, t: rc_att.at[
+                4 * a + 2 * m + t // 2, :, pl.ds(pl.multiple_of(lax.rem(t, 2) * 128, 128), 128)
+            ],
             lambda i: rx_att.at[a, i],
             zr_att.at[a],
             rg_att.at[a],
@@ -624,12 +664,15 @@
 
     att = (attention_family(0), attention_family(1))
 
-    def ffn_core_send():
+    def ffn_free():
         wire.drain()
-        for target in (to_c, to_y, to_x):
-            pl.semaphore_signal(ready, inc=1, device_id=target, device_id_type=MESH)
-        pl.semaphore_wait(ready, 3)
-        ffn.core_send()
+        for target in (to_y, to_x):
+            pl.semaphore_signal(ready.at[0], inc=1, device_id=target, device_id_type=MESH)
+
+    def ffn_chip_send():
+        pl.semaphore_wait(ready.at[0], 2)
+        ffn.first_send()
+        pl.semaphore_signal(ready.at[1], inc=1, device_id=to_c, device_id_type=MESH)
 
     def ffn_finish():
         ffn.collect()
@@ -683,10 +726,24 @@
         )
         wire.push(lambda: halo, s_halo, to_y, y == 1, lambda: spec_g.at[0:64, :])
 
+    def part_rows(yy, p):
+        return tok.at[pl.ds(pl.multiple_of((2 * c + yy) * ROWS + p * 160, 32), 160), :]
+
+    def core_rows(yy, p):
+        return rc_g.at[pl.ds(pl.multiple_of(yy * ROWS + p * 160, 32), 160), :]
+
     def shared_y_send():
         wire.arrived(rc_g.at[0:640], s_rcg, to_c)
-        mine = tok.at[pl.ds(pl.multiple_of(640 * c, 640), 640), :]
-        add_rows(mine, (mine, rc_g.at[0:640]), 640)
+        for p in range(2):
+            mine = part_rows(1 - y, p)
+            add_rows(mine, (mine, core_rows(1 - y, p)), 160, 32)
+            wire.push(
+                lambda p=p: rx_g.at[0, p * 160 : p * 160 + 160],
+                s_rxy[p],
+                to_y,
+                None,
+                lambda p=p: part_rows(1 - y, p),
+            )
         last = jnp.logical_and(x == 1, c == 0)
 
         @pl.when(last)
@@ -695,10 +752,6 @@
             four = tok.at[1280:1536, :]
             add_rows(four, (four, rc_g.at[640:896]), 256)
 
-        def rows_of(yy):
-            return lambda: chunk(2 * c + yy)
-
-        wire.push(lambda: rx_g.at[0], s_rxg[0], to_y, None, rows_of(1 - y))
         wire.push(
             lambda: rx_g.at[1, 0:256],
             s_rcg5,
@@ -706,15 +759,26 @@
             jnp.logical_and(last, y == 1),
             lambda: tok.at[1280:1536, :],
         )
+        for p in range(2):
+            mine = part_rows(y, p)
+            add_rows(mine, (mine, core_rows(y, p)), 160, 32)
 
     def shared_x_send():
-        wire.arrived(rx_g.at[0], s_rxg[0], to_y)
-        mine = chunk(2 * c + y)
-        add_rows(mine, (mine, rx_g.at[0]), ROWS)
-        wire.push(lambda: rx_g.at[1], s_rxg[1], to_x, x == 1, lambda: chunk(2 * c + y))
+        for p in range(2):
+            wire.arrived(rx_g.at[0, p * 160 : p * 160 + 160], s_rxy[p], to_y)
+            mine = part_rows(y, p)
+            add_rows(mine, (mine, rx_g.at[0, p * 160 : p * 160 + 160]), 160, 32)
+            wire.push(
+                lambda p=p: rx_g.at[1, p * 160 : p * 160 + 160],
+                s_rxx[p],
+                to_x,
+                x == 1,
+                lambda p=p: part_rows(y, p),
+            )
 
     def shared_arrived():
-        wire.arrived(rx_g.at[1], s_rxg[1], to_x, x == 0)
+        for p in range(2):
+            wire.arrived(rx_g.at[1, p * 160 : p * 160 + 160], s_rxx[p], to_x, x == 0)
         wire.arrived(rx_g.at[1, 0:256], s_rcg5, to_y, ci == 4)
 
     def tree_peers(make):
@@ -768,10 +832,11 @@
 
     def leave(step):
         if step == 0:
-            ffn_core_send()
+            ffn_free()
         if step == 1:
-            ffn.first_send()
+            ffn_chip_send()
         if step == 2:
+            pl.semaphore_wait(ready.at[1], 1)
             att[1].core_send()
             enc_core_send()
         if step == 3:
@@ -784,26 +849,28 @@
             ffn.tree_send()
         if step == 6:
             shared_core_send()
+            att[1].tree_send()
         if step == 7:
-            att[0].core_send()
             shared_y_send()
+            att[0].first_send()
+            ffn.copy_send()
+            enc_finish()
+            shared_x_send()
         if step == 8:
-            att[0].first_send()
-            att[1].tree_send()
-            ffn.copy_send()
-            shared_x_send()
-            enc_finish()
             att[0].second_send()
             att[1].copy_send()
-            ffn_finish()
+            ffn.relay_copy()
             shared_arrived()
         if step == 9:
             mod_tree_send()
             att[0].tree_send()
-            att_finish(1)
+            att[1].relay_copy()
+            ffn_finish()
             mod_all_send()
             att[0].copy_send()
+            att_finish(1)
             mod_finish()
+            att[0].relay_copy()
             att_finish(0)
 
     def hidden(x):
@@ -837,6 +904,7 @@
         kbuf[rs, :] = nn(hid[rs, :], watt[1]).astype(BF)
         vbuf[rs, :] = nn(hid[rs, :], watt[2]).astype(BF)
 
+    z_done(2)
     c_done(0)
     row_loop(KV, 256, project)
     qbuf[...] = (nn(hloc[...], watt[0]) * 0.125).astype(BF)
@@ -854,7 +922,7 @@
 
     @pl.loop(0, 4)
     def _(hp):
-        for step in range(4):
+        for step in (1, 2):
 
             @pl.when(hp == step)
             def _(step=step):
@@ -898,6 +966,7 @@
 
     row_loop(ROWS, 32, after_self, 0)
 
+    relay(7)
     kenc[...] = nn(enc[...], watt[5]).astype(BF)
     venc[...] = nn(enc[...], watt[6]).astype(BF)
     qb[...] = (nn(hid_b[...], watt[4]) * 0.125).astype(BF)
@@ -933,9 +1002,25 @@
     acc0[...] = jnp.zeros_like(acc0)
     acc1[...] = jnp.zeros_like(acc1)
 
+    def flip(v, by):
+        return v + by - 2 * v * by
+
     @pl.loop(0, 4)
     def _(ft):
-        cols = pl.ds(pl.multiple_of(ft * 512, 512), 512)
+        @pl.when(ft == 2)
+        def _():
+            x_done(4, 1)
+            x_done(5, 1)
+
+        for part in range(4):
+
+            @pl.when(ft == part)
+            def _(part=part):
+                c_part(4, part)
+                c_part(5, part)
+
+        tile = flip(y, lax.rem(ft, 2)) * 2 + flip(x, ft // 2)
+        cols = pl.ds(pl.multiple_of(tile * 512, 512), 512)
         t0[...] = nn(hid_c[...], wup[:, cols])
         t1[...] = nn(cot[...], wdn[:, cols])
 
@@ -951,6 +1036,8 @@
         acc1[...] += nt(b1[...], wup[:, cols])
         gffn[1, :, cols] = tn(cot[...], b0[...]).astype(BF)
         gffn[0, :, cols] = tn(hid_c[...], b1[...]).astype(BF)
+        for m in range(2):
+            ffn.core_copy(m, tile).start()
 
     def back_norm(at, scale, grad_src, stream_src, base_src, want_out):
         sums = [jnp.zeros((1, D), F), jnp.zeros((1, D), F)]
@@ -971,6 +1058,7 @@
 
     gatt[7] = tn(gbf[...], mixb[...]).astype(BF)
     mgr[...] = (nn(gbf[...], watt[7]) * linv_b[...]).astype(BF)
+    leave(1)
 
     @pl.loop(0, 4)
     def _(hp):
@@ -990,7 +1078,6 @@
         kenc[:, lanes] = (dks[0] + dks[1]).astype(BF)
         venc[:, lanes] = (dvs[0] + dvs[1]).astype(BF)
 
-    leave(1)
     gatt[4] = tn(hid_b[...], dq[...]).astype(BF)
     gatt[5] = tn(enc[...], kenc[...]).astype(BF)
     gatt[6] = tn(enc[...], venc[...]).astype(BF)
@@ -1001,6 +1088,7 @@
 
     gatt[3] = tn(gbf[...], mixa[...]).astype(BF)
     mgr[...] = (nn(gbf[...], watt[3]) * linv_a[...]).astype(BF)
+    leave(3)
 
     @pl.when(odd == 0)
     def _():
@@ -1015,7 +1103,10 @@
         spec_o[:, 0:64, :] = jnp.zeros((2, 64, 128), F)
 
     @pl.loop(0, 4)
-    def _(hp):
+    def _(turn):
+        side = jnp.where(turn < 2, 1 - c, c)
+        band = jnp.where(turn < 2, turn, jnp.where(turn == 2, 1 - y, y))
+        hp = band * 2 + side
         lanes = pl.ds(pl.multiple_of(hp * 128, 128), 128)
         prod = mgr[:, lanes].astype(F) * mixa[:, lanes].astype(F)
         dqs, dks, dvs = [], [], []
@@ -1052,53 +1143,66 @@
             kbuf[k_rows, lanes] = (dks_s[lb][0] + dks_s[lb][1]).astype(BF)
             vbuf[k_rows, lanes] = (dvs_s[lb][0] + dvs_s[lb][1]).astype(BF)
 
-        for step in range(3):
-
-            @pl.when(hp == step)
-            def _(step=step):
-                leave(3 + step)
-
-    wk_acc[...] = jnp.zeros_like(wk_acc)
-    wv_acc[...] = jnp.zeros_like(wv_acc)
-
-    def key_side(rs):
-        wk_acc[...] += tn(hid[rs, :], kbuf[rs, :])
-        wv_acc[...] += tn(hid[rs, :], vbuf[rs, :])
-        hid[rs, :] = (nt(kbuf[rs, :], watt[1]) + nt(vbuf[rs, :], watt[2])).astype(BF)
-
-    row_loop(KV, 256, key_side)
-
-    def put_trunk(rs):
-        tok[rs, :] = hid[rs, :]
-
-    row_loop(TRK, 64, put_trunk)
+        total = None
+        for at in range(0, KV, KV // 2):
+            rs = slice(at, at + KV // 2)
+            both = jnp.concatenate([kbuf[rs, lanes], vbuf[rs, lanes]], axis=1)
+            part = tn(both, hid[rs, :])
+            total = part if total is None else total + part
+        kv_grad = jnp.transpose(total)
+        gatt[1, :, lanes] = kv_grad[:, 0:128].astype(BF)
+        gatt[2, :, lanes] = kv_grad[:, 128:256].astype(BF)
+        gatt[0, :, lanes] = tn(hloc[own, :], dq[:, lanes]).astype(BF)
+
+        @pl.when(turn < 2)
+        def _():
+            for m in range(2):
+                for xx in range(2):
+                    att[0].core_copy(m, band * 2 + xx).start()
+
+        @pl.when(turn == 0)
+        def _():
+            leave(4)
+
+        @pl.when(turn == 2)
+        def _():
+            leave(5)
+
+    def key_grad(rs):
+        return (nt(kbuf[rs, :], watt[1]) + nt(vbuf[rs, :], watt[2])).astype(BF)
+
+    for lb in range(3):
+        pe[lb, 0:256, :] = key_grad(slice(TRK + lb * 256, TRK + (lb + 1) * 256))
+
+    def trunk_grad(rs):
+        tok[rs, :] = key_grad(rs)
+
+    row_loop(TRK, 256, trunk_grad)
+
     for b in range(BRANCHES):
         hits = [is_parent(lb, b) for lb in range(3)]
         for piece in range(4):
             total = jnp.zeros((32, D), F)
             for lb in range(3):
-                at = TRK + lb * 256 + piece * 32
-                total += jnp.where(hits[lb], hid[at : at + 32, :].astype(F), 0.0)
+                at = piece * 32
+                total += jnp.where(hits[lb], pe[lb, at : at + 32, :].astype(F), 0.0)
             at = TRK + b * BLK + piece * 32
             tok[at : at + 32, :] = total.astype(BF)
     for lb in range(3):
-        spec_g[lb * BLK : (lb + 1) * BLK, :] = hid[TRK + lb * 256 + BLK : TRK + (lb + 1) * 256, :]
+        spec_g[lb * BLK : (lb + 1) * BLK, :] = pe[lb, BLK : 2 * BLK, :]
 
     leave(6)
-    gatt[0] = tn(hloc[own, :], dq[...]).astype(BF)
-    gatt[1] = wk_acc[...].astype(BF)
-    gatt[2] = wv_acc[...].astype(BF)
-    leave(7)
     acc1[...] = nt(dq[...], watt[0])
-    leave(8)
-
-    wire.arrived(halo, s_halo, to_y, y == 0)
 
     def own_sum(rs):
         extra = spec_g[pl.ds(pl.multiple_of(rs.start + off, 32), 32), :].astype(F)
         acc1[rs, :] += extra
 
     row_loop(ROWS, 32, own_sum, 5)
+    leave(7)
+    leave(8)
+
+    wire.arrived(halo, s_halo, to_y, y == 0)
 
     @pl.when(y == 0)
     def _():
@@ -1213,11 +1317,10 @@
             pltpu.VMEM((ROWS, D), BF),
             pltpu.VMEM((ROWS, D), BF),
             pltpu.VMEM((D, D), F),
-            pltpu.VMEM((D, D), F),
+            pltpu.VMEM((ROWS, D), F),
             pltpu.VMEM((8, D, D), BF),
             pltpu.VMEM((2, D, FF), BF),
-            pltpu.VMEM((ENC, D), BF),
-            pltpu.VMEM((2, 2, 4, D, 128), BF),
+            pltpu.VMEM((8, D, 256), BF),
             pltpu.VMEM((2, 6, D, 128), BF),
             pltpu.VMEM((2, n, 2, rows, 128), BF),
             pltpu.VMEM((2, 4, 2, rows, 128), BF),
@@ -1233,7 +1336,7 @@
             pltpu.SemaphoreType.DMA((16 * n + 160,)),
             pltpu.SemaphoreType.DMA((16 * n + 160,)),
             pltpu.SemaphoreType.DMA((9,)),
-            pltpu.SemaphoreType.REGULAR,
+            pltpu.SemaphoreType.REGULAR((2,)),
         ],
         compiler_params=pltpu.CompilerParams(
             vmem_limit_bytes=VMEM_LIMIT, collective_id=0, has_side_effects=True

time: 177 us -> 161 us (0.910)
  Pallas kernels: 167 us -> 150 us
    pallas_call x1, Pallas kernels: 167 us -> 150 us  [layer_call(): pl.pallas_call(functools.partial(layer_kernel, n), out_shape=(sds((ROWS,...]
where the time goes in v4:
time: 161 us; the launch traced here: 160 us
  Pallas kernels  150 us (93%)
  local copies, waits for them, and re-layouts  8.4 us (5%)
    pallas_call x1, Pallas kernels, layer_call(): pl.pallas_call(functools.partial(layer_kernel, n), out_shape=(sds((ROWS,...  150 us
    unnamed x14, local copies, waits for them, and re-layouts  3.42 us

profile of v4, /device:TPU:0, one launch (start us, length us, event | category | flops | bytes accessed | tf_op | source)
XLA Modules:
  0.0 160.5 jit_solution(15138787757118624342)
XLA Ops:
  1.3 0.1 fusion.2
  1.4 0.6 pad_convert_fusion.cond_parts
  2.0 150.0 %layer.1 = (bf16[320,512]{1,0:T(8,128)(2,1)}, f32[320,512]{1,0:T(8,128)}, f32[128,512]{1,0:T(8,128)}, f32[128,3072]{1,0:T(8,128)}, f32[8,128,256]{2,1,0:T(8,128)}, /*index=5*/f32[2,128,1024]{2,1,0:T(8,128)}) custom-call(s32[1,20]{1,0:T(1,128)} %parents_ref.1, f32[4,8,128]{2,1,0:T(8,128)} %pad_convert_fusion.cond_parts, bf16[128,3072]{1,0:T(8,128)(2,1)} %w_mod.1, ...), custom_call_target="tpu_custom_call" | custom-call | tf_op jit(solution)/shard_map/layer/pallas_call | solution.py:1266
  152.1 0.0 copy-start.1
  152.1 1.8 %slice_bitcast_fusion.2 = (f32[128,256]{1,0:T(8,128)}, f32[128,256]{1,0:T(8,128)}) fusion(f32[8,128,256]{2,1,0:T(8,128)} %get-tuple-element.20), kind=kLoop, calls=%fused_computation.2 | loop fusion | bytes 524288 | tf_op jit(solution)/shard_map/squeeze | solution.py:1391
  153.8 0.0 copy-start.3
  153.8 2.1 %fusion.4 = (f32[3,128,256]{2,1,0:T(8,128)}, f32[3,128,256]{2,1,0:T(8,128)}) fusion(f32[8,128,256]{2,1,0:T(8,128)} %get-tuple-element.20), kind=kLoop, calls=%fused_computation.12 | loop fusion | bytes 1572864 | tf_op jit(solution)/shard_map/slice | solution.py:1390
  156.0 0.0 copy-start.2
  156.0 0.0 copy-done.1
  156.0 0.0 copy-start.4
  156.0 1.1 slice_bitcast_fusion
  157.1 0.0 copy-start
  157.1 0.0 copy-done.3
  157.1 0.7 copy.29
  157.8 0.0 copy-done.2
  157.8 0.8 copy.30
  158.6 0.0 copy-done.4
  158.6 0.7 copy.31
  159.3 0.0 copy-done
  159.3 1.1 copy.32
  (2 shorter events, 0.0 us)
Async XLA Ops:
  152.1 3.9 %copy-start.1 = (f32[2,128,1024]{2,1,0:T(8,128)S(1)}, f32[2,128,1024]{2,1,0:T(8,128)}, u32[]{:S(2)}) copy-start(f32[2,128,1024]{2,1,0:T(8,128)} %get-tuple-element.21) | copy-start | bytes 3145732
  153.8 3.2 %copy-start.3 = (bf16[320,512]{1,0:T(8,128)(2,1)S(1)}, bf16[320,512]{1,0:T(8,128)(2,1)}, u32[]{:S(2)}) copy-start(bf16[320,512]{1,0:T(8,128)(2,1)} %get-tuple-element.16) | copy-start | bytes 983044
  156.0 1.8 %copy-start.2 = (f32[320,512]{1,0:T(8,128)S(1)}, f32[320,512]{1,0:T(8,128)}, u32[]{:S(2)}) copy-start(f32[320,512]{1,0:T(8,128)} %get-tuple-element.17) | copy-start | bytes 1966084
  156.0 2.7 %copy-start.4 = (f32[128,512]{1,0:T(8,128)S(1)}, f32[128,512]{1,0:T(8,128)}, u32[]{:S(2)}) copy-start(f32[128,512]{1,0:T(8,128)} %get-tuple-element.18) | copy-start | bytes 786436
  157.1 2.3 %copy-start = (f32[128,3072]{1,0:T(8,128)S(1)}, f32[128,3072]{1,0:T(8,128)}, u32[]{:S(2)}) copy-start(f32[128,3072]{1,0:T(8,128)} %get-tuple-element.43) | copy-start | bytes 4718596

commit v5 on v4

--- a/solution.py
+++ b/solution.py
@@ -151,6 +151,7 @@
     in_grad,
     enc_out,
     mod_out,
+    cond_out,
     att_out,
     ffn_out,
     watt,
@@ -674,17 +675,24 @@
         ffn.first_send()
         pl.semaphore_signal(ready.at[1], inc=1, device_id=to_c, device_id_type=MESH)
 
+    results = (
+        (rg_ffn, ffn_out),
+        (rg_att.at[0], att_out.at[0]),
+        (rg_att.at[1], att_out.at[1]),
+        (mod2, mod_out),
+        (cond_all, cond_out),
+    )
+
+    def result(i):
+        return pltpu.make_async_copy(results[i][0], results[i][1], local.at[i])
+
     def ffn_finish():
         ffn.collect()
-        for q in range(4):
-            ffn_out[:, :, q * 256 : (q + 1) * 256] = rg_ffn[q].astype(F)
+        result(0).start()
 
     def att_finish(a):
         att[a].collect()
-        for q in range(4):
-            for m in range(2):
-                at = 4 * a + 2 * (q // 2) + m
-                att_out[at, :, (q % 2) * 128 : (q % 2) * 128 + 128] = rg_att[a, q, m].astype(F)
+        result(1 + a).start()
 
     def enc_core_send():
         for xx in range(2):
@@ -806,29 +814,8 @@
 
     def mod_finish():
         peers(lambda k, _, src: wire.arrived(mod2.at[src], s_m2 + k, {"fsdp": src}))
-        cond = cond_all[:, 0, 0:rows]
-        for v in range(6):
-            held = (wk_acc, wv_acc)[v // 4]
-            at = (v % 4) * rows
-            held[at : at + rows, :] = lax.dot_general(
-                cond,
-                mod2[:, v, :],
-                (((0,), (0,)), ((), ())),
-                precision=lax.Precision.HIGHEST,
-                preferred_element_type=F,
-            )
-        copies = [
-            pltpu.make_async_copy(
-                (wk_acc, wv_acc)[v // 4].at[(v % 4) * rows : (v % 4 + 1) * rows, :],
-                mod_out.at[:, v * D : (v + 1) * D],
-                local.at[v],
-            )
-            for v in range(6)
-        ]
-        for copy in copies:
-            copy.start()
-        for copy in copies:
-            copy.wait()
+        result(3).start()
+        result(4).start()
 
     def leave(step):
         if step == 0:
@@ -1235,6 +1222,8 @@
     mgrad[1:2, :] = sums[1]
     leave(9)
 
+    for i in range(5):
+        result(i).wait()
     wire.drain()
     for family in (ffn, *att):
         family.drain()
@@ -1269,12 +1258,13 @@
             sds((ROWS, D), BF),
             sds((ROWS, D), F),
             sds((ENC // 4, D), F),
-            sds((rows, 6 * D), F),
-            sds((8, rows, 256), F),
-            sds((2, rows, 1024), F),
+            sds((n, 8, D), F),
+            sds(cond_parts.shape, F),
+            sds((2, 4, 2, rows, 128), BF),
+            sds((4, 2, rows, 256), BF),
         ),
         in_specs=[pl.BlockSpec(memory_space=pltpu.SMEM), vm, vm, hbm, hbm, vm] + [hbm] * 6,
-        out_specs=(vm, vm, vm, hbm, vm, vm),
+        out_specs=(vm, vm, vm, hbm, hbm, hbm, hbm),
         scratch_shapes=[
             pltpu.VMEM((8, D, D), BF),
             pltpu.VMEM((D, FF), BF),
@@ -1345,6 +1335,57 @@
     )(parents, cond_parts, w_mod, tokens, enc, cot, *weights)
 
 
+def finish_kernel(
+    n, rows, out, grad, enc, mod, cond, att, ffn, o_out, o_grad, o_enc, o_mod, qkv, so, cqkv, co, up, dn
+):
+    o_out[...] = out[...]
+    o_grad[...] = grad[...]
+    o_enc[...] = enc[...]
+    for v in range(6):
+        o_mod[:, v * D : (v + 1) * D] = lax.dot_general(
+            cond[:, 0, 0:rows],
+            mod[:, v, :],
+            (((0,), (0,)), ((), ())),
+            precision=lax.Precision.HIGHEST,
+            preferred_element_type=F,
+        )
+    for q in range(4):
+        up[:, q * 256 : (q + 1) * 256] = ffn[q, 0].astype(F)
+        dn[:, q * 256 : (q + 1) * 256] = ffn[q, 1].astype(F)
+        cols = slice((q % 2) * 128, (q % 2) * 128 + 128)
+        for a, (stack, single) in enumerate(((qkv, so), (cqkv, co))):
+            for m in range(2):
+                value = att[a, q, m].astype(F)
+                at = 2 * (q // 2) + m
+                if at < 3:
+                    stack[at, :, cols] = value
+                else:
+                    single[:, cols] = value
+
+
+def finish_call(n, rows, *parts):
+    vm = pl.BlockSpec(memory_space=pltpu.VMEM)
+    sds = jax.ShapeDtypeStruct
+    return pl.pallas_call(
+        functools.partial(finish_kernel, n, rows),
+        out_shape=(
+            sds((ROWS, D), BF),
+            sds((ROWS, D), F),
+            sds((ENC // 4, D), F),
+            sds((rows, 6 * D), F),
+            sds((3, rows, 256), F),
+            sds((rows, 256), F),
+            sds((3, rows, 256), F),
+            sds((rows, 256), F),
+            sds((rows, 1024), F),
+            sds((rows, 1024), F),
+        ),
+        in_specs=[vm] * 7,
+        out_specs=(vm,) * 10,
+        name="finish",
+    )(*parts)
+
+
 def timestep_code(timesteps, width):
     half = width // 2
     frequency = jnp.exp(-math.log(10000.0) * jnp.arange(half, dtype=F) / half)
@@ -1370,7 +1411,7 @@
     condition = jax.nn.silu(timestep_code(timesteps, D)).astype(BF)
     n = lax.axis_size("fsdp")
     padded_cond = jnp.pad(condition.astype(F).reshape(n, 1, rows), ((0, 0), (0, 7), (0, max(128 - rows, 0))))
-    out, in_grad, enc_grad, grad_mod, att, ffn = layer_call(
+    parts = layer_call(
         n,
         parents,
         padded_cond,
@@ -1380,18 +1421,8 @@
         cotangent[0],
         (w_self_qkv, w_self_out, w_cross_qkv, w_cross_out, w_up, w_down),
     )
-    return (
-        out[None],
-        in_grad[None],
-        enc_grad[None],
-        grad_mod,
-        att[0:3],
-        att[3],
-        att[4:7],
-        att[7],
-        ffn[0],
-        ffn[1],
-    )
+    out, in_grad, enc_grad, grad_mod, *weights = finish_call(n, rows, *parts)
+    return (out[None], in_grad[None], enc_grad[None], grad_mod, *weights)
 
 
 def solution(mesh):

time: 161 us -> 156 us (0.969)
  local copies, waits for them, and re-layouts: 8.4 us -> 0.01 us
  Pallas kernels: 150 us -> 153 us
    pallas_call x0 -> x1, Pallas kernels: none -> 5.17 us  [finish_call(): pl.pallas_call(functools.partial(finish_kernel, n, rows), out_shape=(sds(...]
    unnamed x14 -> x0, local copies, waits for them, and re-layouts: 3.42 us -> none
    squeeze x2 -> x0, local copies, waits for them, and re-layouts: 2.85 us -> none  [the longest x1 1.77 us: per_device(): att[7]]
    pallas_call x1, Pallas kernels: 150 us -> 148 us  [layer_call(): pl.pallas_call(functools.partial(layer_kernel, n), out_shape=(sds((ROWS,...]
    slice x1 -> x0, local copies, waits for them, and re-layouts: 2.12 us -> none  [per_device(): att[4:7]]
where the time goes in v5:
time: 156 us; the launch traced here: 155 us
  Pallas kernels  153 us (98%)
    pallas_call x1, Pallas kernels, layer_call(): pl.pallas_call(functools.partial(layer_kernel, n), out_shape=(sds((ROWS,...  148 us
    pallas_call x1, Pallas kernels, finish_call(): pl.pallas_call(functools.partial(finish_kernel, n, rows), out_shape=(sds(...  5.17 us

profile of v5, /device:TPU:0, one launch (start us, length us, event | category | flops | bytes accessed | tf_op | source)
XLA Modules:
  0.0 154.8 jit_solution(2505503509164913618)
XLA Ops:
  1.3 0.1 fusion.2
  1.4 0.6 pad_convert_fusion.cond_parts
  2.0 147.6 %layer.1 = (bf16[320,512]{1,0:T(8,128)(2,1)}, f32[320,512]{1,0:T(8,128)}, f32[128,512]{1,0:T(8,128)}, f32[4,8,512]{2,1,0:T(8,128)}, f32[4,8,128]{2,1,0:T(8,128)}...) custom-call(s32[1,20]{1,0:T(1,128)} %parents_ref.1, f32[4,8,128]{2,1,0:T(8,128)} %pad_convert_fusion.cond_parts, ...), custom_call_target="tpu_custom_call" | custom-call | tf_op jit(solution)/shard_map/layer/pallas_call | solution.py:1255
  149.6 5.2 %finish.1 = (bf16[320,512]{1,0:T(8,128)(2,1)}, f32[320,512]{1,0:T(8,128)}, f32[128,512]{1,0:T(8,128)}, f32[128,3072]{1,0:T(8,128)}, f32[3,128,256]{2,1,0:T(8,128...) custom-call(bf16[320,512]{1,0:T(8,128)(2,1)} %get-tuple-element.27.o, ...), custom_call_target="tpu_custom_call" | custom-call | tf_op jit(solution)/shard_map/finish/pallas_call | solution.py:1369
  (2 shorter events, 0.0 us)

commit v6 on v5

--- a/solution.py
+++ b/solution.py
@@ -202,6 +202,8 @@
     rx_att,
     zr_att,
     rg_att,
+    zl_att,
+    zs_att,
     zr_ffn,
     rg_ffn,
     rc_g,
@@ -485,6 +487,7 @@
         if step == 4:
             c_done(1)
         if step == 5:
+            y_done(5)
             y_done(3)
             c_done(3)
         if step == 6:
@@ -492,7 +495,6 @@
             x_done(5, 0)
         if step == 7:
             y_done(2)
-            y_done(5)
             enc_done(1)
             c_done(2)
 
@@ -528,7 +530,7 @@
     class Family:
         def __init__(self, unit, core_box, box, landing, held, shape_rows):
             self.unit, self.core_box, self.box = unit, core_box, box
-            self.landing, self.held = landing, held
+            self.landing, self.held, self.tall = landing, held, shape_rows
             self.s_core = [wire.slot(4) for _ in range(2)]
             self.s_one = [[wire.slot() for _ in range(2)] for _ in range(2)]
             self.s_two = [wire.slot() for _ in range(2)]
@@ -554,44 +556,50 @@
                     wire.arrived(self.core_box(m, t), self.s_core[m] + t, to_c)
                     mine = self.unit(m, t // 2, t % 2, c)
                     add_rows(mine, (mine, self.core_box(m, t)), D)
+            self.one_send()
+
+        def piece(self, m, yy, xx):
+            return self.unit(m, yy, xx, c)
+
+        def one_send(self):
             for j in range(2):
                 wire.push(
                     lambda j=j: self.box(j),
                     self.s_one[0][j],
                     to_x,
                     None,
-                    lambda j=j: self.unit(0, j, 1 - x, c),
+                    lambda j=j: self.piece(0, j, 1 - x),
                 )
                 wire.push(
                     lambda j=j: self.box(2 + j),
                     self.s_one[1][j],
                     to_y,
                     None,
-                    lambda j=j: self.unit(1, 1 - y, j, c),
+                    lambda j=j: self.piece(1, 1 - y, j),
                 )
 
         def second_send(self):
             for j in range(2):
                 wire.arrived(self.box(j), self.s_one[0][j], to_x)
-                mine = self.unit(0, j, x, c)
-                add_rows(mine, (mine, self.box(j)), D)
+                mine = self.piece(0, j, x)
+                add_rows(mine, (mine, self.box(j)), self.tall, min(64, self.tall))
             wire.push(
                 lambda: self.box(4),
                 self.s_two[0],
                 to_y,
                 None,
-                lambda: self.unit(0, 1 - y, x, c),
+                lambda: self.piece(0, 1 - y, x),
             )
             for j in range(2):
                 wire.arrived(self.box(2 + j), self.s_one[1][j], to_y)
-                mine = self.unit(1, y, j, c)
-                add_rows(mine, (mine, self.box(2 + j)), D)
+                mine = self.piece(1, y, j)
+                add_rows(mine, (mine, self.box(2 + j)), self.tall, min(64, self.tall))
             wire.push(
                 lambda: self.box(5),
                 self.s_two[1],
                 to_x,
                 None,
-                lambda: self.unit(1, y, 1 - x, c),
+                lambda: self.piece(1, y, 1 - x),
             )
 
         def z_copy(self, m, k, to):
@@ -642,25 +650,71 @@
             for i in range(3):
                 self.g_copy(i).wait_send()
 
+    class TreeFirst(Family):
+        def piece(self, m, yy, xx):
+            return zs_att.at[yy, 2 * xx + m]
+
+        def row_copy(self, yy, k, to):
+            part = pl.ds(pl.multiple_of(to * rows, rows), rows)
+            return wire.copy(
+                gatt.at[4:8, part, att_cols(yy, c)],
+                zl_att.at[fs, yy],
+                self.s_z[yy] + k,
+                {"fsdp": to},
+            )
+
+        def one_send(self):
+            for yy in range(2):
+                peers(lambda k, to, _, yy=yy: self.row_copy(yy, k, to).start())
+                zl_att[fs, yy] = gatt[4:8, my_rows, att_cols(yy, c)]
+
+        def sum_trees(self):
+            for yy in range(2):
+                peers(
+                    lambda k, _, src, yy=yy: wire.arrived(
+                        zl_att.at[src, yy], self.s_z[yy] + k, {"fsdp": src}
+                    )
+                )
+            zs_att[...] = jnp.sum(zl_att[...].astype(F), axis=0).astype(BF)
+            Family.one_send(self)
+
+        def copy_send(self):
+            for m, target in ((0, to_y), (1, to_x)):
+                wire.arrived(self.box(4 + m), self.s_two[m], target)
+                total = self.piece(m, y, x)[...].astype(F) + self.box(4 + m)[...].astype(F)
+                self.held[cx, m] = total.astype(BF)
+            self.g_copy(0).start()
+            self.g_copy(1).start()
+
+        def drain(self):
+            for m in range(2):
+                for t in range(4):
+                    self.core_copy(m, t).wait_send()
+                peers(lambda k, to, _, m=m: self.row_copy(m, k, to).wait_send())
+            for i in range(3):
+                self.g_copy(i).wait_send()
+
     ffn = Family(
         lambda m, yy, xx, cc: gffn.at[m, :, ffn_cols(yy, xx, cc)],
         lambda m, t: rc_att.at[m * 4 + t],
         lambda i: strip(wdn, i),
         zr_ffn,
         rg_ffn,
-        rows,
+        D,
     )
 
     def attention_family(a):
-        return Family(
+        kind = (Family, TreeFirst)[a]
+        tall = (D, rows)[a]
+        return kind(
             lambda m, yy, xx, cc: gatt.at[4 * a + 2 * xx + m, :, att_cols(yy, cc)],
             lambda m, t: rc_att.at[
                 4 * a + 2 * m + t // 2, :, pl.ds(pl.multiple_of(lax.rem(t, 2) * 128, 128), 128)
             ],
-            lambda i: rx_att.at[a, i],
+            lambda i: rx_att.at[a, i, 0:tall],
             zr_att.at[a],
             rg_att.at[a],
-            rows,
+            tall,
         )
 
     att = (attention_family(0), attention_family(1))
@@ -832,32 +886,32 @@
         if step == 4:
             ffn.second_send()
         if step == 5:
-            att[1].second_send()
             ffn.tree_send()
         if step == 6:
             shared_core_send()
-            att[1].tree_send()
         if step == 7:
             shared_y_send()
             att[0].first_send()
-            ffn.copy_send()
+            att[1].sum_trees()
             enc_finish()
             shared_x_send()
         if step == 8:
+            att[1].second_send()
             att[0].second_send()
-            att[1].copy_send()
-            ffn.relay_copy()
+            ffn.copy_send()
             shared_arrived()
         if step == 9:
             mod_tree_send()
             att[0].tree_send()
+            att[1].copy_send()
+            ffn.relay_copy()
+            mod_all_send()
+            att[0].copy_send()
             att[1].relay_copy()
             ffn_finish()
-            mod_all_send()
-            att[0].copy_send()
-            att_finish(1)
             mod_finish()
             att[0].relay_copy()
+            att_finish(1)
             att_finish(0)
 
     def hidden(x):
@@ -1314,6 +1368,8 @@
             pltpu.VMEM((2, 6, D, 128), BF),
             pltpu.VMEM((2, n, 2, rows, 128), BF),
             pltpu.VMEM((2, 4, 2, rows, 128), BF),
+            pltpu.VMEM((n, 2, 4, rows, 128), BF),
+            pltpu.VMEM((2, 4, rows, 128), BF),
             pltpu.VMEM((n, 2, rows, 256), BF),
             pltpu.VMEM((4, 2, rows, 256), BF),
             pltpu.VMEM((896, D), BF),

time: 156 us -> 151 us (0.968)
  Pallas kernels: 153 us -> 149 us
    pallas_call x1, Pallas kernels: 148 us -> 143 us  [layer_call(): pl.pallas_call(functools.partial(layer_kernel, n), out_shape=(sds((ROWS,...]
where the time goes in v6:
time: 151 us
  Pallas kernels  149 us (99%)
    pallas_call x1, Pallas kernels, layer_call(): pl.pallas_call(functools.partial(layer_kernel, n), out_shape=(sds((ROWS,...  143 us
    pallas_call x1, Pallas kernels, finish_call(): pl.pallas_call(functools.partial(finish_kernel, n, rows), out_shape=(sds(...  5.17 us

profile of v6, /device:TPU:0, one launch (start us, length us, event | category | flops | bytes accessed | tf_op | source)
XLA Modules:
  0.0 150.6 jit_solution(12563984658944915944)
XLA Ops:
  1.3 0.1 fusion.2
  1.4 0.6 pad_convert_fusion.cond_parts
  2.0 143.4 %layer.1 = (bf16[320,512]{1,0:T(8,128)(2,1)}, f32[320,512]{1,0:T(8,128)}, f32[128,512]{1,0:T(8,128)}, f32[4,8,512]{2,1,0:T(8,128)}, f32[4,8,128]{2,1,0:T(8,128)}...) custom-call(s32[1,20]{1,0:T(1,128)} %parents_ref.1, f32[4,8,128]{2,1,0:T(8,128)} %pad_convert_fusion.cond_parts, ...), custom_call_target="tpu_custom_call" | custom-call | tf_op jit(solution)/shard_map/layer/pallas_call | solution.py:1309
  145.4 5.2 %finish.1 = (bf16[320,512]{1,0:T(8,128)(2,1)}, f32[320,512]{1,0:T(8,128)}, f32[128,512]{1,0:T(8,128)}, f32[128,3072]{1,0:T(8,128)}, f32[3,128,256]{2,1,0:T(8,128...) custom-call(bf16[320,512]{1,0:T(8,128)(2,1)} %get-tuple-element.27.o, ...), custom_call_target="tpu_custom_call" | custom-call | tf_op jit(solution)/shard_map/finish/pallas_call | solution.py:1425
  (2 shorter events, 0.0 us)

commit v7 on v6

--- a/solution.py
+++ b/solution.py
@@ -1201,11 +1201,11 @@
                 for xx in range(2):
                     att[0].core_copy(m, band * 2 + xx).start()
 
-        @pl.when(turn == 0)
+        @pl.when(turn == 1)
         def _():
             leave(4)
 
-        @pl.when(turn == 2)
+        @pl.when(turn == 3)
         def _():
             leave(5)
 

time: 151 us -> 148 us (0.980)
  Pallas kernels: 149 us -> 145 us
    pallas_call x1, Pallas kernels: 143 us -> 140 us  [layer_call(): pl.pallas_call(functools.partial(layer_kernel, n), out_shape=(sds((ROWS,...]
where the time goes in v7:
time: 148 us; the launch traced here: 147 us
  Pallas kernels  145 us (98%)
    pallas_call x1, Pallas kernels, layer_call(): pl.pallas_call(functools.partial(layer_kernel, n), out_shape=(sds((ROWS,...  140 us
    pallas_call x1, Pallas kernels, finish_call(): pl.pallas_call(functools.partial(finish_kernel, n, rows), out_shape=(sds(...  5.18 us

profile of v7, /device:TPU:0, one launch (start us, length us, event | category | flops | bytes accessed | tf_op | source)
XLA Modules:
  0.0 146.7 jit_solution(10521042605344252343)
XLA Ops:
  1.3 0.1 fusion.2
  1.4 0.6 pad_convert_fusion.cond_parts
  2.0 139.5 %layer.1 = (bf16[320,512]{1,0:T(8,128)(2,1)}, f32[320,512]{1,0:T(8,128)}, f32[128,512]{1,0:T(8,128)}, f32[4,8,512]{2,1,0:T(8,128)}, f32[4,8,128]{2,1,0:T(8,128)}...) custom-call(s32[1,20]{1,0:T(1,128)} %parents_ref.1, f32[4,8,128]{2,1,0:T(8,128)} %pad_convert_fusion.cond_parts, ...), custom_call_target="tpu_custom_call" | custom-call | tf_op jit(solution)/shard_map/layer/pallas_call | solution.py:1309
  141.5 5.2 %finish.1 = (bf16[320,512]{1,0:T(8,128)(2,1)}, f32[320,512]{1,0:T(8,128)}, f32[128,512]{1,0:T(8,128)}, f32[128,3072]{1,0:T(8,128)}, f32[3,128,256]{2,1,0:T(8,128...) custom-call(bf16[320,512]{1,0:T(8,128)(2,1)} %get-tuple-element.27.o, ...), custom_call_target="tpu_custom_call" | custom-call | tf_op jit(solution)/shard_map/finish/pallas_call | solution.py:1425
  (2 shorter events, 0.0 us)

commit v8 on v7

--- a/solution.py
+++ b/solution.py
@@ -892,12 +892,12 @@
         if step == 7:
             shared_y_send()
             att[0].first_send()
-            att[1].sum_trees()
             enc_finish()
             shared_x_send()
         if step == 8:
+            att[1].sum_trees()
+            att[0].second_send()
             att[1].second_send()
-            att[0].second_send()
             ffn.copy_send()
             shared_arrived()
         if step == 9:

time: 148 us -> 147 us (level)
  no operation moved by 1% of the time
where the time goes in v8:
time: 147 us; the launch traced here: 146 us
  Pallas kernels  144 us (98%)
    pallas_call x1, Pallas kernels, layer_call(): pl.pallas_call(functools.partial(layer_kernel, n), out_shape=(sds((ROWS,...  139 us
    pallas_call x1, Pallas kernels, finish_call(): pl.pallas_call(functools.partial(finish_kernel, n, rows), out_shape=(sds(...  5.18 us

profile of v8, /device:TPU:0, one launch (start us, length us, event | category | flops | bytes accessed | tf_op | source)
XLA Modules:
  0.0 146.3 jit_solution(11112362626201268075)
XLA Ops:
  1.3 0.1 fusion.2
  1.4 0.6 pad_convert_fusion.cond_parts
  2.0 139.1 %layer.1 = (bf16[320,512]{1,0:T(8,128)(2,1)}, f32[320,512]{1,0:T(8,128)}, f32[128,512]{1,0:T(8,128)}, f32[4,8,512]{2,1,0:T(8,128)}, f32[4,8,128]{2,1,0:T(8,128)}...) custom-call(s32[1,20]{1,0:T(1,128)} %parents_ref.1, f32[4,8,128]{2,1,0:T(8,128)} %pad_convert_fusion.cond_parts, ...), custom_call_target="tpu_custom_call" | custom-call | tf_op jit(solution)/shard_map/layer/pallas_call | solution.py:1309
  141.1 5.2 %finish.1 = (bf16[320,512]{1,0:T(8,128)(2,1)}, f32[320,512]{1,0:T(8,128)}, f32[128,512]{1,0:T(8,128)}, f32[128,3072]{1,0:T(8,128)}, f32[3,128,256]{2,1,0:T(8,128...) custom-call(bf16[320,512]{1,0:T(8,128)(2,1)} %get-tuple-element.27.o, ...), custom_call_target="tpu_custom_call" | custom-call | tf_op jit(solution)/shard_map/finish/pallas_call | solution.py:1425
  (2 shorter events, 0.0 us)
